TPU v7x, 32 devices: a whole 2x2x4 slice. The times are simulated.
32 devices in a mesh: space: 2 (over y), filt: 4 (over x, core), rep: 4 (over z).
Axes of the slice: x: 2, y: 2, z: 4, core: 2. Of those that a mesh axis runs over, the one named last changes fastest.
Arguments:
- volume: bfloat16 [4, 64, 8, 8, 128], P('rep', 'filt', 'space'), may hold values from -6 to 6
- weight1: bfloat16 [64, 64, 3, 3, 3], P('filt'), may hold values from -0.15625 to 0.15625
- bias1: float32 [64], P('filt'), may hold values from -3 to 3
- weight2: bfloat16 [64, 64, 3, 3, 3], P('filt'), may hold values from -0.15625 to 0.15625
- bias2: float32 [64], P('filt'), may hold values from -3 to 3
- upstream: bfloat16 [4, 64, 8, 8, 128], P('rep', 'filt', 'space'), may hold values from -6 to 6
Outputs:
- output: bfloat16 [4, 64, 8, 8, 128], P('rep', 'filt', 'space')
- volume_grad: bfloat16 [4, 64, 8, 8, 128], P('rep', 'filt', 'space')
- weight_grad1: float32 [64, 64, 3, 3, 3], P('filt')
- bias_grad1: float32 [64], P('filt')
- weight_grad2: float32 [64, 64, 3, 3, 3], P('filt')
- bias_grad2: float32 [64], P('filt')
All inputs are finite; a program needn't handle non-finite values.
Results may differ from a plain program's by a relative error of at most 0.0058.
Values may be sent and summed in bfloat16 or wider, within the bound.
No kernel may reach another device: no remote copies, remote signals or barrier semaphores. Data moves between devices by JAX's collectives and lax.ppermute only.
A program may use at most 64 MiB of HBM per device.

v0:
```python
import math

import jax
import jax.numpy as jnp
from jax import lax
from jax.sharding import PartitionSpec as P

SLOPE = 0.3
NUMBERS = ("NCDHW", "OIDHW", "NCDHW")
SLAB_PADS = ((0, 0), (1, 1), (1, 1))


def extended(block, sides, width):
    for axis, dim in sides:
        count = lax.axis_size(axis)
        forward = [(i, i + 1) for i in range(count - 1)]
        backward = [(target, source) for source, target in forward]
        low = lax.ppermute(
            lax.slice_in_dim(block, block.shape[dim] - width, None, axis=dim), axis, forward
        )
        high = lax.ppermute(lax.slice_in_dim(block, 0, width, axis=dim), axis, backward)
        block = jnp.concatenate([low, block, high], axis=dim)
    return block


def smooth(values):
    return SLOPE * values + (1.0 - SLOPE) * jax.nn.softplus(values)


def smooth_slope(values):
    return SLOPE + (1.0 - SLOPE) * jax.nn.sigmoid(values)


def conv_pads(padded, kernel, pads):
    return lax.conv_general_dilated(
        padded[None],
        kernel,
        (1, 1, 1),
        pads,
        dimension_numbers=NUMBERS,
        preferred_element_type=jnp.float32,
    )[0]


def conv_slab(padded, kernel):
    return conv_pads(padded, kernel, SLAB_PADS)


def flip_kernel(kernel):
    return jnp.transpose(jnp.flip(kernel, (2, 3, 4)), (1, 0, 2, 3, 4))


def spread(own_field):
    border = extended(own_field, (("space", 1),), 1)
    return lax.all_gather(border, "filt", axis=0, tiled=True)


def local_grads(padded, delta, scale, pads):
    product = lax.conv_general_dilated(
        padded[:, None],
        delta[:, None],
        (1, 1, 1),
        pads,
        dimension_numbers=NUMBERS,
        preferred_element_type=jnp.float32,
    )
    weight_part = jnp.transpose(product, (1, 0, 2, 3, 4)) * scale
    bias_part = jnp.sum(delta.astype(jnp.float32), axis=(1, 2, 3)) * scale
    return (weight_part, bias_part)


def layer_total(grads):
    return lax.psum((grads[0], grads[1]), ("space", "rep"))


def back_input(delta, own_weight):
    border = extended(delta, (("space", 1),), 1)
    group_rows = delta.shape[0]
    flipped = flip_kernel(own_weight)
    return lax.psum_scatter(
        conv_slab(border, lax.slice_in_dim(flipped, 0, group_rows * lax.axis_size("filt"), axis=0)),
        "filt",
        scatter_dimension=0,
        tiled=True,
    )


def local(volume, weight1, bias1, weight2, bias2, upstream):
    own_volume = volume[0]
    cells = (
        lax.axis_size("rep")
        * lax.axis_size("space")
        * own_volume.shape[1]
        * own_volume.shape[2]
        * own_volume.shape[3]
    )
    scale = 1.0 / math.sqrt(cells)
    first_slab = spread(own_volume)
    first_pre = conv_slab(first_slab, weight1) + bias1[:, None, None, None]
    hidden = smooth(first_pre).astype(jnp.bfloat16)
    second_slab = spread(hidden)
    second_pre = conv_slab(second_slab, weight2) + bias2[:, None, None, None]
    output = smooth(second_pre).astype(jnp.bfloat16)
    second_delta = (upstream[0].astype(jnp.float32) * smooth_slope(second_pre)).astype(jnp.bfloat16)
    second_grads = layer_total(local_grads(second_slab, second_delta, scale, SLAB_PADS))
    hidden_grad = back_input(second_delta, weight2)
    first_delta = (hidden_grad * smooth_slope(first_pre)).astype(jnp.bfloat16)
    first_grads = layer_total(local_grads(first_slab, first_delta, scale, SLAB_PADS))
    volume_grad = back_input(first_delta, weight1).astype(jnp.bfloat16)
    return (
        output[None],
        volume_grad[None],
        first_grads[0],
        first_grads[1],
        second_grads[0],
        second_grads[1],
    )


def solution(mesh):
    in_specs = (
        P("rep", "filt", "space", None, None),
        P("filt", None, None, None, None),
        P("filt"),
        P("filt", None, None, None, None),
        P("filt"),
        P("rep", "filt", "space", None, None),
    )
    out_specs = (
        P("rep", "filt", "space", None, None),
        P("rep", "filt", "space", None, None),
        P("filt", None, None, None, None),
        P("filt"),
        P("filt", None, None, None, None),
        P("filt"),
    )
    return jax.shard_map(local, mesh=mesh, in_specs=in_specs, out_specs=out_specs, check_vma=False)
```

profile of v0, /device:TPU:0, one launch (start us, length us, event | category | flops | bytes accessed | tf_op | source)
XLA Modules:
  0.0 325.3 jit_solution(5718390030218221948)
XLA Ops:
  9.3 4.9 %collective-permute-start = (bf16[16,1,8,128]{3,2,1,0:T(8,128)(2,1)S(1)}, bf16[16,1,8,128]{3,2,1,0:T(8,128)(2,1)S(1)}, u32[]{:S(2)}, u32[]{:S(2)}) collective-permute-start(bf16[16,1,8,128]{3,2,1,0:T(8,128)(2,1)S(1)} %get-tuple-element.32), channel_id=1, source_target_pairs={{0,16},{1,17},{2,18},{3,19},{4,20},{5,21},{6,22},{7,23},{8,24},{9,... | collective-permute-start | bytes 98312 | tf_op jit(solution)/shard_map/ppermute | solution.py:18
  14.2 1.6 collective-permute-done
  16.7 9.7 %all_gather.6 = bf16[64,6,8,128]{3,2,1,0:T(8,128)(2,1)S(1)} all-gather(bf16[16,6,8,128]{3,2,1,0:T(8,128)(2,1)S(1)} %pad_maximum_fusion), channel_id=1, replica_groups=mesh['space'=2,'filt'=4,'rep'=4] {'filt'}, dimensions={0}, use_global_device_ids=true | all-gather | bytes 983040 | tf_op jit(solution)/shard_map/all_gather | solution.py:55
  28.8 9.7 %fusion.44 = f32[4,8,8,17,16]{4,2,3,1,0:T(8,128)} fusion(bf16[16,64,3,3,3]{1,0,4,3,2:T(8,128)(2,1)S(1)} %copy-done.11, bf16[64,6,8,1,7,2]{0,4,5,2,1,3:T(8,128)(2,1)S(1)} %slice.43, bf16[64,6,8,1,8,17]{0,4,5,2,1,3:T(8,128)(2,1)S(1)} %copy.45, pred[8,17]{0,1:T(8,128)(4,1)S(1)} %copy-done.13), kind=kOutput, calls=%fused_computation.38 | convolution fusion | flops 223465472 | bytes 1255560 | tf_op jit(solution)/shard_map/conv_general_dilated | solution.py:35
  38.4 2.9 copy.46
  43.6 4.5 %collective-permute-start.2 = (bf16[16,1,8,128]{3,0,2,1:T(8,128)(2,1)S(1)}, bf16[16,1,8,128]{3,0,2,1:T(8,128)(2,1)S(1)}, u32[]{:S(2)}, u32[]{:S(2)}) collective-permute-start(bf16[16,1,8,128]{3,0,2,1:T(8,128)(2,1)S(1)} %get-tuple-element.30), channel_id=1, source_target_pairs={{0,16},{1,17},{2,18},{3,19},{4,20},{5,21},{6,22},{7,23},{8,24},{9,... | collective-permute-start | bytes 98312 | tf_op jit(solution)/shard_map/ppermute | solution.py:18
  48.1 1.6 collective-permute-done.2
  49.7 7.8 %all_gather.7 = bf16[64,6,8,128]{3,0,2,1:T(8,128)(2,1)S(1)} all-gather(bf16[16,6,8,128]{3,0,2,1:T(8,128)(2,1)S(1)} %pad_maximum_fusion.1), channel_id=1, replica_groups=mesh['space'=2,'filt'=4,'rep'=4] {'filt'}, dimensions={0}, use_global_device_ids=true | all-gather | bytes 983040 | tf_op jit(solution)/shard_map/all_gather | solution.py:55
  59.5 11.2 %fusion.6 = (bf16[4,8,8,17,16]{4,2,3,1,0:T(8,128)(2,1)}, f32[4,8,8,17,16]{4,2,3,1,0:T(8,128)}) fusion(f32[16]{0:T(128)S(1)} %copy-done.10, bf16[16,64,3,3,3]{1,0,4,3,2:T(8,128)(2,1)S(1)} %copy-done, bf16[64,6,8,1,7,2]{0,4,5,2,1,3:T(8,128)(2,1)S(1)} %slice.47, bf16[64,6,8,1,8,17]{0,4,5,2,1,3:T(8,128)(2,1)S(1)} %copy.49, pred[8,17]{0,1:T(8,128)(4,1)S(1)} %copy-done.13), kind=kOutput, calls=%fused_computation.9 | convolution fusion | flops 224231424 | bytes 1394888 | tf_op jit(solution)/shard_map/conv_general_dilated | solution.py:35
  70.7 2.9 copy.52
  76.7 13.5 %collective-permute-start.4 = (bf16[16,1,8,128]{3,0,2,1:T(8,128)(2,1)S(1)}, bf16[16,1,8,128]{3,0,2,1:T(8,128)(2,1)S(1)}, u32[]{:S(2)}, u32[]{:S(2)}) collective-permute-start(bf16[16,1,8,128]{3,0,2,1:T(8,128)(2,1)S(1)} %get-tuple-element.28), channel_id=1, source_target_pairs={{0,16},{1,17},{2,18},{3,19},{4,20},{5,21},{6,22},{7,23},{8,24},{9,... | collective-permute-start | bytes 98312 | tf_op jit(solution)/shard_map/ppermute | solution.py:18
  90.2 1.6 collective-permute-done.4
  93.1 3.5 %copy.55 = bf16[16,6,8,1,8,17]{0,4,5,2,1,3:T(8,128)(2,1)} copy(bf16[16,6,8,1,8,17]{5,4,0,2,1,3:T(8,128)(2,1)S(1)} %reshape.115) | data formatting | bytes 417792 | tf_op jit(solution)/shard_map/conv_general_dilated | solution.py:35
  97.6 4.5 %fusion.38 = f32[4,8,8,17,64]{4,2,3,1,0:T(8,128)S(1)} fusion(bf16[16,64,3,3,3]{1,0,4,3,2:T(8,128)(2,1)S(1)} %copy-done, bf16[16,6,8,1,7,2]{0,4,5,2,1,3:T(8,128)(2,1)S(1)} %slice.52, bf16[16,6,8,1,8,17]{0,4,5,2,1,3:T(8,128)(2,1)} %copy.55, pred[8,17]{0,1:T(8,128)(4,1)S(1)} %copy-done.13), kind=kOutput, calls=%fused_computation.36 | convolution fusion | flops 221573120 | bytes 1399944 | tf_op jit(solution)/shard_map/conv_general_dilated | solution.py:35
  102.7 1.6 copy.75
  104.4 3.6 %copy.63 = bf16[64,1,6,8,128]{0,1,4,3,2:T(2,128)(2,1)} copy(bf16[64,1,6,8,128]{4,3,2,0,1:T(8,128)(2,1)S(1)} %bitcast.137) | data formatting | bytes 1572864 | tf_op jit(solution)/shard_map/broadcast_in_dim | solution.py:60
  108.0 23.4 %reduce-scatter.3.cloned.1.call-done = f32[16,4,8,128]{3,0,2,1:T(8,128)} async-done(((f32[64,4,8,128]{3,0,2,1:T(8,128)}), f32[16,4,8,128]{3,0,2,1:T(8,128)}) %reduce-scatter.3.cloned.1.call-update) | async-done | bytes 262160 | tf_op jit(solution)/shard_map/reduce_scatter | solution.py:80
  133.9 4.5 %collective-permute-start.6 = (bf16[16,1,8,128]{3,0,2,1:T(8,128)(2,1)S(1)}, bf16[16,1,8,128]{3,0,2,1:T(8,128)(2,1)S(1)}, u32[]{:S(2)}, u32[]{:S(2)}) collective-permute-start(bf16[16,1,8,128]{3,0,2,1:T(8,128)(2,1)S(1)} %get-tuple-element.26), channel_id=1, source_target_pairs={{0,16},{1,17},{2,18},{3,19},{4,20},{5,21},{6,22},{7,23},{8,24},{9,... | collective-permute-start | bytes 98312 | tf_op jit(solution)/shard_map/ppermute | solution.py:18
  138.7 5.4 %copy.66 = bf16[64,1,6,8,128]{0,1,4,3,2:T(2,128)(2,1)} copy(bf16[64,1,6,8,128]{4,0,3,2,1:T(8,128)(2,1)S(1)} %bitcast.139) | data formatting | bytes 1572864 | tf_op jit(solution)/shard_map/broadcast_in_dim | solution.py:60
  144.1 3.7 %copy.67 = bf16[16,1,4,8,128]{0,1,4,3,2:T(2,128)(2,1)} copy(bf16[16,1,4,8,128]{4,0,3,2,1:T(8,128)(2,1)S(1)} %fusion.54) | data formatting | bytes 262144 | tf_op jit(solution)/shard_map/convert_element_type | solution.py:104
  149.2 2.8 copy.60
  152.0 3.1 fusion.35
  155.6 2.1 copy.62
  158.2 31.0 %convolution_multiply_fusion = f32[16,64,3,3,3]{1,0,4,3,2:T(8,128)} fusion(bf16[64,1,6,8,128]{0,1,4,3,2:T(2,128)(2,1)} %copy.66, bf16[16,1,4,8,128]{0,1,4,3,2:T(2,128)(2,1)} %copy.67), kind=kOutput, calls=%fused_computation.39 | convolution fusion | flops 206564352 | bytes 1028096 | tf_op jit(solution)/shard_map/transpose | solution.py:67
  189.2 1.8 copy.50
  192.5 19.8 %all-reduce = (f32[16]{0:T(128)}, f32[16]{0:T(128)}) all-reduce(f32[16]{0:T(128)S(1)} %broadcast_multiply_fusion.1, f32[16]{0:T(128)S(1)} %broadcast_multiply_fusion), channel_id=1, replica_groups=mesh['space'=2,'filt'=4,'rep'=4] {'space','rep'}, use_global_device_ids=true, to_apply=%region_4.5 | all-reduce | flops 32 | bytes 256 | tf_op jit(solution)/shard_map/psum | solution.py:73
  212.3 1.4 copy.64
  213.8 30.5 %convolution_multiply_fusion.1 = f32[16,64,3,3,3]{1,0,4,3,2:T(8,128)} fusion(bf16[64,1,6,8,128]{0,1,4,3,2:T(2,128)(2,1)} %copy.63, bf16[16,1,4,8,128]{0,1,4,3,2:T(2,128)(2,1)S(1)} %copy.64), kind=kOutput, calls=%fused_computation.40 | convolution fusion | flops 206564352 | bytes 1028096 | tf_op jit(solution)/shard_map/transpose | solution.py:67
  244.3 1.6 convert_bitcast_fusion.2
  245.9 69.4 %all-reduce.4.cloned.1.call-done = (f32[16,64,3,3,3]{1,0,4,3,2:T(8,128)}, f32[16,64,3,3,3]{1,0,4,3,2:T(8,128)}) async-done(((f32[16,64,3,3,3]{1,0,4,3,2:T(8,128)}, f32[16,64,3,3,3]{1,0,4,3,2:T(8,128)}), (f32[16,64,3,3,3]{1,0,4,3,2:T(8,128)}, f32[16,64,3,3,3]{1,0,4,3,2:T(8,128)})) %all-reduce.4.cloned.1.call-update) | async-done | bytes 221200 | tf_op jit(solution)/shard_map/psum | solution.py:73
  315.3 1.6 copy.82
  316.9 1.6 copy.83
  (81 shorter events, 22.0 us)
Async XLA Ops:
  7.2 52.0 %copy-start = (bf16[16,64,3,3,3]{1,0,4,3,2:T(8,128)(2,1)S(1)}, bf16[16,64,3,3,3]{1,0,4,3,2:T(8,128)(2,1)}, u32[]{:S(2)}) copy-start(bf16[16,64,3,3,3]{1,0,4,3,2:T(8,128)(2,1)} %param.9) | copy-start | bytes 165892
  7.2 124.2 %reduce-scatter.3.cloned.1.call-start = ((), (), s32[]{:S(2)}) async-start(), calls=%async_computation.2 | async-start | bytes 1310720 | tf_op jit(solution)/shard_map/reduce_scatter | solution.py:80
  8.0 6.2 %collective-permute-start.1 = (bf16[16,1,8,128]{3,2,1,0:T(8,128)(2,1)S(1)}, bf16[16,1,8,128]{3,2,1,0:T(8,128)(2,1)S(1)}, u32[]{:S(2)}, u32[]{:S(2)}) collective-permute-start(bf16[16,1,8,128]{3,2,1,0:T(8,128)(2,1)S(1)} %get-tuple-element.33), channel_id=1, source_target_pairs={{16,0},{17,1},{18,2},{19,3},{20,4},{21,5},{22,6},{23,7},{24,8},{25... | collective-permute-start | bytes 98312 | tf_op jit(solution)/shard_map/ppermute | solution.py:21
  9.3 6.5 %collective-permute-start = (bf16[16,1,8,128]{3,2,1,0:T(8,128)(2,1)S(1)}, bf16[16,1,8,128]{3,2,1,0:T(8,128)(2,1)S(1)}, u32[]{:S(2)}, u32[]{:S(2)}) collective-permute-start(bf16[16,1,8,128]{3,2,1,0:T(8,128)(2,1)S(1)} %get-tuple-element.32), channel_id=1, source_target_pairs={{0,16},{1,17},{2,18},{3,19},{4,20},{5,21},{6,22},{7,23},{8,24},{9,... | collective-permute-start | bytes 98312 | tf_op jit(solution)/shard_map/ppermute | solution.py:18
  27.9 0.9 copy-start.11
  27.9 0.9 copy-start.13
  41.3 0.7 copy-start.9
  42.0 15.6 %copy-start.3 = (f32[4,8,1,136,16]{3,4,1,0,2:T(8,128)}, f32[4,8,1,136,16]{3,4,1,0,2:T(8,128)S(1)}, u32[]{:S(2)}) copy-start(f32[4,8,1,136,16]{3,4,1,0,2:T(8,128)S(1)} %reshape.68) | copy-start | bytes 835588
  42.3 5.9 %collective-permute-start.3 = (bf16[16,1,8,128]{3,0,2,1:T(8,128)(2,1)S(1)}, bf16[16,1,8,128]{3,0,2,1:T(8,128)(2,1)S(1)}, u32[]{:S(2)}, u32[]{:S(2)}) collective-permute-start(bf16[16,1,8,128]{3,0,2,1:T(8,128)(2,1)S(1)} %get-tuple-element.31), channel_id=1, source_target_pairs={{16,0},{17,1},{18,2},{19,3},{20,4},{21,5},{22,6},{23,7},{24,8},{25... | collective-permute-start | bytes 98312 | tf_op jit(solution)/shard_map/ppermute | solution.py:21
  43.6 6.1 %collective-permute-start.2 = (bf16[16,1,8,128]{3,0,2,1:T(8,128)(2,1)S(1)}, bf16[16,1,8,128]{3,0,2,1:T(8,128)(2,1)S(1)}, u32[]{:S(2)}, u32[]{:S(2)}) collective-permute-start(bf16[16,1,8,128]{3,0,2,1:T(8,128)(2,1)S(1)} %get-tuple-element.30), channel_id=1, source_target_pairs={{0,16},{1,17},{2,18},{3,19},{4,20},{5,21},{6,22},{7,23},{8,24},{9,... | collective-permute-start | bytes 98312 | tf_op jit(solution)/shard_map/ppermute | solution.py:18
  57.6 1.3 copy-start.1
  58.8 0.7 copy-start.10
  75.4 14.8 %collective-permute-start.5 = (bf16[16,1,8,128]{3,0,2,1:T(8,128)(2,1)S(1)}, bf16[16,1,8,128]{3,0,2,1:T(8,128)(2,1)S(1)}, u32[]{:S(2)}, u32[]{:S(2)}) collective-permute-start(bf16[16,1,8,128]{3,0,2,1:T(8,128)(2,1)S(1)} %get-tuple-element.29), channel_id=1, source_target_pairs={{16,0},{17,1},{18,2},{19,3},{20,4},{21,5},{22,6},{23,7},{24,8},{25... | collective-permute-start | bytes 98312 | tf_op jit(solution)/shard_map/ppermute | solution.py:21
  76.7 15.1 %collective-permute-start.4 = (bf16[16,1,8,128]{3,0,2,1:T(8,128)(2,1)S(1)}, bf16[16,1,8,128]{3,0,2,1:T(8,128)(2,1)S(1)}, u32[]{:S(2)}, u32[]{:S(2)}) collective-permute-start(bf16[16,1,8,128]{3,0,2,1:T(8,128)(2,1)S(1)} %get-tuple-element.28), channel_id=1, source_target_pairs={{0,16},{1,17},{2,18},{3,19},{4,20},{5,21},{6,22},{7,23},{8,24},{9,... | collective-permute-start | bytes 98312 | tf_op jit(solution)/shard_map/ppermute | solution.py:18
  104.3 27.1 %copy-start.4 = (f32[4,8,1,136,16]{3,4,1,0,2:T(8,128)S(1)}, f32[4,8,1,136,16]{3,4,1,0,2:T(8,128)}, u32[]{:S(2)}) copy-start(f32[4,8,1,136,16]{3,4,1,0,2:T(8,128)} %copy-done.3) | copy-start | bytes 835588
  104.3 140.0 %reduce-scatter.5.cloned.1.call-start = ((), (), s32[]{:S(2)}) async-start(), calls=%async_computation.3 | async-start | bytes 1310720 | tf_op jit(solution)/shard_map/reduce_scatter | solution.py:80
  104.3 34.1 %copy-start.8 = (bf16[1,16,4,8,128]{4,3,2,1,0:T(8,128)(2,1)S(1)}, bf16[1,16,4,8,128]{4,3,2,1,0:T(8,128)(2,1)}, u32[]{:S(2)}) copy-start(bf16[1,16,4,8,128]{4,3,2,1,0:T(8,128)(2,1)} %param.11) | copy-start | bytes 393220
  104.3 34.3 %copy-start.2 = (bf16[64,6,8,128]{3,0,2,1:T(8,128)(2,1)S(1)}, bf16[64,6,8,128]{3,0,2,1:T(8,128)(2,1)}, u32[]{:S(2)}) copy-start(bf16[64,6,8,128]{3,0,2,1:T(8,128)(2,1)} %copy-done.1) | copy-start | bytes 2359300
  132.6 15.2 %copy-start.5 = (bf16[16,4,8,128]{3,0,2,1:T(8,128)(2,1)}, bf16[16,4,8,128]{3,0,2,1:T(8,128)(2,1)S(1)}, u32[]{:S(2)}) copy-start(bf16[16,4,8,128]{3,0,2,1:T(8,128)(2,1)S(1)} %get-tuple-element.25) | copy-start | bytes 393220
  132.6 15.2 %collective-permute-start.7 = (bf16[16,1,8,128]{3,0,2,1:T(8,128)(2,1)S(1)}, bf16[16,1,8,128]{3,0,2,1:T(8,128)(2,1)S(1)}, u32[]{:S(2)}, u32[]{:S(2)}) collective-permute-start(bf16[16,1,8,128]{3,0,2,1:T(8,128)(2,1)S(1)} %get-tuple-element.27), channel_id=1, source_target_pairs={{16,0},{17,1},{18,2},{19,3},{20,4},{21,5},{22,6},{23,7},{24,8},{25... | collective-permute-start | bytes 98312 | tf_op jit(solution)/shard_map/ppermute | solution.py:21
  133.9 13.9 %collective-permute-start.6 = (bf16[16,1,8,128]{3,0,2,1:T(8,128)(2,1)S(1)}, bf16[16,1,8,128]{3,0,2,1:T(8,128)(2,1)S(1)}, u32[]{:S(2)}, u32[]{:S(2)}) collective-permute-start(bf16[16,1,8,128]{3,0,2,1:T(8,128)(2,1)S(1)} %get-tuple-element.26), channel_id=1, source_target_pairs={{0,16},{1,17},{2,18},{3,19},{4,20},{5,21},{6,22},{7,23},{8,24},{9,... | collective-permute-start | bytes 98312 | tf_op jit(solution)/shard_map/ppermute | solution.py:18
  149.2 2.9 copy-start.12
  157.7 31.4 %copy-start.7 = (bf16[4,8,8,17,16]{4,2,3,1,0:T(8,128)(2,1)S(1)}, bf16[4,8,8,17,16]{4,2,3,1,0:T(8,128)(2,1)}, u32[]{:S(2)}) copy-start(bf16[4,8,8,17,16]{4,2,3,1,0:T(8,128)(2,1)} %get-tuple-element.34) | copy-start | bytes 417796
  157.7 157.6 %all-reduce.4.cloned.1.call-start = ((), (), s32[]{:S(2)}) async-start(), calls=%async_computation.4 | async-start | bytes 884736 | tf_op jit(solution)/shard_map/psum | solution.py:73
  189.2 23.1 %copy-start.6 = (bf16[16,4,8,128]{3,0,2,1:T(8,128)(2,1)S(1)}, bf16[16,4,8,128]{3,0,2,1:T(8,128)(2,1)}, u32[]{:S(2)}) copy-start(bf16[16,4,8,128]{3,0,2,1:T(8,128)(2,1)} %copy-done.5) | copy-start | bytes 393220
Sparse Core Ops, SparseCore 0:
  104.4 26.9 reduce-scatter.2
  157.9 23.8 reduce-scatter.4
  244.4 70.9 all-reduce.3
where the time goes:
time: 330 us; the launch traced here: 325 us
  waiting for transfers between devices  97.6 us (30%)
  matrix products  89.8 us (27%)
  local copies, waits for them, and re-layouts  47.4 us (14%)
  blocking collectives  37.4 us (11%)
  starting transfers between devices  33.2 us (10%)
  between operations  14.4 us (4%)
  other arithmetic  5.51 us (2%)
    psum x1, waiting for transfers between devices, layer_total(): return lax.psum((grads[0], grads[1]), ('space', 'rep'))  69.4 us
    transpose x2, matrix products, local_grads(): weight_part = jnp.transpose(product, (1, 0, 2, 3, 4)) * scale  61.4 us
    conv_general_dilated x4, matrix products, conv_pads(): lax.conv_general_dilated(padded[None], kernel, (1, 1, 1), pads, dimension...  28.4 us
    ppermute x4, starting transfers between devices, extended(): lax.ppermute(lax.slice_in_dim(block, block.shape[dim] - width, None, axis...  27.5 us
    reduce_scatter x2, waiting for transfers between devices, back_input(): lax.psum_scatter(conv_slab(border, lax.slice_in_dim(flipped, 0, group_row...  23.4 us
    psum x1, blocking collectives, layer_total(): return lax.psum((grads[0], grads[1]), ('space', 'rep'))  19.8 us
    conv_general_dilated x17, local copies, waits for them, and re-layouts, conv_pads(): lax.conv_general_dilated(padded[None], kernel, (1, 1, 1), pads, dimension...  18 us
    all_gather x2, blocking collectives, spread(): return lax.all_gather(border, 'filt', axis=0, tiled=True)  17.6 us
  transfers between devices with their start and end apart: 11, of which 5 were waited for; matrix products, arithmetic and copies ran while one was open for 25% of the time, Pallas kernels for 0%

commit v1 on v0

v1 whole, which is shorter than its diff:
```python
import functools
import math

import jax
import jax.numpy as jnp
from jax import lax
from jax.experimental import pallas as pl
from jax.experimental.pallas import tpu as pltpu
from jax.sharding import PartitionSpec as P

SLOPE = 0.3
BF = jnp.bfloat16
F32 = jnp.float32
VM = pltpu.VMEM
ANY = pl.BlockSpec(memory_space=pl.ANY)
WHOLE = pl.BlockSpec(memory_space=pltpu.VMEM)


def call(kernel, outs, n_any, n_vmem, scratch=(), flops=0, moved=0, name=None):
    return pl.pallas_call(
        kernel,
        out_shape=outs,
        in_specs=[ANY] * n_any + [WHOLE] * n_vmem,
        out_specs=jax.tree.map(lambda _: WHOLE, outs),
        scratch_shapes=list(scratch),
        compiler_params=pltpu.CompilerParams(vmem_limit_bytes=40 << 20),
        cost_estimate=pl.CostEstimate(flops=flops, bytes_accessed=moved, transcendentals=0),
        name=name,
    )


def shape(dims, kind):
    return jax.ShapeDtypeStruct(tuple(dims), kind)


def parts(values):
    e = jnp.exp(-jnp.abs(values))
    one = 1.0 + e
    soft = jnp.maximum(values, 0.0) + jnp.log(one)
    sig = jnp.where(values >= 0.0, 1.0, e) / one
    return SLOPE * values + (1.0 - SLOPE) * soft, SLOPE + (1.0 - SLOPE) * sig


def slope_of(values):
    e = jnp.exp(-jnp.abs(values))
    return SLOPE + (1.0 - SLOPE) * (jnp.where(values >= 0.0, 1.0, e) / (1.0 + e))


def smooth(values):
    e = jnp.exp(-jnp.abs(values))
    soft = jnp.maximum(values, 0.0) + jnp.log(1.0 + e)
    return SLOPE * values + (1.0 - SLOPE) * soft


def swap(block):
    return jnp.transpose(block.astype(F32), (1, 0, 2))


def pack_field(f_ref, o_ref):
    for x in range(f_ref.shape[1]):
        o_ref[x] = swap(f_ref[:, x]).astype(BF)


def pack_weight(w_ref, b_ref, o_ref):
    group, chan = w_ref.shape[1], w_ref.shape[2]
    for pair in range(5):
        for kz in range(3):
            low = w_ref[6 * pair + kz]
            if pair < 4:
                high = w_ref[6 * pair + 3 + kz]
            else:
                high = jnp.zeros_like(low)
            o_ref[3 * pair + kz] = jnp.concatenate([low, high], axis=1)
    eye = lax.broadcasted_iota(jnp.int32, (group, group), 0) == lax.broadcasted_iota(
        jnp.int32, (group, group), 1
    )
    col = jnp.sum(jnp.where(eye, jnp.broadcast_to(b_ref[...], (group, group)), 0.0), axis=1, keepdims=True)
    col = jnp.broadcast_to(col, (group, 2 * chan))
    first = col.astype(BF)
    rest = col - first.astype(F32)
    second = rest.astype(BF)
    third = (rest - second.astype(F32)).astype(BF)
    lane = lax.broadcasted_iota(jnp.int32, (group, 2 * chan), 1)
    picked = jnp.where(lane == 0, first.astype(F32), jnp.where(lane == 1, second.astype(F32), third.astype(F32)))
    o_ref[15] = picked.astype(BF)


def pack_kernel(f_ref, w_ref, b_ref, of_ref, ow_ref):
    pack_weight(w_ref, b_ref, ow_ref)
    pack_field(f_ref, of_ref)


def pack(field, weight, bias):
    group, layers, ny, nz = field.shape
    chan = weight.shape[1]
    taps = jnp.transpose(weight, (2, 3, 4, 0, 1)).reshape(27, group, chan)
    return call(
        pack_kernel,
        (shape((layers, ny, group, nz), BF), shape((16, group, 2 * chan), BF)),
        0,
        3,
        moved=2 * field.size * 2,
        name="pack",
    )(field, taps, bias.reshape(1, group))


class Plan:
    def __init__(self, layers, ny, nz, chan, groups, spaces):
        self.layers, self.ny, self.nz, self.chan = layers, ny, nz, chan
        self.groups, self.spaces = groups, spaces
        self.group = chan // groups
        self.pair = spaces == 2
        self.window = (2 if self.pair else 3) * layers
        self.sides = 1 if self.pair else 2

    def start(self, reach):
        if self.pair:
            return lax.axis_index("space") * (self.layers - reach)
        return self.layers - reach

    def count(self, reach):
        return self.layers + self.sides * reach

    def own(self):
        return self.start(0)

    def inside(self, layer):
        if self.pair:
            return None
        at = (lax.axis_index("space") - 1) * self.layers + layer
        return jnp.logical_and(at >= 0, at < self.spaces * self.layers)

    def chan_at(self, flip):
        return pl.multiple_of((lax.axis_index("filt") ^ flip) * self.group, self.group)

    def padded(self):
        return (self.window + 2, self.ny + 2, self.chan, self.nz)


def flip_perm(value, flip):
    n = lax.axis_size("filt")
    return lax.ppermute(value, "filt", [(i, i ^ flip) for i in range(n)])


def over(value):
    return lax.ppermute(value, "space", [(0, 1), (1, 0)])


def up(value):
    n = lax.axis_size("space")
    return lax.ppermute(value, "space", [(i, i + 1) for i in range(n - 1)])


def down(value):
    n = lax.axis_size("space")
    return lax.ppermute(value, "space", [(i + 1, i) for i in range(n - 1)])


def gather_all(field, plan):
    if plan.pair and plan.groups == 4:
        half = plan.layers // 2
        x = flip_perm(field, 2)
        y = over(field)
        c = flip_perm(field, 1)
        d0 = over(x[:half])
        d1 = flip_perm(y[half:], 2)
        xc = flip_perm(x, 1)
        yc = flip_perm(y, 1)
        e0 = flip_perm(d0, 1)
        e1 = flip_perm(d1, 1)
        return [
            (field, "own", 0, 0),
            (c, "own", 0, 1),
            (x, "own", 0, 2),
            (xc, "own", 0, 3),
            (y, "other", 0, 0),
            (yc, "other", 0, 1),
            (d0, "other", 0, 2),
            (d1, "other", half, 2),
            (e0, "other", 0, 3),
            (e1, "other", half, 3),
        ]
    out = []
    for flip in range(plan.groups):
        mine = flip_perm(field, flip) if flip else field
        out.append((mine, "own", 0, flip))
        if plan.pair:
            out.append((over(mine), "other", 0, flip))
        else:
            out.append((up(mine), "low", 0, flip))
            out.append((down(mine), "high", 0, flip))
    return out


def gather_halo(field, plan):
    out = []
    if plan.pair:
        s = lax.axis_index("space")
        edge = lax.dynamic_slice_in_dim(field, (1 - s) * (plan.layers - 2), 2, axis=0)
        halos = [(over(edge), "halo")]
    else:
        halos = [(up(field[plan.layers - 2 :]), "low"), (down(field[:2]), "high")]
    for value, place in [(field, "own")] + halos:
        if plan.groups == 4:
            x = flip_perm(value, 2)
            c = flip_perm(value, 1)
            xc = flip_perm(x, 1)
            flips = [value, c, x, xc]
        else:
            flips = [flip_perm(value, k) if k else value for k in range(plan.groups)]
        out += [(v, place, 0, k) for k, v in enumerate(flips)]
    return out


def gather_weight(packed, plan):
    if plan.groups == 4:
        x = flip_perm(packed, 2)
        c = flip_perm(packed, 1)
        xc = flip_perm(x, 1)
        return [packed, c, x, xc]
    return [flip_perm(packed, k) if k else packed for k in range(plan.groups)]


def field_place(plan, place, k):
    if plan.pair:
        s = lax.axis_index("space")
        return 1 + k + (s if place == "own" else 1 - s) * plan.layers
    return 1 + k + {"low": 0, "own": 1, "high": 2}[place] * plan.layers


def halo_place(plan, place):
    if plan.pair:
        s = lax.axis_index("space")
        return 2 * s if place == "own" else (1 - s) * plan.layers
    return {"low": 0, "own": 2, "high": plan.layers + 2}[place]


def load_weight(plan, refs, dst, sem, start):
    for flip, ref in enumerate(refs):
        copy = pltpu.make_async_copy(ref, dst.at[:, pl.ds(plan.chan_at(flip), plan.group), :], sem.at[flip])
        copy.start() if start else copy.wait()


def load_pieces(plan, refs, places, dst, sem, start, halo=False):
    for n, (ref, (place, k, flip)) in enumerate(zip(refs, places)):
        rows = pl.ds(plan.chan_at(flip), plan.group)
        if halo:
            target = dst.at[pl.ds(halo_place(plan, place), ref.shape[0]), :, rows, :]
        else:
            target = dst.at[pl.ds(field_place(plan, place, k), ref.shape[0]), pl.ds(1, plan.ny), rows, :]
        copy = pltpu.make_async_copy(ref, target, sem.at[n])
        copy.start() if start else copy.wait()


def zero_edges(plan, ref):
    zero = jnp.zeros(ref.shape[2:], ref.dtype)
    for x in (0, ref.shape[0] - 1):
        for y in range(ref.shape[1]):
            ref[x, y] = zero
    for x in range(1, ref.shape[0] - 1):
        ref[x, 0] = zero
        ref[x, ref.shape[1] - 1] = zero


def weight_matrix(w_ref, chan):
    cols = []
    for pair in range(5):
        block = w_ref[3 * pair : 3 * pair + 3].reshape(3 * chan, 2 * chan)
        cols.append(block if pair < 4 else block[:, :chan])
    return jnp.concatenate(cols, axis=1)


def bias_column(w_ref):
    rows = w_ref[15].astype(F32)
    return rows[:, 0:1] + rows[:, 1:2] + rows[:, 2:3]


def taps(field_ref, x, y):
    c, nz = field_ref.shape[2], field_ref.shape[3]
    rows = []
    for kx in range(3):
        first = field_ref[x + kx, y : y + 3].reshape(3 * c, nz)
        second = field_ref[x + kx, y + 1 : y + 4].reshape(3 * c, nz)
        rows.append(jnp.concatenate([first, second], axis=1))
    return jnp.concatenate(rows, axis=0)


def z_shift(values, by):
    nz = values.shape[1]
    lane = lax.broadcasted_iota(jnp.int32, values.shape, 1)
    if by > 0:
        return jnp.where(lane == 0, 0.0, pltpu.roll(values, 1, 1))
    return jnp.where(lane == nz - 1, 0.0, pltpu.roll(values, nz - 1, 1))


def z_sum(product, rows, half, nz):
    part = product[:, half * nz : (half + 1) * nz]
    return part[rows : 2 * rows] + z_shift(part[:rows], 1) + z_shift(part[2 * rows :], -1)


def conv_rows(weight, field_ref, x, each):
    ny, nz = field_ref.shape[1] - 2, field_ref.shape[3]
    rows = weight.shape[0] // 3
    for y in range(0, ny, 2):
        product = jnp.dot(weight, taps(field_ref, x, y), preferred_element_type=F32)
        for half in range(2):
            each(y + half, z_sum(product, rows, half, nz))


def first_kernel(plan, places, *refs):
    n = len(places)
    pieces, weights = refs[:n], refs[n : n + plan.groups]
    h_ref, s_ref, a_ref, w_ref, sem, wsem = refs[n + plan.groups :]
    load_weight(plan, weights, w_ref, wsem, True)
    load_pieces(plan, pieces, places, a_ref, sem, True)
    zero_edges(plan, a_ref)
    zero_edges(plan, h_ref)
    load_weight(plan, weights, w_ref, wsem, False)
    load_pieces(plan, pieces, places, a_ref, sem, False)
    start = plan.start(3)
    m_ref = weight_matrix(w_ref, plan.chan)
    bias = bias_column(w_ref)

    def body(t, carry):
        x = start + t
        inside = plan.inside(x)

        def each(y, value):
            act, slope = parts(value + bias)
            if inside is not None:
                act = jnp.where(inside, act, 0.0)
                slope = jnp.where(inside, slope, 0.0)
            h_ref[x + 1, y + 1] = act.astype(BF)
            s_ref[t, y] = slope

        conv_rows(m_ref, a_ref, x, each)
        return carry

    lax.fori_loop(0, plan.count(3), body, 0)


def grads(plan, d_ref, f_ref, sh_ref, acc_ref, g_ref):
    group, nz, ny, chan = plan.group, plan.nz, plan.ny, plan.chan
    rows = pl.ds(plan.chan_at(0), group)
    own = plan.own()
    zero = jnp.zeros((3 * group, nz), BF)

    def shift(t, total):
        sh_ref[t, 0] = zero
        sh_ref[t, ny + 1] = zero
        for y in range(ny):
            value = d_ref[own + t + 1, y + 1, rows, :].astype(F32)
            total = total + value
            sh_ref[t, y + 1] = jnp.concatenate([z_shift(value, -1), value, z_shift(value, 1)], axis=0).astype(BF)
        return total

    total = lax.fori_loop(0, plan.layers, shift, jnp.zeros((group, nz), F32))
    acc_ref[...] = jnp.zeros_like(acc_ref)

    def body(t, carry):
        x = own + t
        for y in range(0, ny, 2):
            left = jnp.concatenate(
                [
                    jnp.concatenate([sh_ref[t, y + 2 - ky], sh_ref[t, y + 3 - ky]], axis=1)
                    for ky in range(3)
                ],
                axis=0,
            )
            right = jnp.concatenate(
                [jnp.concatenate([f_ref[x + kx, y + 1], f_ref[x + kx, y + 2]], axis=1) for kx in range(3)],
                axis=0,
            )
            acc_ref[...] += lax.dot_general(
                left, right, (((1,), (1,)), ((), ())), preferred_element_type=F32
            )
        return carry

    lax.fori_loop(0, plan.layers, body, 0)
    n = 9 * group
    g_ref[0:n] = acc_ref[:, 0 : 2 * chan]
    last = acc_ref[:, 2 * chan :]
    g_ref[n : n + n // 2] = jnp.concatenate([last[: n // 2], last[n // 2 :]], axis=1)
    g_ref[n + n // 2 :] = jnp.broadcast_to(jnp.sum(total, axis=1, keepdims=True), (group, 2 * chan))


def second_kernel(plan, places, *refs):
    n = len(places)
    pieces, weights = refs[:n], refs[n : n + plan.groups]
    h_ref, d_ref, o_ref, g_ref, u_ref, w_ref, p_ref, sh_ref, acc_ref, sem, wsem = refs[n + plan.groups :]
    load_weight(plan, weights, w_ref, wsem, True)
    load_pieces(plan, pieces, places, u_ref, sem, True, halo=True)
    zero_edges(plan, d_ref)
    load_weight(plan, weights, w_ref, wsem, False)
    load_pieces(plan, pieces, places, u_ref, sem, False, halo=True)
    start = plan.start(2)
    m_ref = weight_matrix(w_ref, plan.chan)
    bias = bias_column(w_ref)

    def body(t, carry):
        x = start + t

        def each(y, value):
            pre = value + bias
            p_ref[t, y] = pre
            d_ref[x + 1, y + 1] = (u_ref[t, y].astype(F32) * slope_of(pre)).astype(BF)

        conv_rows(m_ref, h_ref, x, each)
        return carry

    lax.fori_loop(0, plan.count(2), body, 0)
    rows = pl.ds(plan.chan_at(0), plan.group)
    first = plan.own() - start
    for t in range(plan.layers):
        o_ref[:, t] = jnp.transpose(smooth(p_ref[first + t, :, rows, :]), (1, 0, 2)).astype(BF)
    grads(plan, d_ref, h_ref, sh_ref, acc_ref, g_ref)


def flipped_kernel(plan, *refs):
    chan = plan.chan
    weights = refs[: 2 * plan.groups]
    outs = refs[2 * plan.groups : 2 * plan.groups + 2]
    w_refs, sem = refs[2 * plan.groups + 2 : 2 * plan.groups + 4], refs[2 * plan.groups + 4]
    for go in (True, False):
        for k in range(2):
            load_weight(plan, weights[k * plan.groups : (k + 1) * plan.groups], w_refs[k], sem.at[k], go)
    for w_ref, out in zip(w_refs, outs):
        for kz in range(3):
            turned = [jnp.transpose(w_ref[3 * pair + 2 - kz].astype(F32), (1, 0)) for pair in range(5)]
            for pair in range(5):
                low = turned[4 - pair][:chan]
                if pair < 4:
                    block = jnp.concatenate([low, turned[3 - pair][chan:]], axis=1)
                    out[kz, :, 2 * chan * pair : 2 * chan * (pair + 1)] = block.astype(BF)
                else:
                    out[kz, :, 2 * chan * pair :] = low.astype(BF)


def third_kernel(plan, places, *refs):
    n = len(places)
    pieces = refs[:n]
    s_ref, d2_ref, t_ref, d_ref, g_ref, a_ref, sh_ref, acc_ref, sem = refs[n:]
    load_pieces(plan, pieces, places, a_ref, sem, True)
    zero_edges(plan, d_ref)
    zero_edges(plan, a_ref)
    start = plan.start(1)
    skip = start - plan.start(3)
    m_ref = t_ref[...].reshape(3 * plan.chan, 9 * plan.chan)

    def body(t, carry):
        x = start + t

        def each(y, value):
            d_ref[x + 1, y + 1] = (value * s_ref[skip + t, y]).astype(BF)

        conv_rows(m_ref, d2_ref, x, each)
        return carry

    lax.fori_loop(0, plan.count(1), body, 0)
    load_pieces(plan, pieces, places, a_ref, sem, False)
    grads(plan, d_ref, a_ref, sh_ref, acc_ref, g_ref)


def fourth_kernel(plan, d_ref, t_ref, o_ref, r_ref):
    own = plan.own()
    rows = pl.ds(plan.chan_at(0), plan.group)
    m_ref = t_ref[:, rows, :].reshape(3 * plan.group, 9 * plan.chan)

    def body(t, carry):
        def each(y, value):
            r_ref[t, y] = value

        conv_rows(m_ref, d_ref, own + t, each)
        return carry

    lax.fori_loop(0, plan.layers, body, 0)
    for t in range(plan.layers):
        o_ref[:, t] = jnp.transpose(r_ref[t], (1, 0, 2)).astype(BF)


def to_wire(values, rows):
    row = lax.broadcasted_iota(jnp.int32, values.shape, 0)
    lane = lax.broadcasted_iota(jnp.int32, values.shape, 1)
    high = values.astype(BF).astype(F32)
    second = jnp.logical_and(row >= rows, lane >= values.shape[1] // 2)
    return jnp.where(second, values - high, high).astype(BF)


def add_wire(values, wire, rows):
    got = wire.astype(F32)
    row = lax.broadcasted_iota(jnp.int32, values.shape, 0)
    return values + got + jnp.where(row >= rows, pltpu.roll(got, values.shape[1] // 2, 1), 0.0)


def wire_kernel(rows, a_ref, w_ref):
    w_ref[...] = to_wire(a_ref[...], rows)


def step_kernel(rows, a_ref, got_ref, o_ref, w_ref):
    total = add_wire(a_ref[...], got_ref[...], rows)
    o_ref[...] = total
    w_ref[...] = to_wire(total, rows)


def last_kernel(rows, group, scale, a_ref, got_ref, w_ref, b_ref):
    total = add_wire(a_ref[...], got_ref[...], rows) * scale
    n = 9 * group
    chan = total.shape[1] // 2
    w_ref[0:9] = total[:n, :chan].reshape(9, group, chan)
    w_ref[9:18] = total[:n, chan:].reshape(9, group, chan)
    tail = total[n : n + n // 2]
    w_ref[18:27] = jnp.concatenate([tail[:, :chan], tail[:, chan:]], axis=0).reshape(9, group, chan)
    col = total[rows:, :group]
    eye = lax.broadcasted_iota(jnp.int32, (group, group), 0) == lax.broadcasted_iota(
        jnp.int32, (group, group), 1
    )
    b_ref[...] = jnp.sum(jnp.where(eye, col, 0.0), axis=0, keepdims=True)


def rounds(plan):
    out = []
    for axis in ("space", "rep"):
        size, bit = lax.axis_size(axis), 1
        while bit < size:
            out.append((axis, bit))
            bit *= 2
    return out


def total_grads(part, plan, scale):
    rows = part.shape[0] - plan.group
    steps = rounds(plan)
    wire = call(functools.partial(wire_kernel, rows), shape(part.shape, BF), 0, 1, name="wire")(part)
    for n, (axis, bit) in enumerate(steps):
        got = lax.ppermute(wire, axis, [(i, i ^ bit) for i in range(lax.axis_size(axis))])
        if n < len(steps) - 1:
            part, wire = call(
                functools.partial(step_kernel, rows),
                (shape(part.shape, F32), shape(part.shape, BF)),
                0,
                2,
                name="step",
            )(part, got)
    weight, bias = call(
        functools.partial(last_kernel, rows, plan.group, scale),
        (shape((27, plan.group, plan.chan), F32), shape((1, plan.group), F32)),
        0,
        2,
        name="last",
    )(part, got)
    weight = jnp.transpose(weight.reshape(3, 3, 3, plan.group, plan.chan), (3, 4, 0, 1, 2))
    return weight, bias.reshape(plan.group)


def local(volume, weight1, bias1, weight2, bias2, upstream):
    _, group, layers, ny, nz = volume.shape
    chan = weight1.shape[1]
    spaces, groups = lax.axis_size("space"), lax.axis_size("filt")
    plan = Plan(layers, ny, nz, chan, groups, spaces)
    scale = 1.0 / math.sqrt(lax.axis_size("rep") * spaces * layers * ny * nz)

    v, w1 = pack(volume[0], weight1, bias1)
    u, w2 = pack(upstream[0], weight2, bias2)
    w1_all = gather_weight(w1, plan)
    v_all = gather_all(v, plan)
    w2_all = gather_weight(w2, plan)
    u_all = gather_halo(u, plan)
    v_places = [p[1:] for p in v_all]
    u_places = [p[1:] for p in u_all]
    v_all = [p[0] for p in v_all]
    u_all = [p[0] for p in u_all]

    cells = ny * nz
    conv = 2 * 27 * chan * chan * cells
    slots = VM((16, chan, 2 * chan), BF)
    dma = pltpu.SemaphoreType.DMA
    padded = plan.padded()
    grad_rows = 27 * group // 2 + group
    grad_scratch = [VM((layers, ny + 2, 3 * group, nz), BF), VM((9 * group, 3 * chan), F32)]

    turned1, turned2 = call(
        functools.partial(flipped_kernel, plan),
        (shape((3, chan, 9 * chan), BF),) * 2,
        2 * groups,
        0,
        [slots, slots, dma((2, groups))],
        moved=4 << 20,
        name="turn",
    )(*w1_all, *w2_all)

    hidden, slope = call(
        functools.partial(first_kernel, plan, v_places),
        (shape(padded, BF), shape((plan.count(3), ny, chan, nz), F32)),
        len(v_all) + groups,
        0,
        [VM(padded, BF), slots, dma((len(v_all),)), dma((groups,))],
        flops=conv * plan.count(3),
        name="first",
    )(*v_all, *w1_all)

    delta2, output, part2 = call(
        functools.partial(second_kernel, plan, u_places),
        (shape(padded, BF), shape((group, layers, ny, nz), BF), shape((grad_rows, 2 * chan), F32)),
        len(u_all) + groups,
        1,
        [
            VM((plan.count(2), ny, chan, nz), BF),
            slots,
            VM((plan.count(2), ny, chan, nz), F32),
            *grad_scratch,
            dma((len(u_all),)),
            dma((groups,)),
        ],
        flops=conv * plan.count(2),
        name="second",
    )(*u_all, *w2_all, hidden)

    delta1, part1 = call(
        functools.partial(third_kernel, plan, v_places),
        (shape(padded, BF), shape((grad_rows, 2 * chan), F32)),
        len(v_all),
        3,
        [VM(padded, BF), *grad_scratch, dma((len(v_all),))],
        flops=conv * plan.count(1),
        name="third",
    )(*v_all, slope, delta2, turned2)

    volume_grad = call(
        functools.partial(fourth_kernel, plan),
        shape((group, layers, ny, nz), BF),
        0,
        2,
        [VM((layers, ny, group, nz), F32)],
        flops=conv * layers // 4,
        name="fourth",
    )(delta1, turned1)

    grad2, bias_grad2 = total_grads(part2, plan, scale)
    grad1, bias_grad1 = total_grads(part1, plan, scale)
    return (output[None], volume_grad[None], grad1, bias_grad1, grad2, bias_grad2)


def solution(mesh):
    field = P("rep", "filt", "space", None, None)
    kernel = P("filt", None, None, None, None)
    return jax.shard_map(
        local,
        mesh=mesh,
        in_specs=(field, kernel, P("filt"), kernel, P("filt"), field),
        out_specs=(field, field, kernel, P("filt"), kernel, P("filt")),
        check_vma=False,
    )
```

time: 330 us -> 59.7 us (0.18); the launches traced: 325 us -> 59.5 us
  matrix products: 89.8 us -> 0 us
  waiting for transfers between devices: 97.6 us -> 10 us
  local copies, waits for them, and re-layouts: 47.4 us -> 4.92 us
  blocking collectives: 37.4 us -> 0 us
  Pallas kernels: 0 us -> 21.3 us
  between operations: 14.4 us -> 0.79 us
  starting transfers between devices: 33.2 us -> 22.5 us
  other arithmetic: 5.51 us -> 0 us
    psum x1 -> x0, waiting for transfers between devices: 69.4 us -> none  [layer_total(): return lax.psum((grads[0], grads[1]), ('space', 'rep'))]
    transpose x2 -> x0, matrix products: 61.4 us -> none  [local_grads(): weight_part = jnp.transpose(product, (1, 0, 2, 3, 4)) * scale]
    conv_general_dilated x4 -> x0, matrix products: 28.4 us -> none  [conv_pads(): lax.conv_general_dilated(padded[None], kernel, (1, 1, 1), pads, dimension...]
    reduce_scatter x2 -> x0, waiting for transfers between devices: 23.4 us -> none  [back_input(): lax.psum_scatter(conv_slab(border, lax.slice_in_dim(flipped, 0, group_row...]
    pallas_call x0 -> x15, Pallas kernels: none -> 21.3 us  [the longest x1 6.24 us: local(): call(functools.partial(second_kernel, plan, u_places), (shape(padded, BF)...]
    psum x1 -> x0, blocking collectives: 19.8 us -> none  [layer_total(): return lax.psum((grads[0], grads[1]), ('space', 'rep'))]
    conv_general_dilated x17 -> x0, local copies, waits for them, and re-layouts: 18 us -> none  [conv_pads(): lax.conv_general_dilated(padded[None], kernel, (1, 1, 1), pads, dimension...]
    all_gather x2 -> x0, blocking collectives: 17.6 us -> none  [spread(): return lax.all_gather(border, 'filt', axis=0, tiled=True)]
  transfers between devices with their start and end apart: 11 -> 28, of which waited for: 5 -> 7; matrix products, arithmetic and copies ran while one was open for 25% -> 0% of each run, Pallas kernels for 0% -> 24%
where the time goes in v1:
time: 59.7 us; the launch traced here: 59.5 us
  starting transfers between devices  22.5 us (38%)
  Pallas kernels  21.3 us (36%)
  waiting for transfers between devices  10 us (17%)
  local copies, waits for them, and re-layouts  4.92 us (8%)
  between operations  0.79 us (1%)
    ppermute x19, starting transfers between devices, flip_perm(): return lax.ppermute(value, 'filt', [(i, i ^ flip) for i in range(n)])  10 us
    ppermute x6, starting transfers between devices, total_grads(): lax.ppermute(wire, axis, [(i, i ^ bit) for i in range(lax.axis_size(axis))])  9.89 us
    pallas_call x1, Pallas kernels, local(): call(functools.partial(second_kernel, plan, u_places), (shape(padded, BF)...  6.24 us
    pallas_call x1, Pallas kernels, local(): call(functools.partial(first_kernel, plan, v_places), (shape(padded, BF),...  5.04 us
    unnamed x12, local copies, waits for them, and re-layouts  4.9 us
    pallas_call x1, Pallas kernels, local(): call(functools.partial(third_kernel, plan, v_places), (shape(padded, BF),...  4.89 us
    ppermute x19, waiting for transfers between devices, flip_perm(): return lax.ppermute(value, 'filt', [(i, i ^ flip) for i in range(n)])  3.95 us
    ppermute x3, waiting for transfers between devices, over(): return lax.ppermute(value, 'space', [(0, 1), (1, 0)])  3.77 us
  transfers between devices with their start and end apart: 28, of which 7 were waited for; matrix products, arithmetic and copies ran while one was open for 0% of the time, Pallas kernels for 24%

profile of v1, /device:TPU:0, one launch (start us, length us, event | category | flops | bytes accessed | tf_op | source)
XLA Modules:
  0.0 59.5 jit_solution(3600359543606086652)
XLA Ops:
  0.6 0.9 %copy-done = bf16[1,16,4,8,128]{4,3,2,1,0:T(8,128)(2,1)S(1)} copy-done((bf16[1,16,4,8,128]{4,3,2,1,0:T(8,128)(2,1)S(1)}, bf16[1,16,4,8,128]{4,3,2,1,0:T(8,128)(2,1)}, u32[]{:S(2)}) %copy-start) | copy-done | bytes 131096
  1.5 0.9 %copy-done.2 = bf16[16,64,3,3,3]{1,0,4,3,2:T(8,128)(2,1)S(1)} copy-done((bf16[16,64,3,3,3]{1,0,4,3,2:T(8,128)(2,1)S(1)}, bf16[16,64,3,3,3]{1,0,4,3,2:T(8,128)(2,1)}, u32[]{:S(2)}) %copy-start.2) | copy-done | bytes 55320
  2.4 0.7 %copy-done.4 = f32[16]{0:T(128)S(1)} copy-done((f32[16]{0:T(128)S(1)}, f32[16]{0:T(128)}, u32[]{:S(2)}) %copy-start.4) | copy-done | bytes 88
  3.2 3.0 %collective-permute-start.11 = (bf16[4,8,16,128]{3,2,1,0:T(8,128)(2,1)S(1)}, bf16[4,8,16,128]{3,2,1,0:T(8,128)(2,1)S(1)}, u32[]{:S(2)}, u32[]{:S(2)}) collective-permute-start(bf16[4,8,16,128]{3,2,1,0:T(8,128)(2,1)S(1)} %get-tuple-element.33.refs_0_), channel_id=1, source_target_pairs={{0,8},{4,12},{8,0},{12,4},{1,9},{5,13},{9,1},{13,5},{2,10},{6,14},... | collective-permute-start | bytes 393224 | tf_op jit(solution)/shard_map/ppermute | solution.py:142
  6.3 1.5 %collective-permute-start.13 = (bf16[4,8,16,128]{3,2,1,0:T(8,128)(2,1)S(1)}, bf16[4,8,16,128]{3,2,1,0:T(8,128)(2,1)S(1)}, u32[]{:S(2)}, u32[]{:S(2)}) collective-permute-start(bf16[4,8,16,128]{3,2,1,0:T(8,128)(2,1)S(1)} %get-tuple-element.33.refs_0_), channel_id=1, source_target_pairs={{0,16},{16,0},{1,17},{17,1},{2,18},{18,2},{3,19},{19,3},{4,20},{20... | collective-permute-start | bytes 393224 | tf_op jit(solution)/shard_map/ppermute | solution.py:146
  8.3 0.9 %copy-done.1 = bf16[1,16,4,8,128]{4,3,2,1,0:T(8,128)(2,1)S(1)} copy-done((bf16[1,16,4,8,128]{4,3,2,1,0:T(8,128)(2,1)S(1)}, bf16[1,16,4,8,128]{4,3,2,1,0:T(8,128)(2,1)}, u32[]{:S(2)}) %copy-start.1) | copy-done | bytes 131096
  9.2 0.9 %copy-done.3 = bf16[16,64,3,3,3]{1,0,4,3,2:T(8,128)(2,1)S(1)} copy-done((bf16[16,64,3,3,3]{1,0,4,3,2:T(8,128)(2,1)S(1)}, bf16[16,64,3,3,3]{1,0,4,3,2:T(8,128)(2,1)}, u32[]{:S(2)}) %copy-start.3) | copy-done | bytes 55320
  10.1 0.7 %copy-done.5 = f32[16]{0:T(128)S(1)} copy-done((f32[16]{0:T(128)S(1)}, f32[16]{0:T(128)}, u32[]{:S(2)}) %copy-start.5) | copy-done | bytes 88
  11.0 1.0 %collective-permute-done.20.refs_12_.refs_2_ = bf16[16,16,128]{2,1,0:T(8,128)(2,1)S(1)} collective-permute-done((bf16[16,16,128]{2,1,0:T(8,128)(2,1)S(1)}, bf16[16,16,128]{2,1,0:T(8,128)(2,1)S(1)}, u32[]{:S(2)}, u32[]{:S(2)}) %collective-permute-start.20) | collective-permute-done | bytes 65568 | tf_op jit(solution)/shard_map/ppermute | solution.py:142
  12.0 1.0 %collective-permute-start.8 = (bf16[16,16,128]{2,1,0:T(8,128)(2,1)S(1)}, bf16[16,16,128]{2,1,0:T(8,128)(2,1)S(1)}, u32[]{:S(2)}, u32[]{:S(2)}) collective-permute-start(bf16[16,16,128]{2,1,0:T(8,128)(2,1)S(1)} %get-tuple-element.32.refs_8_.refs_4_), channel_id=1, source_target_pairs={{0,8},{4,12},{8,0},{12,4},{1,9},{5,13},{9,1},{13,5},{2,10},{6,14},... | collective-permute-start | bytes 196616 | tf_op jit(solution)/shard_map/ppermute | solution.py:142
  13.0 2.5 %collective-permute-done.3.refs_4_ = bf16[2,8,16,128]{3,2,1,0:T(8,128)(2,1)S(1)} collective-permute-done((bf16[2,8,16,128]{3,2,1,0:T(8,128)(2,1)S(1)}, bf16[2,8,16,128]{3,2,1,0:T(8,128)(2,1)S(1)}, u32[]{:S(2)}, u32[]{:S(2)}) %collective-permute-start.3) | collective-permute-done | bytes 65568 | tf_op jit(solution)/shard_map/ppermute | solution.py:146
  15.5 0.8 %collective-permute-done.8.refs_10_.refs_6_ = bf16[16,16,128]{2,1,0:T(8,128)(2,1)S(1)} collective-permute-done((bf16[16,16,128]{2,1,0:T(8,128)(2,1)S(1)}, bf16[16,16,128]{2,1,0:T(8,128)(2,1)S(1)}, u32[]{:S(2)}, u32[]{:S(2)}) %collective-permute-start.8) | collective-permute-done | bytes 65568 | tf_op jit(solution)/shard_map/ppermute | solution.py:142
  16.3 1.2 %collective-permute-start.5 = (bf16[2,8,16,128]{3,2,1,0:T(8,128)(2,1)S(1)}, bf16[2,8,16,128]{3,2,1,0:T(8,128)(2,1)S(1)}, u32[]{:S(2)}, u32[]{:S(2)}) collective-permute-start(bf16[2,8,16,128]{3,2,1,0:T(8,128)(2,1)S(1)} %collective-permute-done.3.refs_4_), channel_id=1, source_target_pairs={{0,8},{4,12},{8,0},{12,4},{1,9},{5,13},{9,1},{13,5},{2,10},{6,14},... | collective-permute-start | bytes 196616 | tf_op jit(solution)/shard_map/ppermute | solution.py:142
  17.5 1.1 %collective-permute-start.1 = (bf16[4,8,16,128]{3,2,1,0:T(8,128)(2,1)S(1)}, bf16[4,8,16,128]{3,2,1,0:T(8,128)(2,1)S(1)}, u32[]{:S(2)}, u32[]{:S(2)}) collective-permute-start(bf16[4,8,16,128]{3,2,1,0:T(8,128)(2,1)S(1)} %get-tuple-element.31.refs_0_), channel_id=1, source_target_pairs={{0,8},{4,12},{8,0},{12,4},{1,9},{5,13},{9,1},{13,5},{2,10},{6,14},... | collective-permute-start | bytes 393224 | tf_op jit(solution)/shard_map/ppermute | solution.py:142
  18.7 1.0 %collective-permute-start.15 = (bf16[2,8,16,128]{3,2,1,0:T(8,128)(2,1)S(1)}, bf16[2,8,16,128]{3,2,1,0:T(8,128)(2,1)S(1)}, u32[]{:S(2)}, u32[]{:S(2)}) collective-permute-start(bf16[2,8,16,128]{3,2,1,0:T(8,128)(2,1)S(1)} %slice.8), channel_id=1, source_target_pairs={{0,16},{16,0},{1,17},{17,1},{2,18},{18,2},{3,19},{19,3},{4,20},{20... | collective-permute-start | bytes 196616 | tf_op jit(solution)/shard_map/ppermute | solution.py:146
  19.6 1.5 %collective-permute-start.16 = (bf16[2,8,16,128]{3,2,1,0:T(8,128)(2,1)S(1)}, bf16[2,8,16,128]{3,2,1,0:T(8,128)(2,1)S(1)}, u32[]{:S(2)}, u32[]{:S(2)}) collective-permute-start(bf16[2,8,16,128]{3,2,1,0:T(8,128)(2,1)S(1)} %slice.9), channel_id=1, source_target_pairs={{0,8},{4,12},{8,0},{12,4},{1,9},{5,13},{9,1},{13,5},{2,10},{6,14},... | collective-permute-start | bytes 196616 | tf_op jit(solution)/shard_map/ppermute | solution.py:142
  21.7 1.3 %collective-permute-done.15.refs_6_ = bf16[2,8,16,128]{3,2,1,0:T(8,128)(2,1)S(1)} collective-permute-done((bf16[2,8,16,128]{3,2,1,0:T(8,128)(2,1)S(1)}, bf16[2,8,16,128]{3,2,1,0:T(8,128)(2,1)S(1)}, u32[]{:S(2)}, u32[]{:S(2)}) %collective-permute-start.15) | collective-permute-done | bytes 65568 | tf_op jit(solution)/shard_map/ppermute | solution.py:146
  22.9 2.1 %collective-permute-done.16.refs_7_ = bf16[2,8,16,128]{3,2,1,0:T(8,128)(2,1)S(1)} collective-permute-done((bf16[2,8,16,128]{3,2,1,0:T(8,128)(2,1)S(1)}, bf16[2,8,16,128]{3,2,1,0:T(8,128)(2,1)S(1)}, u32[]{:S(2)}, u32[]{:S(2)}) %collective-permute-start.16) | collective-permute-done | bytes 65568 | tf_op jit(solution)/shard_map/ppermute | solution.py:142
  26.8 5.0 %first.1 = (bf16[10,10,64,128]{3,2,1,0:T(8,128)(2,1)S(1)}, f32[7,8,64,128]{3,2,1,0:T(8,128)S(1)}) custom-call(bf16[4,8,16,128]{3,2,1,0:T(8,128)(2,1)S(1)} %get-tuple-element.33.refs_0_, bf16[4,8,16,128]{3,2,1,0:T(8,128)(2,1)S(1)} %collective-permute-done.10.refs_1_, bf16[4,8,16,128]{3,2,1,0:T(8,128)(2,1)S(1)} %collective-permute-done.11.refs_2_, ...), custom_call_target="tpu_custom_call" | custom-call | flops 1585446912 | tf_op jit(solution)/shard_map/first/pallas_call | solution.py:591
  31.9 6.2 %second.1 = (bf16[10,10,64,128]{3,2,1,0:T(8,128)(2,1)S(1)}, bf16[16,4,8,128]{3,2,1,0:T(8,128)(2,1)}, f32[232,128]{1,0:T(8,128)S(1)}) custom-call(bf16[4,8,16,128]{3,2,1,0:T(8,128)(2,1)S(1)} %get-tuple-element.31.refs_0_, bf16[4,8,16,128]{3,2,1,0:T(8,128)(2,1)S(1)} %collective-permute-done.refs_1_, ...), custom_call_target="tpu_custom_call" | custom-call | flops 1358954496 | tf_op jit(solution)/shard_map/second/pallas_call | solution.py:601
  38.2 1.2 %collective-permute-start.25 = (bf16[232,128]{1,0:T(8,128)(2,1)S(1)}, bf16[232,128]{1,0:T(8,128)(2,1)S(1)}, u32[]{:S(2)}, u32[]{:S(2)}) collective-permute-start(bf16[232,128]{1,0:T(8,128)(2,1)S(1)} %wire.3), channel_id=1, source_target_pairs={{0,16},{16,0},{1,17},{17,1},{2,18},{18,2},{3,19},{19,3},{4,20},{20... | collective-permute-start | bytes 178184 | tf_op jit(solution)/shard_map/ppermute | solution.py:535
  39.4 4.9 %third.1 = (bf16[10,10,64,128]{3,2,1,0:T(8,128)(2,1)S(1)}, f32[232,128]{1,0:T(8,128)S(1)}) custom-call(bf16[4,8,16,128]{3,2,1,0:T(8,128)(2,1)S(1)} %get-tuple-element.33.refs_0_, bf16[4,8,16,128]{3,2,1,0:T(8,128)(2,1)S(1)} %collective-permute-done.10.refs_1_, bf16[4,8,16,128]{3,2,1,0:T(8,128)(2,1)S(1)} %collective-permute-done.11.refs_2_, ...), custom_call_target="tpu_custom_call" | custom-call | flops 1132462080 | tf_op jit(solution)/shard_map/third/pallas_call | solution.py:618
  44.3 0.9 %collective-permute-start.22 = (bf16[232,128]{1,0:T(8,128)(2,1)S(1)}, bf16[232,128]{1,0:T(8,128)(2,1)S(1)}, u32[]{:S(2)}, u32[]{:S(2)}) collective-permute-start(bf16[232,128]{1,0:T(8,128)(2,1)S(1)} %wire.2), channel_id=1, source_target_pairs={{0,16},{16,0},{1,17},{17,1},{2,18},{18,2},{3,19},{19,3},{4,20},{20... | collective-permute-start | bytes 178184 | tf_op jit(solution)/shard_map/ppermute | solution.py:535
  45.3 1.6 %collective-permute-start.26 = (bf16[232,128]{1,0:T(8,128)(2,1)S(1)}, bf16[232,128]{1,0:T(8,128)(2,1)S(1)}, u32[]{:S(2)}, u32[]{:S(2)}) collective-permute-start(bf16[232,128]{1,0:T(8,128)(2,1)S(1)} %get-tuple-element.51), channel_id=1, source_target_pairs={{0,1},{1,0},{2,3},{3,2},{4,5},{5,4},{6,7},{7,6},{8,9},{9,8},{10,11... | collective-permute-start | bytes 178184 | tf_op jit(solution)/shard_map/ppermute | solution.py:535
  46.9 1.7 %collective-permute-done.22.got_ref = bf16[232,128]{1,0:T(8,128)(2,1)S(1)} collective-permute-done((bf16[232,128]{1,0:T(8,128)(2,1)S(1)}, bf16[232,128]{1,0:T(8,128)(2,1)S(1)}, u32[]{:S(2)}, u32[]{:S(2)}) %collective-permute-start.22) | collective-permute-done | bytes 59424 | tf_op jit(solution)/shard_map/ppermute | solution.py:535
  48.7 1.6 %collective-permute-start.23 = (bf16[232,128]{1,0:T(8,128)(2,1)S(1)}, bf16[232,128]{1,0:T(8,128)(2,1)S(1)}, u32[]{:S(2)}, u32[]{:S(2)}) collective-permute-start(bf16[232,128]{1,0:T(8,128)(2,1)S(1)} %get-tuple-element.44), channel_id=1, source_target_pairs={{0,1},{1,0},{2,3},{3,2},{4,5},{5,4},{6,7},{7,6},{8,9},{9,8},{10,11... | collective-permute-start | bytes 178184 | tf_op jit(solution)/shard_map/ppermute | solution.py:535
  50.3 2.6 %collective-permute-start.27 = (bf16[232,128]{1,0:T(8,128)(2,1)S(1)}, bf16[232,128]{1,0:T(8,128)(2,1)S(1)}, u32[]{:S(2)}, u32[]{:S(2)}) collective-permute-start(bf16[232,128]{1,0:T(8,128)(2,1)S(1)} %get-tuple-element.53), channel_id=1, source_target_pairs={{0,2},{1,3},{2,0},{3,1},{4,6},{5,7},{6,4},{7,5},{8,10},{9,11},{10,... | collective-permute-start | bytes 178184 | tf_op jit(solution)/shard_map/ppermute | solution.py:535
  52.9 0.6 collective-permute-done.23.got_ref
  53.6 2.0 %collective-permute-start.24 = (bf16[232,128]{1,0:T(8,128)(2,1)S(1)}, bf16[232,128]{1,0:T(8,128)(2,1)S(1)}, u32[]{:S(2)}, u32[]{:S(2)}) collective-permute-start(bf16[232,128]{1,0:T(8,128)(2,1)S(1)} %get-tuple-element.46), channel_id=1, source_target_pairs={{0,2},{1,3},{2,0},{3,1},{4,6},{5,7},{6,4},{7,5},{8,10},{9,11},{10,... | collective-permute-start | bytes 178184 | tf_op jit(solution)/shard_map/ppermute | solution.py:535
  55.6 2.3 %fourth.1 = bf16[16,4,8,128]{3,2,1,0:T(8,128)(2,1)} custom-call(bf16[10,10,64,128]{3,2,1,0:T(8,128)(2,1)S(1)} %get-tuple-element.40.d_ref, bf16[3,64,576]{2,1,0:T(8,128)(2,1)S(1)} %get-tuple-element.41.t_ref), custom_call_target="tpu_custom_call" | custom-call | flops 226492416 | tf_op jit(solution)/shard_map/fourth/pallas_call | solution.py:628
  57.9 0.8 %last.3 = (f32[27,16,64]{2,1,0:T(8,128)}, f32[1,16]{1,0:T(1,128)}) custom-call(f32[232,128]{1,0:T(8,128)S(1)} %get-tuple-element.52.a_ref, bf16[232,128]{1,0:T(8,128)(2,1)S(1)} %collective-permute-done.27.got_ref), custom_call_target="tpu_custom_call" | custom-call | tf_op jit(solution)/shard_map/last/pallas_call | solution.py:544
  58.7 0.8 %last.2 = (f32[27,16,64]{2,1,0:T(8,128)}, f32[1,16]{1,0:T(1,128)}) custom-call(f32[232,128]{1,0:T(8,128)S(1)} %get-tuple-element.45.a_ref, bf16[232,128]{1,0:T(8,128)(2,1)S(1)} %collective-permute-done.24.got_ref), custom_call_target="tpu_custom_call" | custom-call | tf_op jit(solution)/shard_map/last/pallas_call | solution.py:544
  (54 shorter events, 3.7 us)
Async XLA Ops:
  0.6 0.9 %copy-start = (bf16[1,16,4,8,128]{4,3,2,1,0:T(8,128)(2,1)S(1)}, bf16[1,16,4,8,128]{4,3,2,1,0:T(8,128)(2,1)}, u32[]{:S(2)}) copy-start(bf16[1,16,4,8,128]{4,3,2,1,0:T(8,128)(2,1)} %param.6) | copy-start | bytes 393220
  1.5 0.9 %copy-start.2 = (bf16[16,64,3,3,3]{1,0,4,3,2:T(8,128)(2,1)S(1)}, bf16[16,64,3,3,3]{1,0,4,3,2:T(8,128)(2,1)}, u32[]{:S(2)}) copy-start(bf16[16,64,3,3,3]{1,0,4,3,2:T(8,128)(2,1)} %param.7) | copy-start | bytes 165892
  3.2 13.1 %collective-permute-start.11 = (bf16[4,8,16,128]{3,2,1,0:T(8,128)(2,1)S(1)}, bf16[4,8,16,128]{3,2,1,0:T(8,128)(2,1)S(1)}, u32[]{:S(2)}, u32[]{:S(2)}) collective-permute-start(bf16[4,8,16,128]{3,2,1,0:T(8,128)(2,1)S(1)} %get-tuple-element.33.refs_0_), channel_id=1, source_target_pairs={{0,8},{4,12},{8,0},{12,4},{1,9},{5,13},{9,1},{13,5},{2,10},{6,14},... | collective-permute-start | bytes 393224 | tf_op jit(solution)/shard_map/ppermute | solution.py:142
  6.3 11.3 %collective-permute-start.13 = (bf16[4,8,16,128]{3,2,1,0:T(8,128)(2,1)S(1)}, bf16[4,8,16,128]{3,2,1,0:T(8,128)(2,1)S(1)}, u32[]{:S(2)}, u32[]{:S(2)}) collective-permute-start(bf16[4,8,16,128]{3,2,1,0:T(8,128)(2,1)S(1)} %get-tuple-element.33.refs_0_), channel_id=1, source_target_pairs={{0,16},{16,0},{1,17},{17,1},{2,18},{18,2},{3,19},{19,3},{4,20},{20... | collective-permute-start | bytes 393224 | tf_op jit(solution)/shard_map/ppermute | solution.py:146
  7.8 4.3 %collective-permute-start.20 = (bf16[16,16,128]{2,1,0:T(8,128)(2,1)S(1)}, bf16[16,16,128]{2,1,0:T(8,128)(2,1)S(1)}, u32[]{:S(2)}, u32[]{:S(2)}) collective-permute-start(bf16[16,16,128]{2,1,0:T(8,128)(2,1)S(1)} %get-tuple-element.34.refs_10_.refs_0_), channel_id=1, source_target_pairs={{0,8},{4,12},{8,0},{12,4},{1,9},{5,13},{9,1},{13,5},{2,10},{6,14},... | collective-permute-start | bytes 196616 | tf_op jit(solution)/shard_map/ppermute | solution.py:142
  8.3 4.7 %collective-permute-start.19 = (bf16[16,16,128]{2,1,0:T(8,128)(2,1)S(1)}, bf16[16,16,128]{2,1,0:T(8,128)(2,1)S(1)}, u32[]{:S(2)}, u32[]{:S(2)}) collective-permute-start(bf16[16,16,128]{2,1,0:T(8,128)(2,1)S(1)} %get-tuple-element.34.refs_10_.refs_0_), channel_id=1, source_target_pairs={{0,4},{4,0},{8,12},{12,8},{1,5},{5,1},{9,13},{13,9},{2,6},{6,2},{1... | collective-permute-start | bytes 196616 | tf_op jit(solution)/shard_map/ppermute | solution.py:142
  8.3 0.9 %copy-start.1 = (bf16[1,16,4,8,128]{4,3,2,1,0:T(8,128)(2,1)S(1)}, bf16[1,16,4,8,128]{4,3,2,1,0:T(8,128)(2,1)}, u32[]{:S(2)}) copy-start(bf16[1,16,4,8,128]{4,3,2,1,0:T(8,128)(2,1)} %param.11) | copy-start | bytes 393220
  9.2 0.9 %copy-start.3 = (bf16[16,64,3,3,3]{1,0,4,3,2:T(8,128)(2,1)S(1)}, bf16[16,64,3,3,3]{1,0,4,3,2:T(8,128)(2,1)}, u32[]{:S(2)}) copy-start(bf16[16,64,3,3,3]{1,0,4,3,2:T(8,128)(2,1)} %param.9) | copy-start | bytes 165892
  10.9 4.6 %collective-permute-start.3 = (bf16[2,8,16,128]{3,2,1,0:T(8,128)(2,1)S(1)}, bf16[2,8,16,128]{3,2,1,0:T(8,128)(2,1)S(1)}, u32[]{:S(2)}, u32[]{:S(2)}) collective-permute-start(bf16[2,8,16,128]{3,2,1,0:T(8,128)(2,1)S(1)} %constant_dynamic-slice_fusion), channel_id=1, source_target_pairs={{0,16},{16,0},{1,17},{17,1},{2,18},{18,2},{3,19},{19,3},{4,20},{20... | collective-permute-start | bytes 196616 | tf_op jit(solution)/shard_map/ppermute | solution.py:146
  12.0 4.3 %collective-permute-start.8 = (bf16[16,16,128]{2,1,0:T(8,128)(2,1)S(1)}, bf16[16,16,128]{2,1,0:T(8,128)(2,1)S(1)}, u32[]{:S(2)}, u32[]{:S(2)}) collective-permute-start(bf16[16,16,128]{2,1,0:T(8,128)(2,1)S(1)} %get-tuple-element.32.refs_8_.refs_4_), channel_id=1, source_target_pairs={{0,8},{4,12},{8,0},{12,4},{1,9},{5,13},{9,1},{13,5},{2,10},{6,14},... | collective-permute-start | bytes 196616 | tf_op jit(solution)/shard_map/ppermute | solution.py:142
  13.0 6.7 %collective-permute-start.10 = (bf16[4,8,16,128]{3,2,1,0:T(8,128)(2,1)S(1)}, bf16[4,8,16,128]{3,2,1,0:T(8,128)(2,1)S(1)}, u32[]{:S(2)}, u32[]{:S(2)}) collective-permute-start(bf16[4,8,16,128]{3,2,1,0:T(8,128)(2,1)S(1)} %get-tuple-element.33.refs_0_), channel_id=1, source_target_pairs={{0,4},{4,0},{8,12},{12,8},{1,5},{5,1},{9,13},{13,9},{2,6},{6,2},{1... | collective-permute-start | bytes 393224 | tf_op jit(solution)/shard_map/ppermute | solution.py:142
  15.5 2.0 %collective-permute-start.7 = (bf16[16,16,128]{2,1,0:T(8,128)(2,1)S(1)}, bf16[16,16,128]{2,1,0:T(8,128)(2,1)S(1)}, u32[]{:S(2)}, u32[]{:S(2)}) collective-permute-start(bf16[16,16,128]{2,1,0:T(8,128)(2,1)S(1)} %get-tuple-element.32.refs_8_.refs_4_), channel_id=1, source_target_pairs={{0,4},{4,0},{8,12},{12,8},{1,5},{5,1},{9,13},{13,9},{2,6},{6,2},{1... | collective-permute-start | bytes 196616 | tf_op jit(solution)/shard_map/ppermute | solution.py:142
  16.3 2.4 %collective-permute-start.21 = (bf16[16,16,128]{2,1,0:T(8,128)(2,1)S(1)}, bf16[16,16,128]{2,1,0:T(8,128)(2,1)S(1)}, u32[]{:S(2)}, u32[]{:S(2)}) collective-permute-start(bf16[16,16,128]{2,1,0:T(8,128)(2,1)S(1)} %collective-permute-done.20.refs_12_.refs_2_), channel_id=1, source_target_pairs={{0,4},{4,0},{8,12},{12,8},{1,5},{5,1},{9,13},{13,9},{2,6},{6,2},{1... | collective-permute-start | bytes 196616 | tf_op jit(solution)/shard_map/ppermute | solution.py:142
  16.3 4.8 %collective-permute-start.5 = (bf16[2,8,16,128]{3,2,1,0:T(8,128)(2,1)S(1)}, bf16[2,8,16,128]{3,2,1,0:T(8,128)(2,1)S(1)}, u32[]{:S(2)}, u32[]{:S(2)}) collective-permute-start(bf16[2,8,16,128]{3,2,1,0:T(8,128)(2,1)S(1)} %collective-permute-done.3.refs_4_), channel_id=1, source_target_pairs={{0,8},{4,12},{8,0},{12,4},{1,9},{5,13},{9,1},{13,5},{2,10},{6,14},... | collective-permute-start | bytes 196616 | tf_op jit(solution)/shard_map/ppermute | solution.py:142
  17.5 3.6 %collective-permute-start.9 = (bf16[16,16,128]{2,1,0:T(8,128)(2,1)S(1)}, bf16[16,16,128]{2,1,0:T(8,128)(2,1)S(1)}, u32[]{:S(2)}, u32[]{:S(2)}) collective-permute-start(bf16[16,16,128]{2,1,0:T(8,128)(2,1)S(1)} %collective-permute-done.8.refs_10_.refs_6_), channel_id=1, source_target_pairs={{0,4},{4,0},{8,12},{12,8},{1,5},{5,1},{9,13},{13,9},{2,6},{6,2},{1... | collective-permute-start | bytes 196616 | tf_op jit(solution)/shard_map/ppermute | solution.py:142
  17.5 8.1 %collective-permute-start.1 = (bf16[4,8,16,128]{3,2,1,0:T(8,128)(2,1)S(1)}, bf16[4,8,16,128]{3,2,1,0:T(8,128)(2,1)S(1)}, u32[]{:S(2)}, u32[]{:S(2)}) collective-permute-start(bf16[4,8,16,128]{3,2,1,0:T(8,128)(2,1)S(1)} %get-tuple-element.31.refs_0_), channel_id=1, source_target_pairs={{0,8},{4,12},{8,0},{12,4},{1,9},{5,13},{9,1},{13,5},{2,10},{6,14},... | collective-permute-start | bytes 393224 | tf_op jit(solution)/shard_map/ppermute | solution.py:142
  18.7 4.3 %collective-permute-start.15 = (bf16[2,8,16,128]{3,2,1,0:T(8,128)(2,1)S(1)}, bf16[2,8,16,128]{3,2,1,0:T(8,128)(2,1)S(1)}, u32[]{:S(2)}, u32[]{:S(2)}) collective-permute-start(bf16[2,8,16,128]{3,2,1,0:T(8,128)(2,1)S(1)} %slice.8), channel_id=1, source_target_pairs={{0,16},{16,0},{1,17},{17,1},{2,18},{18,2},{3,19},{19,3},{4,20},{20... | collective-permute-start | bytes 196616 | tf_op jit(solution)/shard_map/ppermute | solution.py:146
  19.6 5.4 %collective-permute-start.16 = (bf16[2,8,16,128]{3,2,1,0:T(8,128)(2,1)S(1)}, bf16[2,8,16,128]{3,2,1,0:T(8,128)(2,1)S(1)}, u32[]{:S(2)}, u32[]{:S(2)}) collective-permute-start(bf16[2,8,16,128]{3,2,1,0:T(8,128)(2,1)S(1)} %slice.9), channel_id=1, source_target_pairs={{0,8},{4,12},{8,0},{12,4},{1,9},{5,13},{9,1},{13,5},{2,10},{6,14},... | collective-permute-start | bytes 196616 | tf_op jit(solution)/shard_map/ppermute | solution.py:142
  21.1 5.6 %collective-permute-start.12 = (bf16[4,8,16,128]{3,2,1,0:T(8,128)(2,1)S(1)}, bf16[4,8,16,128]{3,2,1,0:T(8,128)(2,1)S(1)}, u32[]{:S(2)}, u32[]{:S(2)}) collective-permute-start(bf16[4,8,16,128]{3,2,1,0:T(8,128)(2,1)S(1)} %collective-permute-done.11.refs_2_), channel_id=1, source_target_pairs={{0,4},{4,0},{8,12},{12,8},{1,5},{5,1},{9,13},{13,9},{2,6},{6,2},{1... | collective-permute-start | bytes 393224 | tf_op jit(solution)/shard_map/ppermute | solution.py:142
  21.1 5.7 %collective-permute-start.14 = (bf16[4,8,16,128]{3,2,1,0:T(8,128)(2,1)S(1)}, bf16[4,8,16,128]{3,2,1,0:T(8,128)(2,1)S(1)}, u32[]{:S(2)}, u32[]{:S(2)}) collective-permute-start(bf16[4,8,16,128]{3,2,1,0:T(8,128)(2,1)S(1)} %collective-permute-done.13.refs_4_), channel_id=1, source_target_pairs={{0,4},{4,0},{8,12},{12,8},{1,5},{5,1},{9,13},{13,9},{2,6},{6,2},{1... | collective-permute-start | bytes 393224 | tf_op jit(solution)/shard_map/ppermute | solution.py:142
  22.9 3.3 %collective-permute-start.17 = (bf16[2,8,16,128]{3,2,1,0:T(8,128)(2,1)S(1)}, bf16[2,8,16,128]{3,2,1,0:T(8,128)(2,1)S(1)}, u32[]{:S(2)}, u32[]{:S(2)}) collective-permute-start(bf16[2,8,16,128]{3,2,1,0:T(8,128)(2,1)S(1)} %collective-permute-done.15.refs_6_), channel_id=1, source_target_pairs={{0,4},{4,0},{8,12},{12,8},{1,5},{5,1},{9,13},{13,9},{2,6},{6,2},{1... | collective-permute-start | bytes 196616 | tf_op jit(solution)/shard_map/ppermute | solution.py:142
  25.0 1.3 %collective-permute-start.18 = (bf16[2,8,16,128]{3,2,1,0:T(8,128)(2,1)S(1)}, bf16[2,8,16,128]{3,2,1,0:T(8,128)(2,1)S(1)}, u32[]{:S(2)}, u32[]{:S(2)}) collective-permute-start(bf16[2,8,16,128]{3,2,1,0:T(8,128)(2,1)S(1)} %collective-permute-done.16.refs_7_), channel_id=1, source_target_pairs={{0,4},{4,0},{8,12},{12,8},{1,5},{5,1},{9,13},{13,9},{2,6},{6,2},{1... | collective-permute-start | bytes 196616 | tf_op jit(solution)/shard_map/ppermute | solution.py:142
  25.6 6.2 %collective-permute-start = (bf16[4,8,16,128]{3,2,1,0:T(8,128)(2,1)S(1)}, bf16[4,8,16,128]{3,2,1,0:T(8,128)(2,1)S(1)}, u32[]{:S(2)}, u32[]{:S(2)}) collective-permute-start(bf16[4,8,16,128]{3,2,1,0:T(8,128)(2,1)S(1)} %get-tuple-element.31.refs_0_), channel_id=1, source_target_pairs={{0,4},{4,0},{8,12},{12,8},{1,5},{5,1},{9,13},{13,9},{2,6},{6,2},{1... | collective-permute-start | bytes 393224 | tf_op jit(solution)/shard_map/ppermute | solution.py:142
  26.2 5.7 %collective-permute-start.4 = (bf16[2,8,16,128]{3,2,1,0:T(8,128)(2,1)S(1)}, bf16[2,8,16,128]{3,2,1,0:T(8,128)(2,1)S(1)}, u32[]{:S(2)}, u32[]{:S(2)}) collective-permute-start(bf16[2,8,16,128]{3,2,1,0:T(8,128)(2,1)S(1)} %collective-permute-done.3.refs_4_), channel_id=1, source_target_pairs={{0,4},{4,0},{8,12},{12,8},{1,5},{5,1},{9,13},{13,9},{2,6},{6,2},{1... | collective-permute-start | bytes 196616 | tf_op jit(solution)/shard_map/ppermute | solution.py:142
  26.3 5.6 %collective-permute-start.6 = (bf16[2,8,16,128]{3,2,1,0:T(8,128)(2,1)S(1)}, bf16[2,8,16,128]{3,2,1,0:T(8,128)(2,1)S(1)}, u32[]{:S(2)}, u32[]{:S(2)}) collective-permute-start(bf16[2,8,16,128]{3,2,1,0:T(8,128)(2,1)S(1)} %collective-permute-done.5.refs_6_), channel_id=1, source_target_pairs={{0,4},{4,0},{8,12},{12,8},{1,5},{5,1},{9,13},{13,9},{2,6},{6,2},{1... | collective-permute-start | bytes 196616 | tf_op jit(solution)/shard_map/ppermute | solution.py:142
  26.7 5.2 %collective-permute-start.2 = (bf16[4,8,16,128]{3,2,1,0:T(8,128)(2,1)S(1)}, bf16[4,8,16,128]{3,2,1,0:T(8,128)(2,1)S(1)}, u32[]{:S(2)}, u32[]{:S(2)}) collective-permute-start(bf16[4,8,16,128]{3,2,1,0:T(8,128)(2,1)S(1)} %collective-permute-done.1.refs_2_), channel_id=1, source_target_pairs={{0,4},{4,0},{8,12},{12,8},{1,5},{5,1},{9,13},{13,9},{2,6},{6,2},{1... | collective-permute-start | bytes 393224 | tf_op jit(solution)/shard_map/ppermute | solution.py:142
  38.2 7.1 %collective-permute-start.25 = (bf16[232,128]{1,0:T(8,128)(2,1)S(1)}, bf16[232,128]{1,0:T(8,128)(2,1)S(1)}, u32[]{:S(2)}, u32[]{:S(2)}) collective-permute-start(bf16[232,128]{1,0:T(8,128)(2,1)S(1)} %wire.3), channel_id=1, source_target_pairs={{0,16},{16,0},{1,17},{17,1},{2,18},{18,2},{3,19},{19,3},{4,20},{20... | collective-permute-start | bytes 178184 | tf_op jit(solution)/shard_map/ppermute | solution.py:535
  44.3 4.3 %collective-permute-start.22 = (bf16[232,128]{1,0:T(8,128)(2,1)S(1)}, bf16[232,128]{1,0:T(8,128)(2,1)S(1)}, u32[]{:S(2)}, u32[]{:S(2)}) collective-permute-start(bf16[232,128]{1,0:T(8,128)(2,1)S(1)} %wire.2), channel_id=1, source_target_pairs={{0,16},{16,0},{1,17},{17,1},{2,18},{18,2},{3,19},{19,3},{4,20},{20... | collective-permute-start | bytes 178184 | tf_op jit(solution)/shard_map/ppermute | solution.py:535
  45.3 4.9 %collective-permute-start.26 = (bf16[232,128]{1,0:T(8,128)(2,1)S(1)}, bf16[232,128]{1,0:T(8,128)(2,1)S(1)}, u32[]{:S(2)}, u32[]{:S(2)}) collective-permute-start(bf16[232,128]{1,0:T(8,128)(2,1)S(1)} %get-tuple-element.51), channel_id=1, source_target_pairs={{0,1},{1,0},{2,3},{3,2},{4,5},{5,4},{6,7},{7,6},{8,9},{9,8},{10,11... | collective-permute-start | bytes 178184 | tf_op jit(solution)/shard_map/ppermute | solution.py:535
  48.7 4.8 %collective-permute-start.23 = (bf16[232,128]{1,0:T(8,128)(2,1)S(1)}, bf16[232,128]{1,0:T(8,128)(2,1)S(1)}, u32[]{:S(2)}, u32[]{:S(2)}) collective-permute-start(bf16[232,128]{1,0:T(8,128)(2,1)S(1)} %get-tuple-element.44), channel_id=1, source_target_pairs={{0,1},{1,0},{2,3},{3,2},{4,5},{5,4},{6,7},{7,6},{8,9},{9,8},{10,11... | collective-permute-start | bytes 178184 | tf_op jit(solution)/shard_map/ppermute | solution.py:535
  50.3 7.5 %collective-permute-start.27 = (bf16[232,128]{1,0:T(8,128)(2,1)S(1)}, bf16[232,128]{1,0:T(8,128)(2,1)S(1)}, u32[]{:S(2)}, u32[]{:S(2)}) collective-permute-start(bf16[232,128]{1,0:T(8,128)(2,1)S(1)} %get-tuple-element.53), channel_id=1, source_target_pairs={{0,2},{1,3},{2,0},{3,1},{4,6},{5,7},{6,4},{7,5},{8,10},{9,11},{10,... | collective-permute-start | bytes 178184 | tf_op jit(solution)/shard_map/ppermute | solution.py:535
  53.6 5.1 %collective-permute-start.24 = (bf16[232,128]{1,0:T(8,128)(2,1)S(1)}, bf16[232,128]{1,0:T(8,128)(2,1)S(1)}, u32[]{:S(2)}, u32[]{:S(2)}) collective-permute-start(bf16[232,128]{1,0:T(8,128)(2,1)S(1)} %get-tuple-element.46), channel_id=1, source_target_pairs={{0,2},{1,3},{2,0},{3,1},{4,6},{5,7},{6,4},{7,5},{8,10},{9,11},{10,... | collective-permute-start | bytes 178184 | tf_op jit(solution)/shard_map/ppermute | solution.py:535
  (2 other events, 1.3 us)

commit v2 on v1

v2 whole, which is shorter than its diff:
```python
import functools
import math

import jax
import jax.numpy as jnp
from jax import lax
from jax.experimental import pallas as pl
from jax.experimental.pallas import tpu as pltpu
from jax.sharding import PartitionSpec as P

SLOPE = 0.3
NEAR = 3
BF = jnp.bfloat16
F32 = jnp.float32
VM = pltpu.VMEM
ANY = pl.BlockSpec(memory_space=pl.ANY)
WHOLE = pl.BlockSpec(memory_space=pltpu.VMEM)


def call(kernel, outs, n_any, n_vmem, scratch=(), flops=0, moved=0, name=None):
    return pl.pallas_call(
        kernel,
        out_shape=outs,
        in_specs=[ANY] * n_any + [WHOLE] * n_vmem,
        out_specs=jax.tree.map(lambda _: WHOLE, outs),
        scratch_shapes=list(scratch),
        compiler_params=pltpu.CompilerParams(vmem_limit_bytes=40 << 20),
        cost_estimate=pl.CostEstimate(flops=flops, bytes_accessed=moved, transcendentals=0),
        name=name,
    )


def shape(dims, kind):
    return jax.ShapeDtypeStruct(tuple(dims), kind)


def parts(values):
    e = jnp.exp(-jnp.abs(values))
    one = 1.0 + e
    soft = jnp.maximum(values, 0.0) + jnp.log(one)
    sig = jnp.where(values >= 0.0, 1.0, e) / one
    return SLOPE * values + (1.0 - SLOPE) * soft, SLOPE + (1.0 - SLOPE) * sig


def slope_of(values):
    e = jnp.exp(-jnp.abs(values))
    return SLOPE + (1.0 - SLOPE) * (jnp.where(values >= 0.0, 1.0, e) / (1.0 + e))


def smooth(values):
    e = jnp.exp(-jnp.abs(values))
    soft = jnp.maximum(values, 0.0) + jnp.log(1.0 + e)
    return SLOPE * values + (1.0 - SLOPE) * soft


def swap(block):
    return jnp.transpose(block.astype(F32), (1, 0, 2))


def pack_weight(w_ref, b_ref, o_ref, base):
    group, chan, ny = w_ref.shape[1], w_ref.shape[2], o_ref.shape[1]
    for pair in range(5):
        for kz in range(3):
            low = w_ref[6 * pair + kz]
            if pair < 4:
                high = w_ref[6 * pair + 3 + kz]
            else:
                high = jnp.zeros_like(low)
            slot = 3 * pair + kz
            o_ref[base + slot // ny, slot % ny] = jnp.concatenate([low, high], axis=1)
    eye = lax.broadcasted_iota(jnp.int32, (group, group), 0) == lax.broadcasted_iota(
        jnp.int32, (group, group), 1
    )
    col = jnp.sum(jnp.where(eye, jnp.broadcast_to(b_ref[...], (group, group)), 0.0), axis=1, keepdims=True)
    col = jnp.broadcast_to(col, (group, 2 * chan))
    first = col.astype(BF)
    rest = col - first.astype(F32)
    second = rest.astype(BF)
    third = (rest - second.astype(F32)).astype(BF)
    lane = lax.broadcasted_iota(jnp.int32, (group, 2 * chan), 1)
    picked = jnp.where(lane == 0, first.astype(F32), jnp.where(lane == 1, second.astype(F32), third.astype(F32)))
    o_ref[base + 15 // ny, 15 % ny] = picked.astype(BF)


def pack_kernel(edge, *refs):
    if edge:
        f_hbm, w_hbm, b_hbm, n_hbm, o_ref, e_ref, f_ref, w_ref, b_ref, n_ref, sem = refs
    else:
        f_hbm, w_hbm, b_hbm, o_ref, f_ref, w_ref, b_ref, sem = refs
    layers = f_ref.shape[1]
    pairs = [(f_hbm, f_ref), (w_hbm, w_ref), (b_hbm, b_ref)]
    if edge:
        facing = 1 - lax.axis_index("space")
        pairs.append((n_hbm.at[:, pl.ds(facing * (layers - 1), 1)], n_ref))
    copies = [pltpu.make_async_copy(src, dst, sem.at[n]) for n, (src, dst) in enumerate(pairs)]
    for copy in copies:
        copy.start()
    copies[0].wait()
    for x in range(layers):
        o_ref[x] = swap(f_ref[:, x]).astype(BF)
    if edge:
        copies[3].wait()
        for x in range(edge):
            e_ref[x] = o_ref[facing * (layers - edge) + x]
        e_ref[edge] = swap(n_ref[:, 0]).astype(BF)
    copies[1].wait()
    copies[2].wait()
    pack_weight(w_ref, b_ref, o_ref, layers)


def pack(field, weight, bias, name, beside=None, edge=0):
    group, layers, ny, nz = field.shape
    chan = weight.shape[1]
    taps = jnp.transpose(weight, (2, 3, 4, 0, 1)).reshape(27, group, chan)
    args = [field, taps, bias.reshape(1, group)]
    outs = [shape((layers + 16 // ny, ny, group, nz), BF)]
    scratch = [VM(field.shape, BF), VM((27, group, chan), BF), VM((1, group), F32)]
    if edge:
        args.append(beside)
        outs.append(shape((edge + 1, ny, group, nz), BF))
        scratch.append(VM((group, 1, ny, nz), BF))
    return pl.pallas_call(
        functools.partial(pack_kernel, edge),
        out_shape=tuple(outs),
        in_specs=[pl.BlockSpec(memory_space=pltpu.HBM)] * len(args),
        out_specs=(WHOLE,) * len(outs),
        scratch_shapes=scratch + [pltpu.SemaphoreType.DMA((len(args),))],
        compiler_params=pltpu.CompilerParams(vmem_limit_bytes=40 << 20),
        cost_estimate=pl.CostEstimate(flops=0, bytes_accessed=field.size * 4, transcendentals=0),
        name=name,
    )(*(pltpu.with_memory_space_constraint(v, pltpu.HBM) for v in args))


class Plan:
    def __init__(self, layers, ny, nz, chan, groups, spaces):
        self.layers, self.ny, self.nz, self.chan = layers, ny, nz, chan
        self.groups, self.spaces = groups, spaces
        self.group = chan // groups
        self.pair = spaces == 2
        self.quick = self.pair and groups == 4
        self.window = (2 if self.pair else 3) * layers
        self.sides = 1 if self.pair else 2

    def start(self, reach):
        if self.pair:
            return lax.axis_index("space") * (self.layers - reach)
        return self.layers - reach

    def count(self, reach):
        return self.layers + self.sides * reach

    def own(self):
        return self.start(0)

    def inside(self, layer):
        if self.pair:
            return None
        at = (lax.axis_index("space") - 1) * self.layers + layer
        return jnp.logical_and(at >= 0, at < self.spaces * self.layers)

    def chan_at(self, flip):
        return pl.multiple_of((lax.axis_index("filt") ^ flip) * self.group, self.group)

    def padded(self):
        return (self.window + 2, self.ny + 2, self.chan, self.nz)


def flip_perm(value, flip):
    n = lax.axis_size("filt")
    return lax.ppermute(value, "filt", [(i, i ^ flip) for i in range(n)])


def over(value):
    return lax.ppermute(value, "space", [(0, 1), (1, 0)])


def up(value):
    n = lax.axis_size("space")
    return lax.ppermute(value, "space", [(i, i + 1) for i in range(n - 1)])


def down(value):
    n = lax.axis_size("space")
    return lax.ppermute(value, "space", [(i + 1, i) for i in range(n - 1)])


def after(value, *others):
    return lax.optimization_barrier((value, *others))[0]


def gather_quick(volume, weight1, bias1, upstream, weight2, bias2, plan, early_layers):
    n = plan.layers
    packed, edge = pack(volume, weight1, bias1, "pack1", upstream, NEAR)
    x = flip_perm(packed, 2)
    y = over(edge)
    c = flip_perm(packed, 1)
    (second,) = pack(after(upstream, c), weight2, bias2, "pack2")
    y, x = lax.optimization_barrier((y, x, second))[:2]
    d = flip_perm(y, 2)
    xc = flip_perm(x, 1)
    yc = flip_perm(y, 1)
    x2 = flip_perm(second, 2)
    early = early_layers([(v, 0, n, "own", 0, k) for k, v in enumerate([packed, c, x, xc])])
    dc = flip_perm(after(d, early[0]), 1)
    c2 = flip_perm(after(second, early[0]), 1)
    own, other, own2 = [packed, c, x, xc], [y, yc, d, dc], [second, c2, x2, x2]
    return (
        [(v, 0, n, "own", 0, k) for k, v in enumerate(own)],
        [(v, 0, NEAR, "other", 0, k) for k, v in enumerate(other)],
        [(v, 0, n, "own", 0, k) for k, v in enumerate(own2)],
        [(v, NEAR, 1, "halo", 0, k) for k, v in enumerate(other)],
        early,
    )


def gather_plain(volume, weight1, bias1, upstream, weight2, bias2, plan, early_layers):
    n = plan.layers
    (packed,) = pack(volume, weight1, bias1, "pack1")
    (second,) = pack(upstream, weight2, bias2, "pack2")
    own, other, own2, halo = [], [], [], []
    for flip in range(plan.groups):
        mine = flip_perm(packed, flip) if flip else packed
        mine2 = flip_perm(second, flip) if flip else second
        own.append((mine, 0, n, "own", 0, flip))
        own2.append((mine2, 0, n, "own", 0, flip))
        if plan.pair:
            facing = 1 - lax.axis_index("space")
            near = lax.dynamic_slice_in_dim(mine, facing * (n - NEAR), NEAR, axis=0)
            other.append((over(near), 0, NEAR, "other", 0, flip))
            near = lax.dynamic_slice_in_dim(mine2, facing * (n - 1), 1, axis=0)
            halo.append((over(near), 0, 1, "halo", 0, flip))
        else:
            other.append((up(mine[n - NEAR : n]), 0, NEAR, "low", 0, flip))
            other.append((down(mine[:NEAR]), 0, NEAR, "high", 0, flip))
            halo.append((up(mine2[n - 1 : n]), 0, 1, "low", 0, flip))
            halo.append((down(mine2[:1]), 0, 1, "high", 0, flip))
    return own, other, own2, halo, ()


def field_place(plan, place, k):
    n = plan.layers
    if plan.pair:
        s = lax.axis_index("space")
        return 1 + k + (s * n if place == "own" else n - NEAR * s)
    return 1 + k + {"low": n - NEAR, "own": n, "high": 2 * n}[place]


def halo_place(plan, place):
    if plan.pair:
        s = lax.axis_index("space")
        return s if place == "own" else (1 - s) * plan.layers
    return {"low": 0, "own": 1, "high": plan.layers + 1}[place]


def load_weight(plan, refs, dst, sem, start):
    for flip, ref in enumerate(refs):
        copy = pltpu.make_async_copy(
            ref.at[pl.ds(ref.shape[0] - dst.shape[0], dst.shape[0])],
            dst.at[:, :, pl.ds(plan.chan_at(flip), plan.group), :],
            sem.at[flip],
        )
        copy.start() if start else copy.wait()


def load_pieces(plan, refs, places, dst, sem, start, halo=False, near=False):
    for n, (ref, (first, count, place, k, flip)) in enumerate(zip(refs, places)):
        if near and place == "own":
            first = k = (1 - lax.axis_index("space")) * (plan.layers - 2)
            count = 2
        rows = pl.ds(plan.chan_at(flip), plan.group)
        if halo:
            target = dst.at[pl.ds(halo_place(plan, place), count), :, rows, :]
        else:
            target = dst.at[pl.ds(field_place(plan, place, k), count), pl.ds(1, plan.ny), rows, :]
        copy = pltpu.make_async_copy(ref.at[pl.ds(first, count)], target, sem.at[n])
        copy.start() if start else copy.wait()


def zero_rows(ref):
    zero = jnp.zeros(ref.shape[2:], ref.dtype)
    for x in range(ref.shape[0]):
        ref[x, 0] = zero
        ref[x, ref.shape[1] - 1] = zero


def zero_layer(ref, x):
    zero = jnp.zeros(ref.shape[2:], ref.dtype)
    for y in range(1, ref.shape[1] - 1):
        ref[x, y] = zero


def zero_edges(plan, ref):
    zero_rows(ref)
    zero_layer(ref, 0)
    zero_layer(ref, ref.shape[0] - 1)


def slot(w_ref, n):
    return w_ref[n // w_ref.shape[1], n % w_ref.shape[1]]


def weight_matrix(w_ref, chan):
    cols = []
    for pair in range(5):
        block = jnp.concatenate([slot(w_ref, 3 * pair + kz) for kz in range(3)], axis=0)
        cols.append(block if pair < 4 else block[:, :chan])
    return jnp.concatenate(cols, axis=1)


def bias_column(w_ref):
    rows = slot(w_ref, 15).astype(F32)
    return rows[:, 0:1] + rows[:, 1:2] + rows[:, 2:3]


def taps(field_ref, x, y):
    c, nz = field_ref.shape[2], field_ref.shape[3]
    rows = []
    for kx in range(3):
        first = field_ref[x + kx, y : y + 3].reshape(3 * c, nz)
        second = field_ref[x + kx, y + 1 : y + 4].reshape(3 * c, nz)
        rows.append(jnp.concatenate([first, second], axis=1))
    return jnp.concatenate(rows, axis=0)


def z_shift(values, by):
    nz = values.shape[1]
    lane = lax.broadcasted_iota(jnp.int32, values.shape, 1)
    if by > 0:
        return jnp.where(lane == 0, 0.0, pltpu.roll(values, 1, 1))
    return jnp.where(lane == nz - 1, 0.0, pltpu.roll(values, nz - 1, 1))


def z_sum(product, rows, half, nz):
    part = product[:, half * nz : (half + 1) * nz]
    return part[rows : 2 * rows] + z_shift(part[:rows], 1) + z_shift(part[2 * rows :], -1)


def conv_rows(weight, field_ref, x, each):
    ny, nz = field_ref.shape[1] - 2, field_ref.shape[3]
    rows = weight.shape[0] // 3
    for y in range(0, ny, 2):
        product = jnp.dot(weight, taps(field_ref, x, y), preferred_element_type=F32)
        for half in range(2):
            each(y + half, z_sum(product, rows, half, nz))


def first_rows(plan, weight, bias, a_ref, start, count, put):
    def body(t, carry):
        x = start + t
        inside = plan.inside(x)

        def each(y, value):
            act, slope = parts(value + bias)
            if inside is not None:
                act = jnp.where(inside, act, 0.0)
            put(t, x, y, act.astype(BF), slope)

        conv_rows(weight, a_ref, x, each)
        return carry

    lax.fori_loop(0, count, body, 0, unroll=True)


def early_kernel(plan, places, *refs):
    n = len(places)
    pieces = refs[:n]
    h_ref, s_ref, a_ref, w_ref, sem, wsem = refs[n:]
    load_weight(plan, pieces[: plan.groups], w_ref, wsem, True)
    load_pieces(plan, pieces, places, a_ref, sem, True)
    zero_edges(plan, a_ref)
    load_weight(plan, pieces[: plan.groups], w_ref, wsem, False)
    load_pieces(plan, pieces, places, a_ref, sem, False)

    def put(t, x, y, act, slope):
        h_ref[t, y] = act
        s_ref[t, y] = slope

    start = lax.axis_index("space") * (plan.layers + 1)
    first_rows(plan, weight_matrix(w_ref, plan.chan), bias_column(w_ref), a_ref, start, plan.layers - 1, put)


def first_kernel(plan, places, *refs):
    n = len(places)
    pieces, refs = refs[:n], refs[n:]
    if plan.quick:
        eh_ref, es_ref, refs = refs[0], refs[1], refs[2:]
    h_ref, s_ref, a_ref, w_ref, sem, wsem, esem = refs
    load_weight(plan, pieces[: plan.groups], w_ref, wsem, True)
    load_pieces(plan, pieces, places, a_ref, sem, True, near=plan.quick)
    zero_edges(plan, a_ref)
    zero_edges(plan, h_ref)
    base = plan.start(2)
    start, count = base, plan.count(2)
    copies = []
    if plan.quick:
        s = lax.axis_index("space")
        done = s * (plan.layers + 1)
        start, count = plan.layers - 1 - s, count - plan.layers + 1
        copies = [
            pltpu.make_async_copy(
                eh_ref, h_ref.at[pl.ds(done + 1, plan.layers - 1), pl.ds(1, plan.ny)], esem.at[0]
            ),
            pltpu.make_async_copy(es_ref, s_ref.at[pl.ds(done - base, plan.layers - 1)], esem.at[1]),
        ]
    for copy in copies:
        copy.start()
    load_weight(plan, pieces[: plan.groups], w_ref, wsem, False)
    load_pieces(plan, pieces, places, a_ref, sem, False, near=plan.quick)

    def put(t, x, y, act, slope):
        h_ref[x + 1, y + 1] = act
        s_ref[x - base, y] = slope

    first_rows(plan, weight_matrix(w_ref, plan.chan), bias_column(w_ref), a_ref, start, count, put)
    for copy in copies:
        copy.wait()


def grads(plan, get, f_ref, sh_ref, acc_ref, g_ref):
    group, nz, ny, chan = plan.group, plan.nz, plan.ny, plan.chan
    rows = pl.ds(plan.chan_at(0), group)
    own = plan.own()
    zero = jnp.zeros((3 * group, nz), BF)

    def shift(t, total):
        sh_ref[t, 0] = zero
        sh_ref[t, ny + 1] = zero
        for y in range(ny):
            value = get(t, y, rows).astype(F32)
            total = total + value
            sh_ref[t, y + 1] = jnp.concatenate([z_shift(value, -1), value, z_shift(value, 1)], axis=0).astype(BF)
        return total

    total = lax.fori_loop(0, plan.layers, shift, jnp.zeros((group, nz), F32), unroll=True)
    total_w = jnp.zeros(acc_ref.shape, F32)
    for t in range(plan.layers):
        x = own + t
        left = jnp.concatenate(
            [jnp.concatenate([sh_ref[t, y + 2 - ky] for y in range(ny)], axis=1) for ky in range(3)], axis=0
        )
        right = jnp.concatenate(
            [jnp.concatenate([f_ref[x + kx, y + 1] for y in range(ny)], axis=1) for kx in range(3)], axis=0
        )
        total_w += lax.dot_general(left, right, (((1,), (1,)), ((), ())), preferred_element_type=F32)
    acc_ref[...] = total_w
    n = 9 * group
    g_ref[0:n] = acc_ref[:, 0 : 2 * chan]
    last = acc_ref[:, 2 * chan :]
    g_ref[n : n + n // 2] = jnp.concatenate([last[: n // 2], last[n // 2 :]], axis=1)
    g_ref[n + n // 2 :] = jnp.broadcast_to(jnp.sum(total, axis=1, keepdims=True), (group, 2 * chan))


def second_kernel(plan, places, *refs):
    n = len(places)
    pieces = refs[:n]
    weights = pieces[: plan.groups]
    h_ref, d_ref, o_ref, g_ref, t_ref, u_ref, w_ref, p_ref, sh_ref, acc_ref, sem, wsem = refs[n:]
    load_weight(plan, weights, w_ref, wsem, True)
    load_pieces(plan, pieces, places, u_ref, sem, True, halo=True)
    zero_edges(plan, d_ref)
    load_weight(plan, weights, w_ref, wsem, False)
    turn(w_ref, t_ref, plan.chan)
    load_pieces(plan, pieces, places, u_ref, sem, False, halo=True)
    start = plan.start(1)
    m_ref = weight_matrix(w_ref, plan.chan)
    bias = bias_column(w_ref)

    def body(t, carry):
        x = start + t

        def each(y, value):
            pre = value + bias
            p_ref[t, y] = pre
            d_ref[x + 1, y + 1] = (u_ref[t, y].astype(F32) * slope_of(pre)).astype(BF)

        conv_rows(m_ref, h_ref, x, each)
        return carry

    lax.fori_loop(0, plan.count(1), body, 0, unroll=True)
    rows = pl.ds(plan.chan_at(0), plan.group)
    own = plan.own()
    first = own - start
    for t in range(plan.layers):
        o_ref[:, t] = jnp.transpose(smooth(p_ref[first + t, :, rows, :]), (1, 0, 2)).astype(BF)
    grads(plan, lambda t, y, rows: d_ref[own + t + 1, y + 1, rows, :], h_ref, sh_ref, acc_ref, g_ref)


def turn(w_ref, out, chan):
    for kz in range(3):
        turned = [jnp.transpose(slot(w_ref, 3 * pair + 2 - kz).astype(F32), (1, 0)) for pair in range(5)]
        for pair in range(5):
            low = turned[4 - pair][:chan]
            if pair < 4:
                block = jnp.concatenate([low, turned[3 - pair][chan:]], axis=1)
                out[kz, :, 2 * chan * pair : 2 * chan * (pair + 1)] = block.astype(BF)
            else:
                out[kz, :, 2 * chan * pair :] = low.astype(BF)


def turn_kernel(plan, *refs):
    out, w_ref, sem = refs[plan.groups :]
    for go in (True, False):
        load_weight(plan, refs[: plan.groups], w_ref, sem, go)
    turn(w_ref, out, plan.chan)


def third_kernel(plan, places, *refs):
    n = len(places)
    pieces = refs[:n]
    s_ref, d2_ref, t_ref, d_ref, g_ref, a_ref, sh_ref, acc_ref, sem = refs[n:]
    load_pieces(plan, pieces, places, a_ref, sem, True)
    zero_edges(plan, a_ref)
    start = plan.own()
    skip = start - plan.start(2)
    m_ref = t_ref[...].reshape(3 * plan.chan, 9 * plan.chan)

    def body(t, carry):
        def each(y, value):
            d_ref[t, y] = (value * s_ref[skip + t, y]).astype(BF)

        conv_rows(m_ref, d2_ref, start + t, each)
        return carry

    lax.fori_loop(0, plan.layers, body, 0, unroll=True)
    load_pieces(plan, pieces, places, a_ref, sem, False)
    grads(plan, lambda t, y, rows: d_ref[t, y, rows, :], a_ref, sh_ref, acc_ref, g_ref)


def fourth_kernel(plan, d_ref, t_ref, r_ref, *refs):
    *outs, a_ref, sem = refs
    layers, ny = plan.layers, plan.ny
    copy = pltpu.make_async_copy(d_ref, a_ref.at[pl.ds(2, layers), pl.ds(1, ny)], sem)
    copy.start()
    zero_rows(a_ref)
    for x in (0, 1, layers + 2, layers + 3):
        zero_layer(a_ref, x)
    copy.wait()
    rows = pl.ds(plan.chan_at(0), plan.group)
    m_ref = t_ref[:, rows, :].reshape(3 * plan.group, 9 * plan.chan)
    for t in range(layers):

        def each(y, value, t=t):
            r_ref[t, y] = value

        conv_rows(m_ref, a_ref, t + 1, each)
    if plan.pair:
        places = [(1 - lax.axis_index("space")) * (layers + 1)]
    else:
        places = [0, layers + 1]
    for out, place in zip(outs, places):

        def beside(y, value, out=out):
            out[y * plan.group : (y + 1) * plan.group] = value.astype(BF)

        conv_rows(m_ref, a_ref, place, beside)


def finish_volume(plan, r_ref, shares, o_ref):
    layers, ny, group = plan.layers, plan.ny, plan.group
    for layer, ref, base in shares:
        for y in range(ny):
            r_ref[layer, y] += ref[base + y * group : base + (y + 1) * group].astype(F32)
    for t in range(layers):
        o_ref[:, t] = jnp.transpose(r_ref[t], (1, 0, 2)).astype(BF)


def finish_kernel(plan, r_hbm, low_ref, high_ref, o_ref, r_ref, sem):
    copy = pltpu.make_async_copy(r_hbm, r_ref, sem)
    copy.start()
    copy.wait()
    finish_volume(plan, r_ref, [(0, low_ref, 0), (plan.layers - 1, high_ref, 0)], o_ref)


def to_wire(values, rows):
    row = lax.broadcasted_iota(jnp.int32, values.shape, 0)
    lane = lax.broadcasted_iota(jnp.int32, values.shape, 1)
    high = values.astype(BF).astype(F32)
    second = jnp.logical_and(row >= rows, lane >= values.shape[1] // 2)
    return jnp.where(second, values - high, high).astype(BF)


def add_wire(values, wire, rows):
    got = wire.astype(F32)
    row = lax.broadcasted_iota(jnp.int32, values.shape, 0)
    return values + got + jnp.where(row >= rows, pltpu.roll(got, values.shape[1] // 2, 1), 0.0)


def wire_kernel(rows, a_ref, w_ref):
    w_ref[...] = to_wire(a_ref[...], rows)


def step_kernel(rows, a_ref, got_ref, o_ref, w_ref):
    total = add_wire(a_ref[...], got_ref[...], rows)
    o_ref[...] = total
    w_ref[...] = to_wire(total, rows)


def join_kernel(rows, a_ref, got_ref, share_ref, o_ref, w_ref):
    total = add_wire(a_ref[...], got_ref[...], rows)
    o_ref[...] = total
    w_ref[: total.shape[0]] = to_wire(total, rows)
    w_ref[total.shape[0] :] = share_ref[...]


def close_kernel(plan, rows, scale, r_hbm, a_ref, got_ref, w_ref, b_ref, o_ref, r_ref, sem):
    copy = pltpu.make_async_copy(r_hbm, r_ref, sem)
    copy.start()
    last_kernel(rows, plan.group, scale, a_ref, got_ref, w_ref, b_ref)
    copy.wait()
    layer = (1 - lax.axis_index("space")) * (plan.layers - 1)
    finish_volume(plan, r_ref, [(layer, got_ref, a_ref.shape[0])], o_ref)


def last_kernel(rows, group, scale, a_ref, got_ref, w_ref, b_ref):
    total = add_wire(a_ref[...], got_ref[: a_ref.shape[0]], rows) * scale
    n = 9 * group
    chan = total.shape[1] // 2
    w_ref[0:9] = total[:n, :chan].reshape(9, group, chan)
    w_ref[9:18] = total[:n, chan:].reshape(9, group, chan)
    tail = total[n : n + n // 2]
    w_ref[18:27] = jnp.concatenate([tail[:, :chan], tail[:, chan:]], axis=0).reshape(9, group, chan)
    col = total[rows:, :group]
    eye = lax.broadcasted_iota(jnp.int32, (group, group), 0) == lax.broadcasted_iota(
        jnp.int32, (group, group), 1
    )
    b_ref[...] = jnp.sum(jnp.where(eye, col, 0.0), axis=0, keepdims=True)


def rounds(plan):
    out = []
    for axis in ("space", "rep"):
        size, bit = lax.axis_size(axis), 1
        while bit < size:
            out.append((axis, bit))
            bit *= 2
    return out


def exchange(wire, step):
    axis, bit = step
    return lax.ppermute(wire, axis, [(i, i ^ bit) for i in range(lax.axis_size(axis))])


def first_wire(part, plan):
    rows = part.shape[0] - plan.group
    return call(functools.partial(wire_kernel, rows), shape(part.shape, BF), 0, 1, name="wire")(part)


def grad_shapes(plan):
    return shape((27, plan.group, plan.chan), F32), shape((1, plan.group), F32)


def as_grads(weight, bias, plan):
    weight = jnp.transpose(weight.reshape(3, 3, 3, plan.group, plan.chan), (3, 4, 0, 1, 2))
    return weight, bias.reshape(plan.group)


def total_step(part, got, step, plan, share=None):
    rows = part.shape[0] - plan.group
    kernel, args, more = step_kernel, (part, got), 0
    if share is not None:
        kernel, args, more = join_kernel, (part, got, share), share.shape[0]
    part, wire = call(
        functools.partial(kernel, rows),
        (shape(part.shape, F32), shape((part.shape[0] + more, part.shape[1]), BF)),
        0,
        len(args),
        name="step",
    )(*args)
    return part, exchange(wire, step)


def total_last(part, got, plan, scale):
    rows = part.shape[0] - plan.group
    weight, bias = call(
        functools.partial(last_kernel, rows, plan.group, scale), grad_shapes(plan), 0, 2, name="last"
    )(part, got)
    return as_grads(weight, bias, plan)


def local(volume, weight1, bias1, weight2, bias2, upstream):
    _, group, layers, ny, nz = volume.shape
    chan = weight1.shape[1]
    spaces, groups = lax.axis_size("space"), lax.axis_size("filt")
    plan = Plan(layers, ny, nz, chan, groups, spaces)
    scale = 1.0 / math.sqrt(lax.axis_size("rep") * spaces * layers * ny * nz)

    cells = ny * nz
    conv = 2 * 27 * chan * chan * cells
    slots = VM((16 // ny, ny, chan, 2 * chan), BF)
    dma = pltpu.SemaphoreType.DMA
    padded = plan.padded()
    grad_rows = 27 * group // 2 + group
    grad_scratch = [VM((layers, ny + 2, 3 * group, nz), BF), VM((9 * group, 3 * chan), F32)]

    def early_layers(pieces):
        return call(
            functools.partial(early_kernel, plan, [p[1:] for p in pieces]),
            (shape((layers - 1, ny, chan, nz), BF), shape((layers - 1, ny, chan, nz), F32)),
            len(pieces),
            0,
            [VM(padded, BF), slots, dma((len(pieces),)), dma((groups,))],
            flops=1,
            name="early",
        )(*(p[0] for p in pieces))

    gather = gather_quick if plan.quick else gather_plain
    v_own, v_other, u_own, u_other, early = gather(
        volume[0], weight1, bias1, upstream[0], weight2, bias2, plan, early_layers
    )
    v_places = [p[1:] for p in v_own + v_other]
    u_places = [p[1:] for p in u_own + u_other]
    v_all = [p[0] for p in v_own + v_other]
    u_all = [p[0] for p in u_own + u_other]

    turned1 = call(
        functools.partial(turn_kernel, plan),
        shape((3, chan, 9 * chan), BF),
        groups,
        0,
        [slots, dma((groups,))],
        moved=2 << 20,
        name="turn",
    )(*v_all[:groups])

    hidden, slope = call(
        functools.partial(first_kernel, plan, v_places),
        (shape(padded, BF), shape((plan.count(2), ny, chan, nz), F32)),
        len(v_all) + len(early),
        0,
        [VM(padded, BF), slots, dma((len(v_all),)), dma((groups,)), dma((2,))],
        flops=1,
        name="first",
    )(*v_all, *early)

    if plan.quick:
        u_all[3] = flip_perm(after(u_all[2], hidden), 1)
    delta2, output, part2, turned2 = call(
        functools.partial(second_kernel, plan, u_places),
        (
            shape(padded, BF),
            shape((group, layers, ny, nz), BF),
            shape((grad_rows, 2 * chan), F32),
            shape((3, chan, 9 * chan), BF),
        ),
        len(u_all),
        1,
        [
            VM((plan.count(1), ny, chan, nz), BF),
            slots,
            VM((plan.count(1), ny, chan, nz), F32),
            *grad_scratch,
            dma((len(u_all),)),
            dma((groups,)),
        ],
        flops=1,
        name="second",
    )(*u_all, hidden)

    delta1, part1 = call(
        functools.partial(third_kernel, plan, v_places),
        (shape((layers, ny, chan, nz), BF), shape((grad_rows, 2 * chan), F32)),
        len(v_all),
        3,
        [VM(padded, BF), *grad_scratch, dma((len(v_all),))],
        flops=conv * layers,
        name="third",
    )(*v_all, slope, delta2, turned2)

    beside = [shape((ny * group, nz), BF)] * plan.sides
    own_grad, *shares = call(
        functools.partial(fourth_kernel, plan),
        (shape((layers, ny, group, nz), F32), *beside),
        1,
        1,
        [VM((layers + 4, ny + 2, chan, nz), BF), dma],
        flops=1,
        name="fourth",
    )(delta1, turned1)

    steps1 = rounds(plan)
    steps2 = steps1[1:] + steps1[:1]
    got1 = exchange(first_wire(part1, plan), steps1[0])
    got2 = exchange(first_wire(after(part2, part1), plan), steps2[0])
    for step in steps1[1:]:
        part1, got1 = total_step(part1, got1, step, plan)
    for n, step in enumerate(steps2[1:], 2):
        share = shares[0] if plan.pair and n == len(steps2) else None
        part2, got2 = total_step(part2, got2, step, plan, share)
    grad1, bias_grad1 = total_last(part1, got1, plan, scale)
    volume_shape = shape((group, layers, ny, nz), BF)
    finish_scratch = [VM((layers, ny, group, nz), F32), dma]
    if plan.pair:
        *grads2, volume_grad = call(
            functools.partial(close_kernel, plan, part2.shape[0] - group, scale),
            (*grad_shapes(plan), volume_shape),
            1,
            2,
            finish_scratch,
            name="close",
        )(own_grad, part2, got2)
        grad2, bias_grad2 = as_grads(*grads2, plan)
    else:
        grad2, bias_grad2 = total_last(part2, got2, plan, scale)
        volume_grad = call(
            functools.partial(finish_kernel, plan), volume_shape, 1, 2, finish_scratch, name="finish"
        )(own_grad, up(shares[1]), down(shares[0]))
    return (output[None], volume_grad[None], grad1, bias_grad1, grad2, bias_grad2)


def solution(mesh):
    field = P("rep", "filt", "space", None, None)
    kernel = P("filt", None, None, None, None)
    return jax.shard_map(
        local,
        mesh=mesh,
        in_specs=(field, kernel, P("filt"), kernel, P("filt"), field),
        out_specs=(field, field, kernel, P("filt"), kernel, P("filt")),
        check_vma=False,
    )
```

time: 59.7 us -> 48.8 us (0.82)
  Pallas kernels: 21.3 us -> 16.2 us
  local copies, waits for them, and re-layouts: 4.92 us -> 0 us
  starting transfers between devices: 22.5 us -> 18.4 us
  waiting for transfers between devices: 10 us -> 13.4 us
    unnamed x12 -> x0, local copies, waits for them, and re-layouts: 4.9 us -> none
    ppermute x19 -> x9, starting transfers between devices: 10 us -> 5.66 us  [flip_perm(): return lax.ppermute(value, 'filt', [(i, i ^ flip) for i in range(n)])]
    pallas_call x1, Pallas kernels: 5.04 us -> 1.78 us  [local(): call(functools.partial(first_kernel, plan, v_places), (shape(padded, BF),...]
    ppermute x6, waiting for transfers between devices: 2.31 us -> 4.76 us  [exchange(): lax.ppermute(wire, axis, [(i, i ^ bit) for i in range(lax.axis_size(axis))])]
    pallas_call x1, Pallas kernels: 6.24 us -> 3.95 us  [local(): call(functools.partial(second_kernel, plan, u_places), (shape(padded, BF)...]
    ppermute x19 -> x9, waiting for transfers between devices: 3.95 us -> 5.71 us  [flip_perm(): return lax.ppermute(value, 'filt', [(i, i ^ flip) for i in range(n)])]
    ppermute x6, starting transfers between devices: 9.89 us -> 11.2 us  [exchange(): lax.ppermute(wire, axis, [(i, i ^ bit) for i in range(lax.axis_size(axis))])]
    ppermute x3 -> x1, starting transfers between devices: 2.61 us -> 1.52 us  [over(): return lax.ppermute(value, 'space', [(0, 1), (1, 0)])]
  transfers between devices with their start and end apart: 28 -> 16, of which waited for: 7 -> 7; matrix products, arithmetic and copies ran while one was open for 0% -> 0% of each run, Pallas kernels for 24% -> 15%
where the time goes in v2:
time: 48.8 us; the launch traced here: 48.7 us
  starting transfers between devices  18.4 us (38%)
  Pallas kernels  16.2 us (33%)
  waiting for transfers between devices  13.4 us (27%)
  between operations  0.73 us (1%)
    ppermute x6, starting transfers between devices, exchange(): lax.ppermute(wire, axis, [(i, i ^ bit) for i in range(lax.axis_size(axis))])  11.2 us
    ppermute x9, waiting for transfers between devices, flip_perm(): return lax.ppermute(value, 'filt', [(i, i ^ flip) for i in range(n)])  5.71 us
    ppermute x9, starting transfers between devices, flip_perm(): return lax.ppermute(value, 'filt', [(i, i ^ flip) for i in range(n)])  5.66 us
    ppermute x6, waiting for transfers between devices, exchange(): lax.ppermute(wire, axis, [(i, i ^ bit) for i in range(lax.axis_size(axis))])  4.76 us
    pallas_call x1, Pallas kernels, local(): call(functools.partial(second_kernel, plan, u_places), (shape(padded, BF)...  3.95 us
    pallas_call x1, Pallas kernels, local(): call(functools.partial(third_kernel, plan, v_places), (shape((layers, ny,...  3.08 us
    ppermute x1, waiting for transfers between devices, over(): return lax.ppermute(value, 'space', [(0, 1), (1, 0)])  2.94 us
    pallas_call x2, Pallas kernels, pack(): pl.pallas_call(functools.partial(pack_kernel, edge), out_shape=tuple(outs...  2.2 us
  transfers between devices with their start and end apart: 16, of which 7 were waited for; matrix products, arithmetic and copies ran while one was open for 0% of the time, Pallas kernels for 15%

profile of v2, /device:TPU:0, one launch (start us, length us, event | category | flops | bytes accessed | tf_op | source)
XLA Modules:
  0.0 48.7 jit_solution(12966912158133147737)
XLA Ops:
  0.6 1.1 %pack1.1 = (bf16[6,8,16,128]{3,2,1,0:T(8,128)(2,1)S(1)}, bf16[4,8,16,128]{3,2,1,0:T(8,128)(2,1)S(1)}) custom-call(bf16[16,4,8,128]{3,2,1,0:T(8,128)(2,1)} %bitcast.22, bf16[27,16,64]{2,1,0:T(8,128)(2,1)} %bitcast.23, f32[1,16]{1,0:T(1,128)} %bitcast.25, bf16[16,4,8,128]{3,2,1,0:T(8,128)(2,1)} %bitcast.20), custom_call_target="tpu_custom_call" | custom-call | bytes 262144 | tf_op jit(solution)/shard_map/pack1/pallas_call | solution.py:122
  1.8 0.6 %collective-permute-start = (bf16[6,8,16,128]{3,2,1,0:T(8,128)(2,1)S(1)}, bf16[6,8,16,128]{3,2,1,0:T(8,128)(2,1)S(1)}, u32[]{:S(2)}, u32[]{:S(2)}) collective-permute-start(bf16[6,8,16,128]{3,2,1,0:T(8,128)(2,1)S(1)} %get-tuple-element.40.refs_0_), channel_id=1, source_target_pairs={{0,4},{4,0},{8,12},{12,8},{1,5},{5,1},{9,13},{13,9},{2,6},{6,2},{1... | collective-permute-start | bytes 589832 | tf_op jit(solution)/shard_map/ppermute | solution.py:170
  2.3 2.6 %collective-permute-start.2 = (bf16[6,8,16,128]{3,2,1,0:T(8,128)(2,1)S(1)}, bf16[6,8,16,128]{3,2,1,0:T(8,128)(2,1)S(1)}, u32[]{:S(2)}, u32[]{:S(2)}) collective-permute-start(bf16[6,8,16,128]{3,2,1,0:T(8,128)(2,1)S(1)} %get-tuple-element.40.refs_0_), channel_id=1, source_target_pairs={{0,8},{4,12},{8,0},{12,4},{1,9},{5,13},{9,1},{13,5},{2,10},{6,14},... | collective-permute-start | bytes 589832 | tf_op jit(solution)/shard_map/ppermute | solution.py:170
  4.9 1.5 %collective-permute-start.1 = (bf16[4,8,16,128]{3,2,1,0:T(8,128)(2,1)S(1)}, bf16[4,8,16,128]{3,2,1,0:T(8,128)(2,1)S(1)}, u32[]{:S(2)}, u32[]{:S(2)}) collective-permute-start(bf16[4,8,16,128]{3,2,1,0:T(8,128)(2,1)S(1)} %get-tuple-element.42), channel_id=1, source_target_pairs={{0,16},{16,0},{1,17},{17,1},{2,18},{18,2},{3,19},{19,3},{4,20},{20... | collective-permute-start | bytes 393224 | tf_op jit(solution)/shard_map/ppermute | solution.py:174
  6.4 1.1 %pack2.1.refs_0_ = bf16[6,8,16,128]{3,2,1,0:T(8,128)(2,1)S(1)} custom-call(bf16[16,4,8,128]{3,2,1,0:T(8,128)(2,1)} %bitcast.21, bf16[27,16,64]{2,1,0:T(8,128)(2,1)} %bitcast.24, f32[1,16]{1,0:T(1,128)} %bitcast.26), custom_call_target="tpu_custom_call" | custom-call | bytes 262144 | tf_op jit(solution)/shard_map/pack2/pallas_call | solution.py:122
  7.5 2.9 %collective-permute-done.1.refs_4_ = bf16[4,8,16,128]{3,2,1,0:T(8,128)(2,1)S(1)} collective-permute-done((bf16[4,8,16,128]{3,2,1,0:T(8,128)(2,1)S(1)}, bf16[4,8,16,128]{3,2,1,0:T(8,128)(2,1)S(1)}, u32[]{:S(2)}, u32[]{:S(2)}) %collective-permute-start.1) | collective-permute-done | bytes 131104 | tf_op jit(solution)/shard_map/ppermute | solution.py:174
  10.4 1.7 %collective-permute-start.7 = (bf16[4,8,16,128]{3,2,1,0:T(8,128)(2,1)S(1)}, bf16[4,8,16,128]{3,2,1,0:T(8,128)(2,1)S(1)}, u32[]{:S(2)}, u32[]{:S(2)}) collective-permute-start(bf16[4,8,16,128]{3,2,1,0:T(8,128)(2,1)S(1)} %collective-permute-done.1.refs_4_), channel_id=1, source_target_pairs={{0,8},{4,12},{8,0},{12,4},{1,9},{5,13},{9,1},{13,5},{2,10},{6,14},... | collective-permute-start | bytes 393224 | tf_op jit(solution)/shard_map/ppermute | solution.py:170
  12.1 0.3 collective-permute-start.5
  12.5 1.5 %early.1 = (bf16[3,8,64,128]{3,2,1,0:T(8,128)(2,1)S(1)}, f32[3,8,64,128]{3,2,1,0:T(8,128)S(1)}) custom-call(bf16[6,8,16,128]{3,2,1,0:T(8,128)(2,1)S(1)} %get-tuple-element.40.refs_0_, bf16[6,8,16,128]{3,2,1,0:T(8,128)(2,1)S(1)} %collective-permute-done.refs_1_, bf16[6,8,16,128]{3,2,1,0:T(8,128)(2,1)S(1)} %collective-permute-done.2.refs_2_, ...), custom_call_target="tpu_custom_call" | custom-call | flops 1 | tf_op jit(solution)/shard_map/early/pallas_call | solution.py:697
  14.0 2.8 %collective-permute-done.7.refs_6_ = bf16[4,8,16,128]{3,2,1,0:T(8,128)(2,1)S(1)} collective-permute-done((bf16[4,8,16,128]{3,2,1,0:T(8,128)(2,1)S(1)}, bf16[4,8,16,128]{3,2,1,0:T(8,128)(2,1)S(1)}, u32[]{:S(2)}, u32[]{:S(2)}) %collective-permute-start.7) | collective-permute-done | bytes 131104 | tf_op jit(solution)/shard_map/ppermute | solution.py:170
  16.8 0.5 %collective-permute-start.4 = (bf16[6,8,16,128]{3,2,1,0:T(8,128)(2,1)S(1)}, bf16[6,8,16,128]{3,2,1,0:T(8,128)(2,1)S(1)}, u32[]{:S(2)}, u32[]{:S(2)}) collective-permute-start(bf16[6,8,16,128]{3,2,1,0:T(8,128)(2,1)S(1)} %pack2.1.refs_0_), channel_id=1, source_target_pairs={{0,4},{4,0},{8,12},{12,8},{1,5},{5,1},{9,13},{13,9},{2,6},{6,2},{1... | collective-permute-start | bytes 589832 | tf_op jit(solution)/shard_map/ppermute | solution.py:170
  17.3 0.8 %collective-permute-done.8.refs_7_ = bf16[4,8,16,128]{3,2,1,0:T(8,128)(2,1)S(1)} collective-permute-done((bf16[4,8,16,128]{3,2,1,0:T(8,128)(2,1)S(1)}, bf16[4,8,16,128]{3,2,1,0:T(8,128)(2,1)S(1)}, u32[]{:S(2)}, u32[]{:S(2)}) %collective-permute-start.8) | collective-permute-done | bytes 131104 | tf_op jit(solution)/shard_map/ppermute | solution.py:170
  18.1 1.8 %first.1 = (bf16[10,10,64,128]{3,2,1,0:T(8,128)(2,1)S(1)}, f32[6,8,64,128]{3,2,1,0:T(8,128)S(1)}) custom-call(bf16[6,8,16,128]{3,2,1,0:T(8,128)(2,1)S(1)} %get-tuple-element.40.refs_0_, bf16[6,8,16,128]{3,2,1,0:T(8,128)(2,1)S(1)} %collective-permute-done.refs_1_, bf16[6,8,16,128]{3,2,1,0:T(8,128)(2,1)S(1)} %collective-permute-done.2.refs_2_, ...), custom_call_target="tpu_custom_call" | custom-call | flops 1 | tf_op jit(solution)/shard_map/first/pallas_call | solution.py:726
  19.9 0.6 %collective-permute-done.5.refs_2_ = bf16[6,8,16,128]{3,2,1,0:T(8,128)(2,1)S(1)} collective-permute-done((bf16[6,8,16,128]{3,2,1,0:T(8,128)(2,1)S(1)}, bf16[6,8,16,128]{3,2,1,0:T(8,128)(2,1)S(1)}, u32[]{:S(2)}, u32[]{:S(2)}) %collective-permute-start.5) | collective-permute-done | bytes 196640 | tf_op jit(solution)/shard_map/ppermute | solution.py:170
  20.6 1.4 %collective-permute-done.9.refs_3_ = bf16[6,8,16,128]{3,2,1,0:T(8,128)(2,1)S(1)} collective-permute-done((bf16[6,8,16,128]{3,2,1,0:T(8,128)(2,1)S(1)}, bf16[6,8,16,128]{3,2,1,0:T(8,128)(2,1)S(1)}, u32[]{:S(2)}, u32[]{:S(2)}) %collective-permute-start.9) | collective-permute-done | bytes 196640 | tf_op jit(solution)/shard_map/ppermute | solution.py:170
  22.0 3.9 %second.1 = (bf16[10,10,64,128]{3,2,1,0:T(8,128)(2,1)S(1)}, bf16[16,4,8,128]{3,2,1,0:T(8,128)(2,1)}, f32[232,128]{1,0:T(8,128)S(1)}, bf16[3,64,576]{2,1,0:T(8,128)(2,1)S(1)}) custom-call(bf16[6,8,16,128]{3,2,1,0:T(8,128)(2,1)S(1)} %pack2.1.refs_0_, bf16[6,8,16,128]{3,2,1,0:T(8,128)(2,1)S(1)} %collective-permute-done.4.refs_1_, ...), custom_call_target="tpu_custom_call" | custom-call | flops 1 | tf_op jit(solution)/shard_map/second/pallas_call | solution.py:738
  25.9 3.1 %third.1 = (bf16[4,8,64,128]{3,2,1,0:T(8,128)(2,1)S(1)}, f32[232,128]{1,0:T(8,128)S(1)}) custom-call(bf16[6,8,16,128]{3,2,1,0:T(8,128)(2,1)S(1)} %get-tuple-element.40.refs_0_, bf16[6,8,16,128]{3,2,1,0:T(8,128)(2,1)S(1)} %collective-permute-done.refs_1_, bf16[6,8,16,128]{3,2,1,0:T(8,128)(2,1)S(1)} %collective-permute-done.2.refs_2_, ...), custom_call_target="tpu_custom_call" | custom-call | flops 905969664 | tf_op jit(solution)/shard_map/third/pallas_call | solution.py:760
  29.1 1.8 %collective-permute-start.10 = (bf16[232,128]{1,0:T(8,128)(2,1)S(1)}, bf16[232,128]{1,0:T(8,128)(2,1)S(1)}, u32[]{:S(2)}, u32[]{:S(2)}) collective-permute-start(bf16[232,128]{1,0:T(8,128)(2,1)S(1)} %wire.2), channel_id=1, source_target_pairs={{0,1},{1,0},{2,3},{3,2},{4,5},{5,4},{6,7},{7,6},{8,9},{9,8},{10,11... | collective-permute-start | bytes 178184 | tf_op jit(solution)/shard_map/ppermute | solution.py:641
  30.9 1.6 %collective-permute-start.13 = (bf16[232,128]{1,0:T(8,128)(2,1)S(1)}, bf16[232,128]{1,0:T(8,128)(2,1)S(1)}, u32[]{:S(2)}, u32[]{:S(2)}) collective-permute-start(bf16[232,128]{1,0:T(8,128)(2,1)S(1)} %wire.3), channel_id=1, source_target_pairs={{0,16},{16,0},{1,17},{17,1},{2,18},{18,2},{3,19},{19,3},{4,20},{20... | collective-permute-start | bytes 178184 | tf_op jit(solution)/shard_map/ppermute | solution.py:641
  32.5 0.8 %collective-permute-done.10.got_ref = bf16[232,128]{1,0:T(8,128)(2,1)S(1)} collective-permute-done((bf16[232,128]{1,0:T(8,128)(2,1)S(1)}, bf16[232,128]{1,0:T(8,128)(2,1)S(1)}, u32[]{:S(2)}, u32[]{:S(2)}) %collective-permute-start.10) | collective-permute-done | bytes 59424 | tf_op jit(solution)/shard_map/ppermute | solution.py:641
  33.3 0.1 step.4
  33.4 2.8 %collective-permute-start.11 = (bf16[232,128]{1,0:T(8,128)(2,1)S(1)}, bf16[232,128]{1,0:T(8,128)(2,1)S(1)}, u32[]{:S(2)}, u32[]{:S(2)}) collective-permute-start(bf16[232,128]{1,0:T(8,128)(2,1)S(1)} %get-tuple-element.61), channel_id=1, source_target_pairs={{0,2},{1,3},{2,0},{3,1},{4,6},{5,7},{6,4},{7,5},{8,10},{9,11},{10,... | collective-permute-start | bytes 178184 | tf_op jit(solution)/shard_map/ppermute | solution.py:641
  36.3 1.6 %collective-permute-start.14 = (bf16[232,128]{1,0:T(8,128)(2,1)S(1)}, bf16[232,128]{1,0:T(8,128)(2,1)S(1)}, u32[]{:S(2)}, u32[]{:S(2)}) collective-permute-start(bf16[232,128]{1,0:T(8,128)(2,1)S(1)} %get-tuple-element.67), channel_id=1, source_target_pairs={{0,1},{1,0},{2,3},{3,2},{4,5},{5,4},{6,7},{7,6},{8,9},{9,8},{10,11... | collective-permute-start | bytes 178184 | tf_op jit(solution)/shard_map/ppermute | solution.py:641
  37.9 0.3 turn.1.t_ref
  38.2 1.3 %fourth.1 = (f32[4,8,16,128]{3,2,1,0:T(8,128)S(1)}, bf16[128,128]{1,0:T(8,128)(2,1)S(1)}) custom-call(bf16[4,8,64,128]{3,2,1,0:T(8,128)(2,1)S(1)} %get-tuple-element.55.d_ref, bf16[3,64,576]{2,1,0:T(8,128)(2,1)S(1)} %turn.1.t_ref), custom_call_target="tpu_custom_call" | custom-call | flops 1 | tf_op jit(solution)/shard_map/fourth/pallas_call | solution.py:771
  39.6 0.1 step.5
  39.7 1.5 %collective-permute-start.12 = (bf16[360,128]{1,0:T(8,128)(2,1)S(1)}, bf16[360,128]{1,0:T(8,128)(2,1)S(1)}, u32[]{:S(2)}, u32[]{:S(2)}) collective-permute-start(bf16[360,128]{1,0:T(8,128)(2,1)S(1)} %get-tuple-element.64), channel_id=1, source_target_pairs={{0,16},{16,0},{1,17},{17,1},{2,18},{18,2},{3,19},{19,3},{4,20},{20... | collective-permute-start | bytes 276488 | tf_op jit(solution)/shard_map/ppermute | solution.py:641
  41.2 0.1 step.7
  41.3 1.8 %collective-permute-start.15 = (bf16[232,128]{1,0:T(8,128)(2,1)S(1)}, bf16[232,128]{1,0:T(8,128)(2,1)S(1)}, u32[]{:S(2)}, u32[]{:S(2)}) collective-permute-start(bf16[232,128]{1,0:T(8,128)(2,1)S(1)} %get-tuple-element.69), channel_id=1, source_target_pairs={{0,2},{1,3},{2,0},{3,1},{4,6},{5,7},{6,4},{7,5},{8,10},{9,11},{10,... | collective-permute-start | bytes 178184 | tf_op jit(solution)/shard_map/ppermute | solution.py:641
  43.1 3.9 %collective-permute-done.15.got_ref = bf16[232,128]{1,0:T(8,128)(2,1)S(1)} collective-permute-done((bf16[232,128]{1,0:T(8,128)(2,1)S(1)}, bf16[232,128]{1,0:T(8,128)(2,1)S(1)}, u32[]{:S(2)}, u32[]{:S(2)}) %collective-permute-start.15) | collective-permute-done | bytes 59424 | tf_op jit(solution)/shard_map/ppermute | solution.py:641
  47.0 0.8 %last.1 = (f32[27,16,64]{2,1,0:T(8,128)}, f32[1,16]{1,0:T(1,128)}) custom-call(f32[232,128]{1,0:T(8,128)S(1)} %get-tuple-element.68.a_ref, bf16[232,128]{1,0:T(8,128)(2,1)S(1)} %collective-permute-done.15.got_ref), custom_call_target="tpu_custom_call" | custom-call | tf_op jit(solution)/shard_map/last/pallas_call | solution.py:675
  47.8 0.9 %close.1 = (f32[27,16,64]{2,1,0:T(8,128)}, f32[1,16]{1,0:T(1,128)}, bf16[16,4,8,128]{3,2,1,0:T(8,128)(2,1)}) custom-call(f32[4,8,16,128]{3,2,1,0:T(8,128)S(1)} %get-tuple-element.56.r_hbm, f32[232,128]{1,0:T(8,128)S(1)} %get-tuple-element.63.a_ref, bf16[360,128]{1,0:T(8,128)(2,1)S(1)} %collective-permute-done.12.got_ref), custom_call_target="tpu_custom_call" | custom-call | tf_op jit(solution)/shard_map/close/pallas_call | solution.py:794
  (16 shorter events, 0.1 us)
Async XLA Ops:
  1.8 4.6 %collective-permute-start = (bf16[6,8,16,128]{3,2,1,0:T(8,128)(2,1)S(1)}, bf16[6,8,16,128]{3,2,1,0:T(8,128)(2,1)S(1)}, u32[]{:S(2)}, u32[]{:S(2)}) collective-permute-start(bf16[6,8,16,128]{3,2,1,0:T(8,128)(2,1)S(1)} %get-tuple-element.40.refs_0_), channel_id=1, source_target_pairs={{0,4},{4,0},{8,12},{12,8},{1,5},{5,1},{9,13},{13,9},{2,6},{6,2},{1... | collective-permute-start | bytes 589832 | tf_op jit(solution)/shard_map/ppermute | solution.py:170
  2.3 8.1 %collective-permute-start.2 = (bf16[6,8,16,128]{3,2,1,0:T(8,128)(2,1)S(1)}, bf16[6,8,16,128]{3,2,1,0:T(8,128)(2,1)S(1)}, u32[]{:S(2)}, u32[]{:S(2)}) collective-permute-start(bf16[6,8,16,128]{3,2,1,0:T(8,128)(2,1)S(1)} %get-tuple-element.40.refs_0_), channel_id=1, source_target_pairs={{0,8},{4,12},{8,0},{12,4},{1,9},{5,13},{9,1},{13,5},{2,10},{6,14},... | collective-permute-start | bytes 589832 | tf_op jit(solution)/shard_map/ppermute | solution.py:170
  4.9 5.6 %collective-permute-start.1 = (bf16[4,8,16,128]{3,2,1,0:T(8,128)(2,1)S(1)}, bf16[4,8,16,128]{3,2,1,0:T(8,128)(2,1)S(1)}, u32[]{:S(2)}, u32[]{:S(2)}) collective-permute-start(bf16[4,8,16,128]{3,2,1,0:T(8,128)(2,1)S(1)} %get-tuple-element.42), channel_id=1, source_target_pairs={{0,16},{16,0},{1,17},{17,1},{2,18},{18,2},{3,19},{19,3},{4,20},{20... | collective-permute-start | bytes 393224 | tf_op jit(solution)/shard_map/ppermute | solution.py:174
  10.4 2.0 %collective-permute-start.3 = (bf16[6,8,16,128]{3,2,1,0:T(8,128)(2,1)S(1)}, bf16[6,8,16,128]{3,2,1,0:T(8,128)(2,1)S(1)}, u32[]{:S(2)}, u32[]{:S(2)}) collective-permute-start(bf16[6,8,16,128]{3,2,1,0:T(8,128)(2,1)S(1)} %collective-permute-done.2.refs_2_), channel_id=1, source_target_pairs={{0,4},{4,0},{8,12},{12,8},{1,5},{5,1},{9,13},{13,9},{2,6},{6,2},{1... | collective-permute-start | bytes 589832 | tf_op jit(solution)/shard_map/ppermute | solution.py:170
  10.4 6.4 %collective-permute-start.7 = (bf16[4,8,16,128]{3,2,1,0:T(8,128)(2,1)S(1)}, bf16[4,8,16,128]{3,2,1,0:T(8,128)(2,1)S(1)}, u32[]{:S(2)}, u32[]{:S(2)}) collective-permute-start(bf16[4,8,16,128]{3,2,1,0:T(8,128)(2,1)S(1)} %collective-permute-done.1.refs_4_), channel_id=1, source_target_pairs={{0,8},{4,12},{8,0},{12,4},{1,9},{5,13},{9,1},{13,5},{2,10},{6,14},... | collective-permute-start | bytes 393224 | tf_op jit(solution)/shard_map/ppermute | solution.py:170
  12.1 8.4 %collective-permute-start.5 = (bf16[6,8,16,128]{3,2,1,0:T(8,128)(2,1)S(1)}, bf16[6,8,16,128]{3,2,1,0:T(8,128)(2,1)S(1)}, u32[]{:S(2)}, u32[]{:S(2)}) collective-permute-start(bf16[6,8,16,128]{3,2,1,0:T(8,128)(2,1)S(1)} %pack2.1.refs_0_), channel_id=1, source_target_pairs={{0,8},{4,12},{8,0},{12,4},{1,9},{5,13},{9,1},{13,5},{2,10},{6,14},... | collective-permute-start | bytes 589832 | tf_op jit(solution)/shard_map/ppermute | solution.py:170
  12.5 4.9 %collective-permute-start.6 = (bf16[4,8,16,128]{3,2,1,0:T(8,128)(2,1)S(1)}, bf16[4,8,16,128]{3,2,1,0:T(8,128)(2,1)S(1)}, u32[]{:S(2)}, u32[]{:S(2)}) collective-permute-start(bf16[4,8,16,128]{3,2,1,0:T(8,128)(2,1)S(1)} %collective-permute-done.1.refs_4_), channel_id=1, source_target_pairs={{0,4},{4,0},{8,12},{12,8},{1,5},{5,1},{9,13},{13,9},{2,6},{6,2},{1... | collective-permute-start | bytes 393224 | tf_op jit(solution)/shard_map/ppermute | solution.py:170
  16.8 1.3 %collective-permute-start.8 = (bf16[4,8,16,128]{3,2,1,0:T(8,128)(2,1)S(1)}, bf16[4,8,16,128]{3,2,1,0:T(8,128)(2,1)S(1)}, u32[]{:S(2)}, u32[]{:S(2)}) collective-permute-start(bf16[4,8,16,128]{3,2,1,0:T(8,128)(2,1)S(1)} %collective-permute-done.7.refs_6_), channel_id=1, source_target_pairs={{0,4},{4,0},{8,12},{12,8},{1,5},{5,1},{9,13},{13,9},{2,6},{6,2},{1... | collective-permute-start | bytes 393224 | tf_op jit(solution)/shard_map/ppermute | solution.py:170
  16.8 3.8 %collective-permute-start.4 = (bf16[6,8,16,128]{3,2,1,0:T(8,128)(2,1)S(1)}, bf16[6,8,16,128]{3,2,1,0:T(8,128)(2,1)S(1)}, u32[]{:S(2)}, u32[]{:S(2)}) collective-permute-start(bf16[6,8,16,128]{3,2,1,0:T(8,128)(2,1)S(1)} %pack2.1.refs_0_), channel_id=1, source_target_pairs={{0,4},{4,0},{8,12},{12,8},{1,5},{5,1},{9,13},{13,9},{2,6},{6,2},{1... | collective-permute-start | bytes 589832 | tf_op jit(solution)/shard_map/ppermute | solution.py:170
  20.6 1.4 %collective-permute-start.9 = (bf16[6,8,16,128]{3,2,1,0:T(8,128)(2,1)S(1)}, bf16[6,8,16,128]{3,2,1,0:T(8,128)(2,1)S(1)}, u32[]{:S(2)}, u32[]{:S(2)}) collective-permute-start(bf16[6,8,16,128]{3,2,1,0:T(8,128)(2,1)S(1)} %collective-permute-done.5.refs_2_), channel_id=1, source_target_pairs={{0,4},{4,0},{8,12},{12,8},{1,5},{5,1},{9,13},{13,9},{2,6},{6,2},{1... | collective-permute-start | bytes 589832 | tf_op jit(solution)/shard_map/ppermute | solution.py:170
  29.1 4.3 %collective-permute-start.10 = (bf16[232,128]{1,0:T(8,128)(2,1)S(1)}, bf16[232,128]{1,0:T(8,128)(2,1)S(1)}, u32[]{:S(2)}, u32[]{:S(2)}) collective-permute-start(bf16[232,128]{1,0:T(8,128)(2,1)S(1)} %wire.2), channel_id=1, source_target_pairs={{0,1},{1,0},{2,3},{3,2},{4,5},{5,4},{6,7},{7,6},{8,9},{9,8},{10,11... | collective-permute-start | bytes 178184 | tf_op jit(solution)/shard_map/ppermute | solution.py:641
  30.9 5.3 %collective-permute-start.13 = (bf16[232,128]{1,0:T(8,128)(2,1)S(1)}, bf16[232,128]{1,0:T(8,128)(2,1)S(1)}, u32[]{:S(2)}, u32[]{:S(2)}) collective-permute-start(bf16[232,128]{1,0:T(8,128)(2,1)S(1)} %wire.3), channel_id=1, source_target_pairs={{0,16},{16,0},{1,17},{17,1},{2,18},{18,2},{3,19},{19,3},{4,20},{20... | collective-permute-start | bytes 178184 | tf_op jit(solution)/shard_map/ppermute | solution.py:641
  33.4 6.2 %collective-permute-start.11 = (bf16[232,128]{1,0:T(8,128)(2,1)S(1)}, bf16[232,128]{1,0:T(8,128)(2,1)S(1)}, u32[]{:S(2)}, u32[]{:S(2)}) collective-permute-start(bf16[232,128]{1,0:T(8,128)(2,1)S(1)} %get-tuple-element.61), channel_id=1, source_target_pairs={{0,2},{1,3},{2,0},{3,1},{4,6},{5,7},{6,4},{7,5},{8,10},{9,11},{10,... | collective-permute-start | bytes 178184 | tf_op jit(solution)/shard_map/ppermute | solution.py:641
  36.3 4.9 %collective-permute-start.14 = (bf16[232,128]{1,0:T(8,128)(2,1)S(1)}, bf16[232,128]{1,0:T(8,128)(2,1)S(1)}, u32[]{:S(2)}, u32[]{:S(2)}) collective-permute-start(bf16[232,128]{1,0:T(8,128)(2,1)S(1)} %get-tuple-element.67), channel_id=1, source_target_pairs={{0,1},{1,0},{2,3},{3,2},{4,5},{5,4},{6,7},{7,6},{8,9},{9,8},{10,11... | collective-permute-start | bytes 178184 | tf_op jit(solution)/shard_map/ppermute | solution.py:641
  39.7 8.2 %collective-permute-start.12 = (bf16[360,128]{1,0:T(8,128)(2,1)S(1)}, bf16[360,128]{1,0:T(8,128)(2,1)S(1)}, u32[]{:S(2)}, u32[]{:S(2)}) collective-permute-start(bf16[360,128]{1,0:T(8,128)(2,1)S(1)} %get-tuple-element.64), channel_id=1, source_target_pairs={{0,16},{16,0},{1,17},{17,1},{2,18},{18,2},{3,19},{19,3},{4,20},{20... | collective-permute-start | bytes 276488 | tf_op jit(solution)/shard_map/ppermute | solution.py:641
  41.3 5.8 %collective-permute-start.15 = (bf16[232,128]{1,0:T(8,128)(2,1)S(1)}, bf16[232,128]{1,0:T(8,128)(2,1)S(1)}, u32[]{:S(2)}, u32[]{:S(2)}) collective-permute-start(bf16[232,128]{1,0:T(8,128)(2,1)S(1)} %get-tuple-element.69), channel_id=1, source_target_pairs={{0,2},{1,3},{2,0},{3,1},{4,6},{5,7},{6,4},{7,5},{8,10},{9,11},{10,... | collective-permute-start | bytes 178184 | tf_op jit(solution)/shard_map/ppermute | solution.py:641

commit v3 on v2

--- a/solution.py
+++ b/solution.py
@@ -602,13 +602,15 @@
     w_ref[total.shape[0] :] = share_ref[...]
 
 
-def close_kernel(plan, rows, scale, r_hbm, a_ref, got_ref, w_ref, b_ref, o_ref, r_ref, sem):
+def close_kernel(plan, rows, scale, r_hbm, a1_ref, got1_ref, a2_ref, got2_ref, *refs):
+    w1_ref, b1_ref, w2_ref, b2_ref, o_ref, r_ref, sem = refs
     copy = pltpu.make_async_copy(r_hbm, r_ref, sem)
     copy.start()
-    last_kernel(rows, plan.group, scale, a_ref, got_ref, w_ref, b_ref)
+    last_kernel(rows, plan.group, scale, a1_ref, got1_ref, w1_ref, b1_ref)
+    last_kernel(rows, plan.group, scale, a2_ref, got2_ref, w2_ref, b2_ref)
     copy.wait()
     layer = (1 - lax.axis_index("space")) * (plan.layers - 1)
-    finish_volume(plan, r_ref, [(layer, got_ref, a_ref.shape[0])], o_ref)
+    finish_volume(plan, r_ref, [(layer, got2_ref, a2_ref.shape[0])], o_ref)
 
 
 def last_kernel(rows, group, scale, a_ref, got_ref, w_ref, b_ref):
@@ -763,7 +765,7 @@
         len(v_all),
         3,
         [VM(padded, BF), *grad_scratch, dma((len(v_all),))],
-        flops=conv * layers,
+        flops=1,
         name="third",
     )(*v_all, slope, delta2, turned2)
 
@@ -781,26 +783,27 @@
     steps1 = rounds(plan)
     steps2 = steps1[1:] + steps1[:1]
     got1 = exchange(first_wire(part1, plan), steps1[0])
-    got2 = exchange(first_wire(after(part2, part1), plan), steps2[0])
+    got2 = exchange(first_wire(part2, plan), steps2[0])
     for step in steps1[1:]:
         part1, got1 = total_step(part1, got1, step, plan)
     for n, step in enumerate(steps2[1:], 2):
         share = shares[0] if plan.pair and n == len(steps2) else None
         part2, got2 = total_step(part2, got2, step, plan, share)
-    grad1, bias_grad1 = total_last(part1, got1, plan, scale)
     volume_shape = shape((group, layers, ny, nz), BF)
     finish_scratch = [VM((layers, ny, group, nz), F32), dma]
     if plan.pair:
-        *grads2, volume_grad = call(
+        w1, b1, w2, b2, volume_grad = call(
             functools.partial(close_kernel, plan, part2.shape[0] - group, scale),
-            (*grad_shapes(plan), volume_shape),
+            (*grad_shapes(plan), *grad_shapes(plan), volume_shape),
             1,
-            2,
+            4,
             finish_scratch,
             name="close",
-        )(own_grad, part2, got2)
-        grad2, bias_grad2 = as_grads(*grads2, plan)
+        )(own_grad, part1, got1, part2, got2)
+        grad1, bias_grad1 = as_grads(w1, b1, plan)
+        grad2, bias_grad2 = as_grads(w2, b2, plan)
     else:
+        grad1, bias_grad1 = total_last(part1, got1, plan, scale)
         grad2, bias_grad2 = total_last(part2, got2, plan, scale)
         volume_grad = call(
             functools.partial(finish_kernel, plan), volume_shape, 1, 2, finish_scratch, name="finish"

time: 48.8 us -> 45.8 us (0.939)
  starting transfers between devices: 18.4 us -> 16.9 us
  waiting for transfers between devices: 13.4 us -> 12.5 us
  Pallas kernels: 16.2 us -> 15.5 us
    ppermute x6, starting transfers between devices: 11.2 us -> 9.74 us  [exchange(): lax.ppermute(wire, axis, [(i, i ^ bit) for i in range(lax.axis_size(axis))])]
    ppermute x6, waiting for transfers between devices: 4.76 us -> 3.84 us  [exchange(): lax.ppermute(wire, axis, [(i, i ^ bit) for i in range(lax.axis_size(axis))])]
    pallas_call x1 -> x0, Pallas kernels: 0.79 us -> none  [total_last(): call(functools.partial(last_kernel, rows, plan.group, scale), grad_shapes...]
  transfers between devices with their start and end apart: 16 -> 16, of which waited for: 7 -> 8; matrix products, arithmetic and copies ran while one was open for 0% -> 0% of each run, Pallas kernels for 15% -> 21%
where the time goes in v3:
time: 45.8 us; the launch traced here: 45.6 us
  starting transfers between devices  16.9 us (37%)
  Pallas kernels  15.5 us (34%)
  waiting for transfers between devices  12.5 us (27%)
  between operations  0.73 us (2%)
    ppermute x6, starting transfers between devices, exchange(): lax.ppermute(wire, axis, [(i, i ^ bit) for i in range(lax.axis_size(axis))])  9.74 us
    ppermute x9, waiting for transfers between devices, flip_perm(): return lax.ppermute(value, 'filt', [(i, i ^ flip) for i in range(n)])  5.71 us
    ppermute x9, starting transfers between devices, flip_perm(): return lax.ppermute(value, 'filt', [(i, i ^ flip) for i in range(n)])  5.66 us
    pallas_call x1, Pallas kernels, local(): call(functools.partial(second_kernel, plan, u_places), (shape(padded, BF)...  3.95 us
    ppermute x6, waiting for transfers between devices, exchange(): lax.ppermute(wire, axis, [(i, i ^ bit) for i in range(lax.axis_size(axis))])  3.84 us
    pallas_call x1, Pallas kernels, local(): call(functools.partial(third_kernel, plan, v_places), (shape((layers, ny,...  3.06 us
    ppermute x1, waiting for transfers between devices, over(): return lax.ppermute(value, 'space', [(0, 1), (1, 0)])  2.94 us
    pallas_call x2, Pallas kernels, pack(): pl.pallas_call(functools.partial(pack_kernel, edge), out_shape=tuple(outs...  2.2 us
  transfers between devices with their start and end apart: 16, of which 8 were waited for; matrix products, arithmetic and copies ran while one was open for 0% of the time, Pallas kernels for 21%

profile of v3, /device:TPU:0, one launch (start us, length us, event | category | flops | bytes accessed | tf_op | source)
XLA Modules:
  0.0 45.6 jit_solution(9229683888071461294)
XLA Ops:
  0.6 1.1 %pack1.1 = (bf16[6,8,16,128]{3,2,1,0:T(8,128)(2,1)S(1)}, bf16[4,8,16,128]{3,2,1,0:T(8,128)(2,1)S(1)}) custom-call(bf16[16,4,8,128]{3,2,1,0:T(8,128)(2,1)} %bitcast.22, bf16[27,16,64]{2,1,0:T(8,128)(2,1)} %bitcast.23, f32[1,16]{1,0:T(1,128)} %bitcast.25, bf16[16,4,8,128]{3,2,1,0:T(8,128)(2,1)} %bitcast.20), custom_call_target="tpu_custom_call" | custom-call | bytes 262144 | tf_op jit(solution)/shard_map/pack1/pallas_call | solution.py:122
  1.8 0.6 %collective-permute-start = (bf16[6,8,16,128]{3,2,1,0:T(8,128)(2,1)S(1)}, bf16[6,8,16,128]{3,2,1,0:T(8,128)(2,1)S(1)}, u32[]{:S(2)}, u32[]{:S(2)}) collective-permute-start(bf16[6,8,16,128]{3,2,1,0:T(8,128)(2,1)S(1)} %get-tuple-element.39.refs_0_), channel_id=1, source_target_pairs={{0,4},{4,0},{8,12},{12,8},{1,5},{5,1},{9,13},{13,9},{2,6},{6,2},{1... | collective-permute-start | bytes 589832 | tf_op jit(solution)/shard_map/ppermute | solution.py:170
  2.3 2.6 %collective-permute-start.2 = (bf16[6,8,16,128]{3,2,1,0:T(8,128)(2,1)S(1)}, bf16[6,8,16,128]{3,2,1,0:T(8,128)(2,1)S(1)}, u32[]{:S(2)}, u32[]{:S(2)}) collective-permute-start(bf16[6,8,16,128]{3,2,1,0:T(8,128)(2,1)S(1)} %get-tuple-element.39.refs_0_), channel_id=1, source_target_pairs={{0,8},{4,12},{8,0},{12,4},{1,9},{5,13},{9,1},{13,5},{2,10},{6,14},... | collective-permute-start | bytes 589832 | tf_op jit(solution)/shard_map/ppermute | solution.py:170
  4.9 1.5 %collective-permute-start.1 = (bf16[4,8,16,128]{3,2,1,0:T(8,128)(2,1)S(1)}, bf16[4,8,16,128]{3,2,1,0:T(8,128)(2,1)S(1)}, u32[]{:S(2)}, u32[]{:S(2)}) collective-permute-start(bf16[4,8,16,128]{3,2,1,0:T(8,128)(2,1)S(1)} %get-tuple-element.41), channel_id=1, source_target_pairs={{0,16},{16,0},{1,17},{17,1},{2,18},{18,2},{3,19},{19,3},{4,20},{20... | collective-permute-start | bytes 393224 | tf_op jit(solution)/shard_map/ppermute | solution.py:174
  6.4 1.1 %pack2.1.refs_0_ = bf16[6,8,16,128]{3,2,1,0:T(8,128)(2,1)S(1)} custom-call(bf16[16,4,8,128]{3,2,1,0:T(8,128)(2,1)} %bitcast.21, bf16[27,16,64]{2,1,0:T(8,128)(2,1)} %bitcast.24, f32[1,16]{1,0:T(1,128)} %bitcast.26), custom_call_target="tpu_custom_call" | custom-call | bytes 262144 | tf_op jit(solution)/shard_map/pack2/pallas_call | solution.py:122
  7.5 2.9 %collective-permute-done.1.refs_4_ = bf16[4,8,16,128]{3,2,1,0:T(8,128)(2,1)S(1)} collective-permute-done((bf16[4,8,16,128]{3,2,1,0:T(8,128)(2,1)S(1)}, bf16[4,8,16,128]{3,2,1,0:T(8,128)(2,1)S(1)}, u32[]{:S(2)}, u32[]{:S(2)}) %collective-permute-start.1) | collective-permute-done | bytes 131104 | tf_op jit(solution)/shard_map/ppermute | solution.py:174
  10.4 1.7 %collective-permute-start.7 = (bf16[4,8,16,128]{3,2,1,0:T(8,128)(2,1)S(1)}, bf16[4,8,16,128]{3,2,1,0:T(8,128)(2,1)S(1)}, u32[]{:S(2)}, u32[]{:S(2)}) collective-permute-start(bf16[4,8,16,128]{3,2,1,0:T(8,128)(2,1)S(1)} %collective-permute-done.1.refs_4_), channel_id=1, source_target_pairs={{0,8},{4,12},{8,0},{12,4},{1,9},{5,13},{9,1},{13,5},{2,10},{6,14},... | collective-permute-start | bytes 393224 | tf_op jit(solution)/shard_map/ppermute | solution.py:170
  12.1 0.3 collective-permute-start.5
  12.5 1.5 %early.1 = (bf16[3,8,64,128]{3,2,1,0:T(8,128)(2,1)S(1)}, f32[3,8,64,128]{3,2,1,0:T(8,128)S(1)}) custom-call(bf16[6,8,16,128]{3,2,1,0:T(8,128)(2,1)S(1)} %get-tuple-element.39.refs_0_, bf16[6,8,16,128]{3,2,1,0:T(8,128)(2,1)S(1)} %collective-permute-done.refs_1_, bf16[6,8,16,128]{3,2,1,0:T(8,128)(2,1)S(1)} %collective-permute-done.2.refs_2_, ...), custom_call_target="tpu_custom_call" | custom-call | flops 1 | tf_op jit(solution)/shard_map/early/pallas_call | solution.py:699
  14.0 2.8 %collective-permute-done.7.refs_6_ = bf16[4,8,16,128]{3,2,1,0:T(8,128)(2,1)S(1)} collective-permute-done((bf16[4,8,16,128]{3,2,1,0:T(8,128)(2,1)S(1)}, bf16[4,8,16,128]{3,2,1,0:T(8,128)(2,1)S(1)}, u32[]{:S(2)}, u32[]{:S(2)}) %collective-permute-start.7) | collective-permute-done | bytes 131104 | tf_op jit(solution)/shard_map/ppermute | solution.py:170
  16.8 0.5 %collective-permute-start.4 = (bf16[6,8,16,128]{3,2,1,0:T(8,128)(2,1)S(1)}, bf16[6,8,16,128]{3,2,1,0:T(8,128)(2,1)S(1)}, u32[]{:S(2)}, u32[]{:S(2)}) collective-permute-start(bf16[6,8,16,128]{3,2,1,0:T(8,128)(2,1)S(1)} %pack2.1.refs_0_), channel_id=1, source_target_pairs={{0,4},{4,0},{8,12},{12,8},{1,5},{5,1},{9,13},{13,9},{2,6},{6,2},{1... | collective-permute-start | bytes 589832 | tf_op jit(solution)/shard_map/ppermute | solution.py:170
  17.3 0.8 %collective-permute-done.8.refs_7_ = bf16[4,8,16,128]{3,2,1,0:T(8,128)(2,1)S(1)} collective-permute-done((bf16[4,8,16,128]{3,2,1,0:T(8,128)(2,1)S(1)}, bf16[4,8,16,128]{3,2,1,0:T(8,128)(2,1)S(1)}, u32[]{:S(2)}, u32[]{:S(2)}) %collective-permute-start.8) | collective-permute-done | bytes 131104 | tf_op jit(solution)/shard_map/ppermute | solution.py:170
  18.1 1.8 %first.1 = (bf16[10,10,64,128]{3,2,1,0:T(8,128)(2,1)S(1)}, f32[6,8,64,128]{3,2,1,0:T(8,128)S(1)}) custom-call(bf16[6,8,16,128]{3,2,1,0:T(8,128)(2,1)S(1)} %get-tuple-element.39.refs_0_, bf16[6,8,16,128]{3,2,1,0:T(8,128)(2,1)S(1)} %collective-permute-done.refs_1_, bf16[6,8,16,128]{3,2,1,0:T(8,128)(2,1)S(1)} %collective-permute-done.2.refs_2_, ...), custom_call_target="tpu_custom_call" | custom-call | flops 1 | tf_op jit(solution)/shard_map/first/pallas_call | solution.py:728
  19.9 0.6 %collective-permute-done.5.refs_2_ = bf16[6,8,16,128]{3,2,1,0:T(8,128)(2,1)S(1)} collective-permute-done((bf16[6,8,16,128]{3,2,1,0:T(8,128)(2,1)S(1)}, bf16[6,8,16,128]{3,2,1,0:T(8,128)(2,1)S(1)}, u32[]{:S(2)}, u32[]{:S(2)}) %collective-permute-start.5) | collective-permute-done | bytes 196640 | tf_op jit(solution)/shard_map/ppermute | solution.py:170
  20.6 1.4 %collective-permute-done.9.refs_3_ = bf16[6,8,16,128]{3,2,1,0:T(8,128)(2,1)S(1)} collective-permute-done((bf16[6,8,16,128]{3,2,1,0:T(8,128)(2,1)S(1)}, bf16[6,8,16,128]{3,2,1,0:T(8,128)(2,1)S(1)}, u32[]{:S(2)}, u32[]{:S(2)}) %collective-permute-start.9) | collective-permute-done | bytes 196640 | tf_op jit(solution)/shard_map/ppermute | solution.py:170
  22.0 3.9 %second.1 = (bf16[10,10,64,128]{3,2,1,0:T(8,128)(2,1)S(1)}, bf16[16,4,8,128]{3,2,1,0:T(8,128)(2,1)}, f32[232,128]{1,0:T(8,128)S(1)}, bf16[3,64,576]{2,1,0:T(8,128)(2,1)S(1)}) custom-call(bf16[6,8,16,128]{3,2,1,0:T(8,128)(2,1)S(1)} %pack2.1.refs_0_, bf16[6,8,16,128]{3,2,1,0:T(8,128)(2,1)S(1)} %collective-permute-done.4.refs_1_, ...), custom_call_target="tpu_custom_call" | custom-call | flops 1 | tf_op jit(solution)/shard_map/second/pallas_call | solution.py:740
  26.0 1.8 %collective-permute-start.13 = (bf16[232,128]{1,0:T(8,128)(2,1)S(1)}, bf16[232,128]{1,0:T(8,128)(2,1)S(1)}, u32[]{:S(2)}, u32[]{:S(2)}) collective-permute-start(bf16[232,128]{1,0:T(8,128)(2,1)S(1)} %wire.3), channel_id=1, source_target_pairs={{0,1},{1,0},{2,3},{3,2},{4,5},{5,4},{6,7},{7,6},{8,9},{9,8},{10,11... | collective-permute-start | bytes 178184 | tf_op jit(solution)/shard_map/ppermute | solution.py:643
  27.8 3.1 %third.1 = (bf16[4,8,64,128]{3,2,1,0:T(8,128)(2,1)S(1)}, f32[232,128]{1,0:T(8,128)S(1)}) custom-call(bf16[6,8,16,128]{3,2,1,0:T(8,128)(2,1)S(1)} %get-tuple-element.39.refs_0_, bf16[6,8,16,128]{3,2,1,0:T(8,128)(2,1)S(1)} %collective-permute-done.refs_1_, bf16[6,8,16,128]{3,2,1,0:T(8,128)(2,1)S(1)} %collective-permute-done.2.refs_2_, ...), custom_call_target="tpu_custom_call" | custom-call | flops 1 | tf_op jit(solution)/shard_map/third/pallas_call | solution.py:762
  30.9 1.6 %collective-permute-start.10 = (bf16[232,128]{1,0:T(8,128)(2,1)S(1)}, bf16[232,128]{1,0:T(8,128)(2,1)S(1)}, u32[]{:S(2)}, u32[]{:S(2)}) collective-permute-start(bf16[232,128]{1,0:T(8,128)(2,1)S(1)} %wire.2), channel_id=1, source_target_pairs={{0,16},{16,0},{1,17},{17,1},{2,18},{18,2},{3,19},{19,3},{4,20},{20... | collective-permute-start | bytes 178184 | tf_op jit(solution)/shard_map/ppermute | solution.py:643
  32.5 0.1 step.6
  32.6 2.6 %collective-permute-start.14 = (bf16[232,128]{1,0:T(8,128)(2,1)S(1)}, bf16[232,128]{1,0:T(8,128)(2,1)S(1)}, u32[]{:S(2)}, u32[]{:S(2)}) collective-permute-start(bf16[232,128]{1,0:T(8,128)(2,1)S(1)} %get-tuple-element.63), channel_id=1, source_target_pairs={{0,2},{1,3},{2,0},{3,1},{4,6},{5,7},{6,4},{7,5},{8,10},{9,11},{10,... | collective-permute-start | bytes 178184 | tf_op jit(solution)/shard_map/ppermute | solution.py:643
  35.2 0.5 %collective-permute-start.11 = (bf16[232,128]{1,0:T(8,128)(2,1)S(1)}, bf16[232,128]{1,0:T(8,128)(2,1)S(1)}, u32[]{:S(2)}, u32[]{:S(2)}) collective-permute-start(bf16[232,128]{1,0:T(8,128)(2,1)S(1)} %get-tuple-element.58), channel_id=1, source_target_pairs={{0,1},{1,0},{2,3},{3,2},{4,5},{5,4},{6,7},{7,6},{8,9},{9,8},{10,11... | collective-permute-start | bytes 178184 | tf_op jit(solution)/shard_map/ppermute | solution.py:643
  35.7 0.3 turn.1.t_ref
  36.1 1.3 %fourth.1 = (f32[4,8,16,128]{3,2,1,0:T(8,128)S(1)}, bf16[128,128]{1,0:T(8,128)(2,1)S(1)}) custom-call(bf16[4,8,64,128]{3,2,1,0:T(8,128)(2,1)S(1)} %get-tuple-element.54.d_ref, bf16[3,64,576]{2,1,0:T(8,128)(2,1)S(1)} %turn.1.t_ref), custom_call_target="tpu_custom_call" | custom-call | flops 1 | tf_op jit(solution)/shard_map/fourth/pallas_call | solution.py:773
  37.4 0.9 %collective-permute-done.14.got_ref = bf16[232,128]{1,0:T(8,128)(2,1)S(1)} collective-permute-done((bf16[232,128]{1,0:T(8,128)(2,1)S(1)}, bf16[232,128]{1,0:T(8,128)(2,1)S(1)}, u32[]{:S(2)}, u32[]{:S(2)}) %collective-permute-start.14) | collective-permute-done | bytes 59424 | tf_op jit(solution)/shard_map/ppermute | solution.py:643
  38.3 0.1 step.7
  38.4 0.7 %collective-permute-start.15 = (bf16[360,128]{1,0:T(8,128)(2,1)S(1)}, bf16[360,128]{1,0:T(8,128)(2,1)S(1)}, u32[]{:S(2)}, u32[]{:S(2)}) collective-permute-start(bf16[360,128]{1,0:T(8,128)(2,1)S(1)} %get-tuple-element.66), channel_id=1, source_target_pairs={{0,16},{16,0},{1,17},{17,1},{2,18},{18,2},{3,19},{19,3},{4,20},{20... | collective-permute-start | bytes 276488 | tf_op jit(solution)/shard_map/ppermute | solution.py:643
  39.0 0.4 collective-permute-done.11.got_ref
  39.5 0.1 step.5
  39.5 2.6 %collective-permute-start.12 = (bf16[232,128]{1,0:T(8,128)(2,1)S(1)}, bf16[232,128]{1,0:T(8,128)(2,1)S(1)}, u32[]{:S(2)}, u32[]{:S(2)}) collective-permute-start(bf16[232,128]{1,0:T(8,128)(2,1)S(1)} %get-tuple-element.60), channel_id=1, source_target_pairs={{0,2},{1,3},{2,0},{3,1},{4,6},{5,7},{6,4},{7,5},{8,10},{9,11},{10,... | collective-permute-start | bytes 178184 | tf_op jit(solution)/shard_map/ppermute | solution.py:643
  42.1 2.5 %collective-permute-done.12.got1_ref = bf16[232,128]{1,0:T(8,128)(2,1)S(1)} collective-permute-done((bf16[232,128]{1,0:T(8,128)(2,1)S(1)}, bf16[232,128]{1,0:T(8,128)(2,1)S(1)}, u32[]{:S(2)}, u32[]{:S(2)}) %collective-permute-start.12) | collective-permute-done | bytes 59424 | tf_op jit(solution)/shard_map/ppermute | solution.py:643
  44.7 1.0 %close.1 = (f32[27,16,64]{2,1,0:T(8,128)}, f32[1,16]{1,0:T(1,128)}, f32[27,16,64]{2,1,0:T(8,128)}, f32[1,16]{1,0:T(1,128)}, bf16[16,4,8,128]{3,2,1,0:T(8,128)(2,1)}) custom-call(f32[4,8,16,128]{3,2,1,0:T(8,128)S(1)} %get-tuple-element.55.r_hbm, f32[232,128]{1,0:T(8,128)S(1)} %get-tuple-element.59.a1_ref, ...), custom_call_target="tpu_custom_call" | custom-call | tf_op jit(solution)/shard_map/close/pallas_call | solution.py:795
  (15 shorter events, 0.1 us)
Async XLA Ops:
  1.8 4.6 %collective-permute-start = (bf16[6,8,16,128]{3,2,1,0:T(8,128)(2,1)S(1)}, bf16[6,8,16,128]{3,2,1,0:T(8,128)(2,1)S(1)}, u32[]{:S(2)}, u32[]{:S(2)}) collective-permute-start(bf16[6,8,16,128]{3,2,1,0:T(8,128)(2,1)S(1)} %get-tuple-element.39.refs_0_), channel_id=1, source_target_pairs={{0,4},{4,0},{8,12},{12,8},{1,5},{5,1},{9,13},{13,9},{2,6},{6,2},{1... | collective-permute-start | bytes 589832 | tf_op jit(solution)/shard_map/ppermute | solution.py:170
  2.3 8.1 %collective-permute-start.2 = (bf16[6,8,16,128]{3,2,1,0:T(8,128)(2,1)S(1)}, bf16[6,8,16,128]{3,2,1,0:T(8,128)(2,1)S(1)}, u32[]{:S(2)}, u32[]{:S(2)}) collective-permute-start(bf16[6,8,16,128]{3,2,1,0:T(8,128)(2,1)S(1)} %get-tuple-element.39.refs_0_), channel_id=1, source_target_pairs={{0,8},{4,12},{8,0},{12,4},{1,9},{5,13},{9,1},{13,5},{2,10},{6,14},... | collective-permute-start | bytes 589832 | tf_op jit(solution)/shard_map/ppermute | solution.py:170
  4.9 5.6 %collective-permute-start.1 = (bf16[4,8,16,128]{3,2,1,0:T(8,128)(2,1)S(1)}, bf16[4,8,16,128]{3,2,1,0:T(8,128)(2,1)S(1)}, u32[]{:S(2)}, u32[]{:S(2)}) collective-permute-start(bf16[4,8,16,128]{3,2,1,0:T(8,128)(2,1)S(1)} %get-tuple-element.41), channel_id=1, source_target_pairs={{0,16},{16,0},{1,17},{17,1},{2,18},{18,2},{3,19},{19,3},{4,20},{20... | collective-permute-start | bytes 393224 | tf_op jit(solution)/shard_map/ppermute | solution.py:174
  10.4 2.0 %collective-permute-start.3 = (bf16[6,8,16,128]{3,2,1,0:T(8,128)(2,1)S(1)}, bf16[6,8,16,128]{3,2,1,0:T(8,128)(2,1)S(1)}, u32[]{:S(2)}, u32[]{:S(2)}) collective-permute-start(bf16[6,8,16,128]{3,2,1,0:T(8,128)(2,1)S(1)} %collective-permute-done.2.refs_2_), channel_id=1, source_target_pairs={{0,4},{4,0},{8,12},{12,8},{1,5},{5,1},{9,13},{13,9},{2,6},{6,2},{1... | collective-permute-start | bytes 589832 | tf_op jit(solution)/shard_map/ppermute | solution.py:170
  10.4 6.4 %collective-permute-start.7 = (bf16[4,8,16,128]{3,2,1,0:T(8,128)(2,1)S(1)}, bf16[4,8,16,128]{3,2,1,0:T(8,128)(2,1)S(1)}, u32[]{:S(2)}, u32[]{:S(2)}) collective-permute-start(bf16[4,8,16,128]{3,2,1,0:T(8,128)(2,1)S(1)} %collective-permute-done.1.refs_4_), channel_id=1, source_target_pairs={{0,8},{4,12},{8,0},{12,4},{1,9},{5,13},{9,1},{13,5},{2,10},{6,14},... | collective-permute-start | bytes 393224 | tf_op jit(solution)/shard_map/ppermute | solution.py:170
  12.1 8.4 %collective-permute-start.5 = (bf16[6,8,16,128]{3,2,1,0:T(8,128)(2,1)S(1)}, bf16[6,8,16,128]{3,2,1,0:T(8,128)(2,1)S(1)}, u32[]{:S(2)}, u32[]{:S(2)}) collective-permute-start(bf16[6,8,16,128]{3,2,1,0:T(8,128)(2,1)S(1)} %pack2.1.refs_0_), channel_id=1, source_target_pairs={{0,8},{4,12},{8,0},{12,4},{1,9},{5,13},{9,1},{13,5},{2,10},{6,14},... | collective-permute-start | bytes 589832 | tf_op jit(solution)/shard_map/ppermute | solution.py:170
  12.5 4.9 %collective-permute-start.6 = (bf16[4,8,16,128]{3,2,1,0:T(8,128)(2,1)S(1)}, bf16[4,8,16,128]{3,2,1,0:T(8,128)(2,1)S(1)}, u32[]{:S(2)}, u32[]{:S(2)}) collective-permute-start(bf16[4,8,16,128]{3,2,1,0:T(8,128)(2,1)S(1)} %collective-permute-done.1.refs_4_), channel_id=1, source_target_pairs={{0,4},{4,0},{8,12},{12,8},{1,5},{5,1},{9,13},{13,9},{2,6},{6,2},{1... | collective-permute-start | bytes 393224 | tf_op jit(solution)/shard_map/ppermute | solution.py:170
  16.8 1.3 %collective-permute-start.8 = (bf16[4,8,16,128]{3,2,1,0:T(8,128)(2,1)S(1)}, bf16[4,8,16,128]{3,2,1,0:T(8,128)(2,1)S(1)}, u32[]{:S(2)}, u32[]{:S(2)}) collective-permute-start(bf16[4,8,16,128]{3,2,1,0:T(8,128)(2,1)S(1)} %collective-permute-done.7.refs_6_), channel_id=1, source_target_pairs={{0,4},{4,0},{8,12},{12,8},{1,5},{5,1},{9,13},{13,9},{2,6},{6,2},{1... | collective-permute-start | bytes 393224 | tf_op jit(solution)/shard_map/ppermute | solution.py:170
  16.8 3.8 %collective-permute-start.4 = (bf16[6,8,16,128]{3,2,1,0:T(8,128)(2,1)S(1)}, bf16[6,8,16,128]{3,2,1,0:T(8,128)(2,1)S(1)}, u32[]{:S(2)}, u32[]{:S(2)}) collective-permute-start(bf16[6,8,16,128]{3,2,1,0:T(8,128)(2,1)S(1)} %pack2.1.refs_0_), channel_id=1, source_target_pairs={{0,4},{4,0},{8,12},{12,8},{1,5},{5,1},{9,13},{13,9},{2,6},{6,2},{1... | collective-permute-start | bytes 589832 | tf_op jit(solution)/shard_map/ppermute | solution.py:170
  20.6 1.4 %collective-permute-start.9 = (bf16[6,8,16,128]{3,2,1,0:T(8,128)(2,1)S(1)}, bf16[6,8,16,128]{3,2,1,0:T(8,128)(2,1)S(1)}, u32[]{:S(2)}, u32[]{:S(2)}) collective-permute-start(bf16[6,8,16,128]{3,2,1,0:T(8,128)(2,1)S(1)} %collective-permute-done.5.refs_2_), channel_id=1, source_target_pairs={{0,4},{4,0},{8,12},{12,8},{1,5},{5,1},{9,13},{13,9},{2,6},{6,2},{1... | collective-permute-start | bytes 589832 | tf_op jit(solution)/shard_map/ppermute | solution.py:170
  26.0 6.5 %collective-permute-start.13 = (bf16[232,128]{1,0:T(8,128)(2,1)S(1)}, bf16[232,128]{1,0:T(8,128)(2,1)S(1)}, u32[]{:S(2)}, u32[]{:S(2)}) collective-permute-start(bf16[232,128]{1,0:T(8,128)(2,1)S(1)} %wire.3), channel_id=1, source_target_pairs={{0,1},{1,0},{2,3},{3,2},{4,5},{5,4},{6,7},{7,6},{8,9},{9,8},{10,11... | collective-permute-start | bytes 178184 | tf_op jit(solution)/shard_map/ppermute | solution.py:643
  30.9 4.3 %collective-permute-start.10 = (bf16[232,128]{1,0:T(8,128)(2,1)S(1)}, bf16[232,128]{1,0:T(8,128)(2,1)S(1)}, u32[]{:S(2)}, u32[]{:S(2)}) collective-permute-start(bf16[232,128]{1,0:T(8,128)(2,1)S(1)} %wire.2), channel_id=1, source_target_pairs={{0,16},{16,0},{1,17},{17,1},{2,18},{18,2},{3,19},{19,3},{4,20},{20... | collective-permute-start | bytes 178184 | tf_op jit(solution)/shard_map/ppermute | solution.py:643
  32.6 5.7 %collective-permute-start.14 = (bf16[232,128]{1,0:T(8,128)(2,1)S(1)}, bf16[232,128]{1,0:T(8,128)(2,1)S(1)}, u32[]{:S(2)}, u32[]{:S(2)}) collective-permute-start(bf16[232,128]{1,0:T(8,128)(2,1)S(1)} %get-tuple-element.63), channel_id=1, source_target_pairs={{0,2},{1,3},{2,0},{3,1},{4,6},{5,7},{6,4},{7,5},{8,10},{9,11},{10,... | collective-permute-start | bytes 178184 | tf_op jit(solution)/shard_map/ppermute | solution.py:643
  35.2 4.2 %collective-permute-start.11 = (bf16[232,128]{1,0:T(8,128)(2,1)S(1)}, bf16[232,128]{1,0:T(8,128)(2,1)S(1)}, u32[]{:S(2)}, u32[]{:S(2)}) collective-permute-start(bf16[232,128]{1,0:T(8,128)(2,1)S(1)} %get-tuple-element.58), channel_id=1, source_target_pairs={{0,1},{1,0},{2,3},{3,2},{4,5},{5,4},{6,7},{7,6},{8,9},{9,8},{10,11... | collective-permute-start | bytes 178184 | tf_op jit(solution)/shard_map/ppermute | solution.py:643
  38.4 6.3 %collective-permute-start.15 = (bf16[360,128]{1,0:T(8,128)(2,1)S(1)}, bf16[360,128]{1,0:T(8,128)(2,1)S(1)}, u32[]{:S(2)}, u32[]{:S(2)}) collective-permute-start(bf16[360,128]{1,0:T(8,128)(2,1)S(1)} %get-tuple-element.66), channel_id=1, source_target_pairs={{0,16},{16,0},{1,17},{17,1},{2,18},{18,2},{3,19},{19,3},{4,20},{20... | collective-permute-start | bytes 276488 | tf_op jit(solution)/shard_map/ppermute | solution.py:643
  39.5 5.1 %collective-permute-start.12 = (bf16[232,128]{1,0:T(8,128)(2,1)S(1)}, bf16[232,128]{1,0:T(8,128)(2,1)S(1)}, u32[]{:S(2)}, u32[]{:S(2)}) collective-permute-start(bf16[232,128]{1,0:T(8,128)(2,1)S(1)} %get-tuple-element.60), channel_id=1, source_target_pairs={{0,2},{1,3},{2,0},{3,1},{4,6},{5,7},{6,4},{7,5},{8,10},{9,11},{10,... | collective-permute-start | bytes 178184 | tf_op jit(solution)/shard_map/ppermute | solution.py:643

commit v4 on v3

--- a/solution.py
+++ b/solution.py
@@ -200,9 +200,9 @@
     xc = flip_perm(x, 1)
     yc = flip_perm(y, 1)
     x2 = flip_perm(second, 2)
-    early = early_layers([(v, 0, n, "own", 0, k) for k, v in enumerate([packed, c, x, xc])])
-    dc = flip_perm(after(d, early[0]), 1)
-    c2 = flip_perm(after(second, early[0]), 1)
+    c2 = flip_perm(second, 1)
+    early, ahead = early_layers([(v, 0, n, "own", 0, k) for k, v in enumerate([packed, c, x, xc])], (second, c2))
+    dc = flip_perm(after(d, ahead[0]), 1)
     own, other, own2 = [packed, c, x, xc], [y, yc, d, dc], [second, c2, x2, x2]
     return (
         [(v, 0, n, "own", 0, k) for k, v in enumerate(own)],
@@ -210,6 +210,7 @@
         [(v, 0, n, "own", 0, k) for k, v in enumerate(own2)],
         [(v, NEAR, 1, "halo", 0, k) for k, v in enumerate(other)],
         early,
+        ahead,
     )
 
 
@@ -234,7 +235,7 @@
             other.append((down(mine[:NEAR]), 0, NEAR, "high", 0, flip))
             halo.append((up(mine2[n - 1 : n]), 0, 1, "low", 0, flip))
             halo.append((down(mine2[:1]), 0, 1, "high", 0, flip))
-    return own, other, own2, halo, ()
+    return own, other, own2, halo, (), ()
 
 
 def field_place(plan, place, k):
@@ -252,12 +253,13 @@
     return {"low": 0, "own": 1, "high": plan.layers + 1}[place]
 
 
-def load_weight(plan, refs, dst, sem, start):
-    for flip, ref in enumerate(refs):
+def load_weight(plan, refs, dst, sem, start, flips=None):
+    for n, ref in enumerate(refs):
+        flip = flips[n] if flips else n
         copy = pltpu.make_async_copy(
             ref.at[pl.ds(ref.shape[0] - dst.shape[0], dst.shape[0])],
             dst.at[:, :, pl.ds(plan.chan_at(flip), plan.group), :],
-            sem.at[flip],
+            sem.at[n],
         )
         copy.start() if start else copy.wait()
 
@@ -295,21 +297,21 @@
     zero_layer(ref, ref.shape[0] - 1)
 
 
-def slot(w_ref, n):
-    return w_ref[n // w_ref.shape[1], n % w_ref.shape[1]]
-
-
-def weight_matrix(w_ref, chan):
+def slot(w_ref, n, rows=slice(None)):
+    return w_ref[n // w_ref.shape[1], n % w_ref.shape[1], rows, :]
+
+
+def weight_matrix(w_ref, chan, rows=slice(None)):
     cols = []
     for pair in range(5):
-        block = jnp.concatenate([slot(w_ref, 3 * pair + kz) for kz in range(3)], axis=0)
+        block = jnp.concatenate([slot(w_ref, 3 * pair + kz, rows) for kz in range(3)], axis=0)
         cols.append(block if pair < 4 else block[:, :chan])
     return jnp.concatenate(cols, axis=1)
 
 
-def bias_column(w_ref):
-    rows = slot(w_ref, 15).astype(F32)
-    return rows[:, 0:1] + rows[:, 1:2] + rows[:, 2:3]
+def bias_column(w_ref, rows=slice(None)):
+    terms = slot(w_ref, 15, rows).astype(F32)
+    return terms[:, 0:1] + terms[:, 1:2] + terms[:, 2:3]
 
 
 def taps(field_ref, x, y):
@@ -416,38 +418,62 @@
         copy.wait()
 
 
-def grads(plan, get, f_ref, sh_ref, acc_ref, g_ref):
+def grad_sums(plan, count, get, f_ref, base, sh_ref):
     group, nz, ny, chan = plan.group, plan.nz, plan.ny, plan.chan
-    rows = pl.ds(plan.chan_at(0), group)
-    own = plan.own()
     zero = jnp.zeros((3 * group, nz), BF)
-
-    def shift(t, total):
+    total = jnp.zeros((group, nz), F32)
+    sums = jnp.zeros((9 * group, 3 * chan), F32)
+    for t in range(count):
         sh_ref[t, 0] = zero
         sh_ref[t, ny + 1] = zero
         for y in range(ny):
-            value = get(t, y, rows).astype(F32)
+            value = get(t, y).astype(F32)
             total = total + value
             sh_ref[t, y + 1] = jnp.concatenate([z_shift(value, -1), value, z_shift(value, 1)], axis=0).astype(BF)
-        return total
-
-    total = lax.fori_loop(0, plan.layers, shift, jnp.zeros((group, nz), F32), unroll=True)
-    total_w = jnp.zeros(acc_ref.shape, F32)
-    for t in range(plan.layers):
-        x = own + t
+    for t in range(count):
         left = jnp.concatenate(
             [jnp.concatenate([sh_ref[t, y + 2 - ky] for y in range(ny)], axis=1) for ky in range(3)], axis=0
         )
         right = jnp.concatenate(
-            [jnp.concatenate([f_ref[x + kx, y + 1] for y in range(ny)], axis=1) for kx in range(3)], axis=0
+            [jnp.concatenate([f_ref[base + t + kx, y + 1] for y in range(ny)], axis=1) for kx in range(3)], axis=0
         )
-        total_w += lax.dot_general(left, right, (((1,), (1,)), ((), ())), preferred_element_type=F32)
-    acc_ref[...] = total_w
+        sums += lax.dot_general(left, right, (((1,), (1,)), ((), ())), preferred_element_type=F32)
+    return sums, total
+
+
+def pack_grads(plan, sums, total, acc_ref, g_ref):
+    group, chan = plan.group, plan.chan
+    acc_ref[...] = sums
     n = 9 * group
     g_ref[0:n] = acc_ref[:, 0 : 2 * chan]
     last = acc_ref[:, 2 * chan :]
     g_ref[n : n + n // 2] = jnp.concatenate([last[: n // 2], last[n // 2 :]], axis=1)
     g_ref[n + n // 2 :] = jnp.broadcast_to(jnp.sum(total, axis=1, keepdims=True), (group, 2 * chan))
+
+
+def grads(plan, get, f_ref, sh_ref, acc_ref, g_ref):
+    rows = pl.ds(plan.chan_at(0), plan.group)
+    sums, total = grad_sums(plan, plan.layers, lambda t, y: get(t, y, rows), f_ref, plan.own(), sh_ref)
+    pack_grads(plan, sums, total, acc_ref, g_ref)
+
+
+def second_rows(plan, rows, h_ref, u_ref, w_ref, put, first, count, layer):
+    matrix = weight_matrix(w_ref, plan.chan, rows)
+    bias = bias_column(w_ref, rows)
+    for n in range(count):
+
+        def each(y, value, t=first + n, x=layer + n):
+            pre = value + bias
+            delta = (u_ref[t, y, rows, :].astype(F32) * slope_of(pre)).astype(BF)
+            put(t, x, y, pre, delta)
+
+        conv_rows(matrix, h_ref, layer + n, each)
+
+
+def put_output(plan, p_ref, rows, o_ref):
+    first = plan.own() - plan.start(1)
+    for t in range(plan.layers):
+        o_ref[:, t] = jnp.transpose(smooth(p_ref[first + t, :, rows, :]), (1, 0, 2)).astype(BF)
 
 
 def second_kernel(plan, places, *refs):
@@ -461,28 +487,106 @@
     load_weight(plan, weights, w_ref, wsem, False)
     turn(w_ref, t_ref, plan.chan)
     load_pieces(plan, pieces, places, u_ref, sem, False, halo=True)
-    start = plan.start(1)
-    m_ref = weight_matrix(w_ref, plan.chan)
-    bias = bias_column(w_ref)
-
-    def body(t, carry):
-        x = start + t
-
-        def each(y, value):
-            pre = value + bias
-            p_ref[t, y] = pre
-            d_ref[x + 1, y + 1] = (u_ref[t, y].astype(F32) * slope_of(pre)).astype(BF)
-
-        conv_rows(m_ref, h_ref, x, each)
-        return carry
-
-    lax.fori_loop(0, plan.count(1), body, 0, unroll=True)
-    rows = pl.ds(plan.chan_at(0), plan.group)
+
+    def put(t, x, y, pre, delta):
+        p_ref[t, y] = pre
+        d_ref[x + 1, y + 1] = delta
+
+    second_rows(plan, pl.ds(0, plan.chan), h_ref, u_ref, w_ref, put, 0, plan.count(1), plan.start(1))
+    put_output(plan, p_ref, pl.ds(plan.chan_at(0), plan.group), o_ref)
     own = plan.own()
-    first = own - start
-    for t in range(plan.layers):
-        o_ref[:, t] = jnp.transpose(smooth(p_ref[first + t, :, rows, :]), (1, 0, 2)).astype(BF)
     grads(plan, lambda t, y, rows: d_ref[own + t + 1, y + 1, rows, :], h_ref, sh_ref, acc_ref, g_ref)
+
+
+def chip_rows(plan, other):
+    half = plan.chan // 2
+    return pl.ds(pl.multiple_of(((lax.axis_index("filt") >> 1) ^ other) * half, half), half)
+
+
+def own_rows(plan):
+    return pl.ds(pl.multiple_of((lax.axis_index("filt") & 1) * plan.group, plan.group), plan.group)
+
+
+def ahead_kernel(plan, eh_hbm, own_hbm, chip_hbm, d_ref, o_ref, a_ref, b_ref, h_ref, u_ref, w_ref, p_ref, sh_ref, sem, wsem):
+    s = lax.axis_index("space")
+    count = plan.layers - 2
+    load_weight(plan, (own_hbm, chip_hbm), w_ref, wsem, True, (0, 1))
+    copies = [
+        pltpu.make_async_copy(eh_hbm, h_ref.at[pl.ds(1 - s, count + 1), pl.ds(1, plan.ny)], sem.at[2])
+    ]
+    for flip, ref in enumerate((own_hbm, chip_hbm)):
+        target = u_ref.at[:, :, pl.ds(plan.chan_at(flip), plan.group), :]
+        copies.append(pltpu.make_async_copy(ref.at[pl.ds(2 * s, count)], target, sem.at[flip]))
+    for copy in copies:
+        copy.start()
+    zero_rows(h_ref)
+    zero_layer(h_ref, s * (count + 1))
+    load_weight(plan, (own_hbm, chip_hbm), w_ref, wsem, False, (0, 1))
+    for copy in copies:
+        copy.wait()
+
+    def put(t, x, y, pre, delta):
+        p_ref[t, y] = pre
+        d_ref[t, y] = delta
+
+    second_rows(plan, chip_rows(plan, 0), h_ref, u_ref, w_ref, put, 0, count, 0)
+    mine = own_rows(plan)
+    for t in range(count):
+        o_ref[:, t] = jnp.transpose(smooth(p_ref[t, :, mine, :]), (1, 0, 2)).astype(BF)
+    a_ref[...], b_ref[...] = grad_sums(plan, count, lambda t, y: d_ref[t, y, mine, :], h_ref, 0, sh_ref)
+
+
+def near_kernel(plan, places, *refs):
+    n = len(places)
+    pieces, ahead, refs = refs[:n], refs[n], refs[n + 1 :]
+    h_ref, ao_ref, aa_ref, ab_ref, d_ref, o_ref, g_ref, u_ref, w_ref, p_ref, sh_ref, acc_ref, sem, wsem, asem = refs
+    s = lax.axis_index("space")
+    done = plan.layers - 2
+    left = plan.count(1) - done
+    load_weight(plan, pieces[:2], w_ref, wsem, True, (0, 1))
+    load_pieces(plan, pieces, places, u_ref, sem, True, halo=True)
+    copy = pltpu.make_async_copy(ahead, d_ref.at[pl.ds(s * left, done)], asem)
+    copy.start()
+    load_weight(plan, pieces[:2], w_ref, wsem, False, (0, 1))
+    load_pieces(plan, pieces, places, u_ref, sem, False, halo=True)
+
+    def put(t, x, y, pre, delta):
+        p_ref[t, y] = pre
+        d_ref[t, y] = delta
+
+    start, first, slab = plan.start(1), (1 - s) * done, (1 - s) * done
+    second_rows(plan, chip_rows(plan, 0), h_ref, u_ref, w_ref, put, first, left, start + first)
+    mine = own_rows(plan)
+    o_ref[:, pl.ds(2 * s, done)] = ao_ref[...]
+    at = plan.own() - start + slab
+    for t in range(2):
+        value = jnp.transpose(smooth(p_ref[at + t, :, mine, :]), (1, 0, 2)).astype(BF)
+        o_ref[:, pl.ds(slab + t, 1)] = value[:, None]
+    sums, total = grad_sums(plan, 2, lambda t, y: d_ref[at + t, y, mine, :], h_ref, plan.own() + slab, sh_ref)
+    pack_grads(plan, sums + aa_ref[...], total + ab_ref[...], acc_ref, g_ref)
+    copy.wait()
+
+
+def far_kernel(plan, places, *refs):
+    n = len(places)
+    pieces, weights, refs = refs[:n], refs[n : n + 4], refs[n + 4 :]
+    near_ref, h_ref, d_ref, t_ref, u_ref, w_ref, sem, wsem, nsem = refs
+    load_weight(plan, weights, w_ref, wsem, True)
+    load_pieces(plan, pieces, places, u_ref, sem, True, halo=True)
+    joined = d_ref.at[pl.ds(plan.start(1) + 1, plan.count(1)), pl.ds(1, plan.ny), chip_rows(plan, 0), :]
+    copy = pltpu.make_async_copy(near_ref, joined, nsem)
+    copy.start()
+    zero_edges(plan, d_ref)
+    load_weight(plan, weights, w_ref, wsem, False)
+    turn(w_ref, t_ref, plan.chan)
+    load_pieces(plan, pieces, places, u_ref, sem, False, halo=True)
+    rows = chip_rows(plan, 1)
+
+    def put(t, x, y, pre, delta):
+        d_ref[x + 1, y + 1, rows, :] = delta
+
+    second_rows(plan, rows, h_ref, u_ref, w_ref, put, 0, plan.count(1), plan.start(1))
+    copy.wait()
 
 
 def turn(w_ref, out, chan):
@@ -602,10 +706,11 @@
     w_ref[total.shape[0] :] = share_ref[...]
 
 
-def close_kernel(plan, rows, scale, r_hbm, a1_ref, got1_ref, a2_ref, got2_ref, *refs):
-    w1_ref, b1_ref, w2_ref, b2_ref, o_ref, r_ref, sem = refs
+def close_kernel(plan, rows, scale, r_hbm, a1_ref, got1_ref, a2_ref, got2_ref, out_ref, *refs):
+    w1_ref, b1_ref, w2_ref, b2_ref, o_ref, out2_ref, r_ref, sem = refs
     copy = pltpu.make_async_copy(r_hbm, r_ref, sem)
     copy.start()
+    out2_ref[...] = out_ref[...]
     last_kernel(rows, plan.group, scale, a1_ref, got1_ref, w1_ref, b1_ref)
     last_kernel(rows, plan.group, scale, a2_ref, got2_ref, w2_ref, b2_ref)
     copy.wait()
@@ -695,8 +800,10 @@
     grad_rows = 27 * group // 2 + group
     grad_scratch = [VM((layers, ny + 2, 3 * group, nz), BF), VM((9 * group, 3 * chan), F32)]
 
-    def early_layers(pieces):
-        return call(
+    half = lambda n: (n, ny, chan // 2, nz)
+
+    def early_layers(pieces, pieces2):
+        early = call(
             functools.partial(early_kernel, plan, [p[1:] for p in pieces]),
             (shape((layers - 1, ny, chan, nz), BF), shape((layers - 1, ny, chan, nz), F32)),
             len(pieces),
@@ -705,9 +812,33 @@
             flops=1,
             name="early",
         )(*(p[0] for p in pieces))
+        some = layers - 2
+        ahead, ahead_output, ahead_sums, ahead_total = call(
+            functools.partial(ahead_kernel, plan),
+            (
+                shape(half(some), BF),
+                shape((group, some, ny, nz), BF),
+                shape((9 * group, 3 * chan), F32),
+                shape((group, nz), F32),
+            ),
+            3,
+            0,
+            [
+                VM((layers, ny + 2, chan, nz), BF),
+                VM((some, ny, chan, nz), BF),
+                slots,
+                VM(half(some), F32),
+                VM((some, ny + 2, 3 * group, nz), BF),
+                dma((3,)),
+                dma((2,)),
+            ],
+            flops=1,
+            name="ahead",
+        )(early[0], *pieces2)
+        return early, (ahead, ahead_output, ahead_sums, ahead_total)
 
     gather = gather_quick if plan.quick else gather_plain
-    v_own, v_other, u_own, u_other, early = gather(
+    v_own, v_other, u_own, u_other, early, ahead = gather(
         volume[0], weight1, bias1, upstream[0], weight2, bias2, plan, early_layers
     )
     v_places = [p[1:] for p in v_own + v_other]
@@ -737,27 +868,59 @@
 
     if plan.quick:
         u_all[3] = flip_perm(after(u_all[2], hidden), 1)
-    delta2, output, part2, turned2 = call(
-        functools.partial(second_kernel, plan, u_places),
-        (
-            shape(padded, BF),
-            shape((group, layers, ny, nz), BF),
-            shape((grad_rows, 2 * chan), F32),
-            shape((3, chan, 9 * chan), BF),
-        ),
-        len(u_all),
-        1,
-        [
-            VM((plan.count(1), ny, chan, nz), BF),
-            slots,
-            VM((plan.count(1), ny, chan, nz), F32),
-            *grad_scratch,
-            dma((len(u_all),)),
-            dma((groups,)),
-        ],
-        flops=1,
-        name="second",
-    )(*u_all, hidden)
+        here, there = (0, 1, 4, 5), (2, 3, 6, 7)
+        near2, output, part2 = call(
+            functools.partial(near_kernel, plan, [u_places[k] for k in here]),
+            (
+                shape(half(plan.count(1)), BF),
+                shape((group, layers, ny, nz), BF),
+                shape((grad_rows, 2 * chan), F32),
+            ),
+            5,
+            4,
+            [
+                VM((plan.count(1), ny, chan, nz), BF),
+                slots,
+                VM(half(plan.count(1)), F32),
+                *grad_scratch,
+                dma((4,)),
+                dma((2,)),
+                dma,
+            ],
+            flops=1,
+            name="near",
+        )(*(u_all[k] for k in here), ahead[0], hidden, *ahead[1:])
+        delta2, turned2 = call(
+            functools.partial(far_kernel, plan, [u_places[k] for k in there]),
+            (shape(padded, BF), shape((3, chan, 9 * chan), BF)),
+            9,
+            1,
+            [VM((plan.count(1), ny, chan, nz), BF), slots, dma((4,)), dma((4,)), dma],
+            flops=1,
+            name="far",
+        )(*(u_all[k] for k in there), *u_all[:4], near2, hidden)
+    else:
+        delta2, output, part2, turned2 = call(
+            functools.partial(second_kernel, plan, u_places),
+            (
+                shape(padded, BF),
+                shape((group, layers, ny, nz), BF),
+                shape((grad_rows, 2 * chan), F32),
+                shape((3, chan, 9 * chan), BF),
+            ),
+            len(u_all),
+            1,
+            [
+                VM((plan.count(1), ny, chan, nz), BF),
+                slots,
+                VM((plan.count(1), ny, chan, nz), F32),
+                *grad_scratch,
+                dma((len(u_all),)),
+                dma((groups,)),
+            ],
+            flops=1,
+            name="second",
+        )(*u_all, hidden)
 
     delta1, part1 = call(
         functools.partial(third_kernel, plan, v_places),
@@ -792,14 +955,14 @@
     volume_shape = shape((group, layers, ny, nz), BF)
     finish_scratch = [VM((layers, ny, group, nz), F32), dma]
     if plan.pair:
-        w1, b1, w2, b2, volume_grad = call(
+        w1, b1, w2, b2, volume_grad, output = call(
             functools.partial(close_kernel, plan, part2.shape[0] - group, scale),
-            (*grad_shapes(plan), *grad_shapes(plan), volume_shape),
+            (*grad_shapes(plan), *grad_shapes(plan), volume_shape, volume_shape),
             1,
-            4,
+            5,
             finish_scratch,
             name="close",
-        )(own_grad, part1, got1, part2, got2)
+        )(own_grad, part1, got1, part2, got2, output)
         grad1, bias_grad1 = as_grads(w1, b1, plan)
         grad2, bias_grad2 = as_grads(w2, b2, plan)
     else:

time: 45.8 us -> 44.5 us (0.972)
  waiting for transfers between devices: 12.5 us -> 9.88 us
  Pallas kernels: 15.5 us -> 16.8 us
    ppermute x9, waiting for transfers between devices: 5.71 us -> 2.92 us  [flip_perm(): return lax.ppermute(value, 'filt', [(i, i ^ flip) for i in range(n)])]
    pallas_call x1 -> x3, Pallas kernels: 3.95 us -> 5.22 us  [the longest x1 1.95 us: local(): call(functools.partial(far_kernel, plan, [u_places[k] for k in there]), (...]
  transfers between devices with their start and end apart: 16 -> 16, of which waited for: 8 -> 8; matrix products, arithmetic and copies ran while one was open for 0% -> 0% of each run, Pallas kernels for 21% -> 33%
where the time goes in v4:
time: 44.5 us; the launch traced here: 44.3 us
  starting transfers between devices  16.9 us (38%)
  Pallas kernels  16.8 us (38%)
  waiting for transfers between devices  9.88 us (22%)
  between operations  0.75 us (2%)
    ppermute x6, starting transfers between devices, exchange(): lax.ppermute(wire, axis, [(i, i ^ bit) for i in range(lax.axis_size(axis))])  9.57 us
    ppermute x9, starting transfers between devices, flip_perm(): return lax.ppermute(value, 'filt', [(i, i ^ flip) for i in range(n)])  5.76 us
    ppermute x6, waiting for transfers between devices, exchange(): lax.ppermute(wire, axis, [(i, i ^ bit) for i in range(lax.axis_size(axis))])  4.02 us
    pallas_call x1, Pallas kernels, local(): call(functools.partial(third_kernel, plan, v_places), (shape((layers, ny,...  3.08 us
    ppermute x1, waiting for transfers between devices, over(): return lax.ppermute(value, 'space', [(0, 1), (1, 0)])  2.94 us
    ppermute x9, waiting for transfers between devices, flip_perm(): return lax.ppermute(value, 'filt', [(i, i ^ flip) for i in range(n)])  2.92 us
    pallas_call x2, Pallas kernels, pack(): pl.pallas_call(functools.partial(pack_kernel, edge), out_shape=tuple(outs...  2.2 us
    pallas_call x1, Pallas kernels, local(): call(functools.partial(far_kernel, plan, [u_places[k] for k in there]), (...  1.95 us
  transfers between devices with their start and end apart: 16, of which 8 were waited for; matrix products, arithmetic and copies ran while one was open for 0% of the time, Pallas kernels for 33%

profile of v4, /device:TPU:0, one launch (start us, length us, event | category | flops | bytes accessed | tf_op | source)
XLA Modules:
  0.0 44.3 jit_solution(5601412088302645819)
XLA Ops:
  0.6 1.1 %pack1.1 = (bf16[6,8,16,128]{3,2,1,0:T(8,128)(2,1)S(1)}, bf16[4,8,16,128]{3,2,1,0:T(8,128)(2,1)S(1)}) custom-call(bf16[16,4,8,128]{3,2,1,0:T(8,128)(2,1)} %bitcast.22, bf16[27,16,64]{2,1,0:T(8,128)(2,1)} %bitcast.23, f32[1,16]{1,0:T(1,128)} %bitcast.25, bf16[16,4,8,128]{3,2,1,0:T(8,128)(2,1)} %bitcast.20), custom_call_target="tpu_custom_call" | custom-call | bytes 262144 | tf_op jit(solution)/shard_map/pack1/pallas_call | solution.py:122
  1.8 0.6 %collective-permute-start = (bf16[6,8,16,128]{3,2,1,0:T(8,128)(2,1)S(1)}, bf16[6,8,16,128]{3,2,1,0:T(8,128)(2,1)S(1)}, u32[]{:S(2)}, u32[]{:S(2)}) collective-permute-start(bf16[6,8,16,128]{3,2,1,0:T(8,128)(2,1)S(1)} %get-tuple-element.44.refs_0_), channel_id=1, source_target_pairs={{0,4},{4,0},{8,12},{12,8},{1,5},{5,1},{9,13},{13,9},{2,6},{6,2},{1... | collective-permute-start | bytes 589832 | tf_op jit(solution)/shard_map/ppermute | solution.py:170
  2.3 2.6 %collective-permute-start.2 = (bf16[6,8,16,128]{3,2,1,0:T(8,128)(2,1)S(1)}, bf16[6,8,16,128]{3,2,1,0:T(8,128)(2,1)S(1)}, u32[]{:S(2)}, u32[]{:S(2)}) collective-permute-start(bf16[6,8,16,128]{3,2,1,0:T(8,128)(2,1)S(1)} %get-tuple-element.44.refs_0_), channel_id=1, source_target_pairs={{0,8},{4,12},{8,0},{12,4},{1,9},{5,13},{9,1},{13,5},{2,10},{6,14},... | collective-permute-start | bytes 589832 | tf_op jit(solution)/shard_map/ppermute | solution.py:170
  4.9 1.5 %collective-permute-start.1 = (bf16[4,8,16,128]{3,2,1,0:T(8,128)(2,1)S(1)}, bf16[4,8,16,128]{3,2,1,0:T(8,128)(2,1)S(1)}, u32[]{:S(2)}, u32[]{:S(2)}) collective-permute-start(bf16[4,8,16,128]{3,2,1,0:T(8,128)(2,1)S(1)} %get-tuple-element.45), channel_id=1, source_target_pairs={{0,16},{16,0},{1,17},{17,1},{2,18},{18,2},{3,19},{19,3},{4,20},{20... | collective-permute-start | bytes 393224 | tf_op jit(solution)/shard_map/ppermute | solution.py:174
  6.4 1.1 %pack2.1.own_hbm.refs_0_.refs_4_ = bf16[6,8,16,128]{3,2,1,0:T(8,128)(2,1)S(1)} custom-call(bf16[16,4,8,128]{3,2,1,0:T(8,128)(2,1)} %bitcast.21, bf16[27,16,64]{2,1,0:T(8,128)(2,1)} %bitcast.24, f32[1,16]{1,0:T(1,128)} %bitcast.26), custom_call_target="tpu_custom_call" | custom-call | bytes 262144 | tf_op jit(solution)/shard_map/pack2/pallas_call | solution.py:122
  7.5 2.9 %collective-permute-done.1.refs_4_.refs_2_ = bf16[4,8,16,128]{3,2,1,0:T(8,128)(2,1)S(1)} collective-permute-done((bf16[4,8,16,128]{3,2,1,0:T(8,128)(2,1)S(1)}, bf16[4,8,16,128]{3,2,1,0:T(8,128)(2,1)S(1)}, u32[]{:S(2)}, u32[]{:S(2)}) %collective-permute-start.1) | collective-permute-done | bytes 131104 | tf_op jit(solution)/shard_map/ppermute | solution.py:174
  10.4 0.5 %collective-permute-start.6 = (bf16[6,8,16,128]{3,2,1,0:T(8,128)(2,1)S(1)}, bf16[6,8,16,128]{3,2,1,0:T(8,128)(2,1)S(1)}, u32[]{:S(2)}, u32[]{:S(2)}) collective-permute-start(bf16[6,8,16,128]{3,2,1,0:T(8,128)(2,1)S(1)} %pack2.1.own_hbm.refs_0_.refs_4_), channel_id=1, source_target_pairs={{0,4},{4,0},{8,12},{12,8},{1,5},{5,1},{9,13},{13,9},{2,6},{6,2},{1... | collective-permute-start | bytes 589832 | tf_op jit(solution)/shard_map/ppermute | solution.py:170
  10.9 1.7 %collective-permute-start.5 = (bf16[4,8,16,128]{3,2,1,0:T(8,128)(2,1)S(1)}, bf16[4,8,16,128]{3,2,1,0:T(8,128)(2,1)S(1)}, u32[]{:S(2)}, u32[]{:S(2)}) collective-permute-start(bf16[4,8,16,128]{3,2,1,0:T(8,128)(2,1)S(1)} %collective-permute-done.1.refs_4_.refs_2_), channel_id=1, source_target_pairs={{0,8},{4,12},{8,0},{12,4},{1,9},{5,13},{9,1},{13,5},{2,10},{6,14},... | collective-permute-start | bytes 393224 | tf_op jit(solution)/shard_map/ppermute | solution.py:170
  12.6 0.3 collective-permute-start.8
  13.0 1.5 %early.1 = (bf16[3,8,64,128]{3,2,1,0:T(8,128)(2,1)S(1)}, f32[3,8,64,128]{3,2,1,0:T(8,128)S(1)}) custom-call(bf16[6,8,16,128]{3,2,1,0:T(8,128)(2,1)S(1)} %get-tuple-element.44.refs_0_, bf16[6,8,16,128]{3,2,1,0:T(8,128)(2,1)S(1)} %collective-permute-done.refs_1_, bf16[6,8,16,128]{3,2,1,0:T(8,128)(2,1)S(1)} %collective-permute-done.2.refs_2_, ...), custom_call_target="tpu_custom_call" | custom-call | flops 1 | tf_op jit(solution)/shard_map/early/pallas_call | solution.py:806
  14.5 1.3 %ahead.1 = (bf16[2,8,32,128]{3,2,1,0:T(8,128)(2,1)S(1)}, bf16[16,2,8,128]{3,2,1,0:T(8,128)(2,1)S(1)}, f32[144,192]{1,0:T(8,128)S(1)}, f32[16,128]{1,0:T(8,128)S(1)}) custom-call(bf16[3,8,64,128]{3,2,1,0:T(8,128)(2,1)S(1)} %get-tuple-element.49.eh_hbm.refs_8_, bf16[6,8,16,128]{3,2,1,0:T(8,128)(2,1)S(1)} %pack2.1.own_hbm.refs_0_.refs_4_, ...), custom_call_target="tpu_custom_call" | custom-call | flops 1 | tf_op jit(solution)/shard_map/ahead/pallas_call | solution.py:816
  15.9 1.5 %collective-permute-done.5.refs_6_.refs_2_ = bf16[4,8,16,128]{3,2,1,0:T(8,128)(2,1)S(1)} collective-permute-done((bf16[4,8,16,128]{3,2,1,0:T(8,128)(2,1)S(1)}, bf16[4,8,16,128]{3,2,1,0:T(8,128)(2,1)S(1)}, u32[]{:S(2)}, u32[]{:S(2)}) %collective-permute-start.5) | collective-permute-done | bytes 131104 | tf_op jit(solution)/shard_map/ppermute | solution.py:170
  17.3 1.3 %collective-permute-done.7.refs_7_.refs_3_ = bf16[4,8,16,128]{3,2,1,0:T(8,128)(2,1)S(1)} collective-permute-done((bf16[4,8,16,128]{3,2,1,0:T(8,128)(2,1)S(1)}, bf16[4,8,16,128]{3,2,1,0:T(8,128)(2,1)S(1)}, u32[]{:S(2)}, u32[]{:S(2)}) %collective-permute-start.7) | collective-permute-done | bytes 131104 | tf_op jit(solution)/shard_map/ppermute | solution.py:170
  18.7 1.8 %first.1 = (bf16[10,10,64,128]{3,2,1,0:T(8,128)(2,1)S(1)}, f32[6,8,64,128]{3,2,1,0:T(8,128)S(1)}) custom-call(bf16[6,8,16,128]{3,2,1,0:T(8,128)(2,1)S(1)} %get-tuple-element.44.refs_0_, bf16[6,8,16,128]{3,2,1,0:T(8,128)(2,1)S(1)} %collective-permute-done.refs_1_, bf16[6,8,16,128]{3,2,1,0:T(8,128)(2,1)S(1)} %collective-permute-done.2.refs_2_, ...), custom_call_target="tpu_custom_call" | custom-call | flops 1 | tf_op jit(solution)/shard_map/first/pallas_call | solution.py:859
  20.4 0.1 collective-permute-done.8.refs_0_.refs_6_
  20.6 0.1 collective-permute-start.9
  20.7 1.9 %near.1 = (bf16[5,8,32,128]{3,2,1,0:T(8,128)(2,1)S(1)}, bf16[16,4,8,128]{3,2,1,0:T(8,128)(2,1)S(1)}, f32[232,128]{1,0:T(8,128)S(1)}) custom-call(bf16[6,8,16,128]{3,2,1,0:T(8,128)(2,1)S(1)} %pack2.1.own_hbm.refs_0_.refs_4_, bf16[6,8,16,128]{3,2,1,0:T(8,128)(2,1)S(1)} %collective-permute-done.6.chip_hbm.refs_1_.refs_5_, ...), custom_call_target="tpu_custom_call" | custom-call | flops 1 | tf_op jit(solution)/shard_map/near/pallas_call | solution.py:872
  22.6 1.8 %collective-permute-start.13 = (bf16[232,128]{1,0:T(8,128)(2,1)S(1)}, bf16[232,128]{1,0:T(8,128)(2,1)S(1)}, u32[]{:S(2)}, u32[]{:S(2)}) collective-permute-start(bf16[232,128]{1,0:T(8,128)(2,1)S(1)} %wire.3), channel_id=1, source_target_pairs={{0,1},{1,0},{2,3},{3,2},{4,5},{5,4},{6,7},{7,6},{8,9},{9,8},{10,11... | collective-permute-start | bytes 178184 | tf_op jit(solution)/shard_map/ppermute | solution.py:748
  24.4 1.9 %far.1 = (bf16[10,10,64,128]{3,2,1,0:T(8,128)(2,1)S(1)}, bf16[3,64,576]{2,1,0:T(8,128)(2,1)S(1)}) custom-call(bf16[6,8,16,128]{3,2,1,0:T(8,128)(2,1)S(1)} %collective-permute-done.8.refs_0_.refs_6_, bf16[6,8,16,128]{3,2,1,0:T(8,128)(2,1)S(1)} %collective-permute-done.9.refs_1_.refs_7_, bf16[4,8,16,128]{3,2,1,0:T(8,128)(2,1)S(1)} %collective-permute-done.5.refs_6_.refs_2_, ...), custom_call_target="tpu_custom_call" | custom-call | flops 1 | tf_op jit(solution)/shard_map/far/pallas_call | solution.py:893
  26.4 3.1 %third.1 = (bf16[4,8,64,128]{3,2,1,0:T(8,128)(2,1)S(1)}, f32[232,128]{1,0:T(8,128)S(1)}) custom-call(bf16[6,8,16,128]{3,2,1,0:T(8,128)(2,1)S(1)} %get-tuple-element.44.refs_0_, bf16[6,8,16,128]{3,2,1,0:T(8,128)(2,1)S(1)} %collective-permute-done.refs_1_, bf16[6,8,16,128]{3,2,1,0:T(8,128)(2,1)S(1)} %collective-permute-done.2.refs_2_, ...), custom_call_target="tpu_custom_call" | custom-call | flops 1 | tf_op jit(solution)/shard_map/third/pallas_call | solution.py:925
  29.5 1.6 %collective-permute-start.10 = (bf16[232,128]{1,0:T(8,128)(2,1)S(1)}, bf16[232,128]{1,0:T(8,128)(2,1)S(1)}, u32[]{:S(2)}, u32[]{:S(2)}) collective-permute-start(bf16[232,128]{1,0:T(8,128)(2,1)S(1)} %wire.2), channel_id=1, source_target_pairs={{0,16},{16,0},{1,17},{17,1},{2,18},{18,2},{3,19},{19,3},{4,20},{20... | collective-permute-start | bytes 178184 | tf_op jit(solution)/shard_map/ppermute | solution.py:748
  31.2 2.6 %collective-permute-start.14 = (bf16[232,128]{1,0:T(8,128)(2,1)S(1)}, bf16[232,128]{1,0:T(8,128)(2,1)S(1)}, u32[]{:S(2)}, u32[]{:S(2)}) collective-permute-start(bf16[232,128]{1,0:T(8,128)(2,1)S(1)} %get-tuple-element.71), channel_id=1, source_target_pairs={{0,2},{1,3},{2,0},{3,1},{4,6},{5,7},{6,4},{7,5},{8,10},{9,11},{10,... | collective-permute-start | bytes 178184 | tf_op jit(solution)/shard_map/ppermute | solution.py:748
  33.9 0.4 collective-permute-start.11
  34.3 0.3 turn.1.t_ref
  34.7 1.3 %fourth.1 = (f32[4,8,16,128]{3,2,1,0:T(8,128)S(1)}, bf16[128,128]{1,0:T(8,128)(2,1)S(1)}) custom-call(bf16[4,8,64,128]{3,2,1,0:T(8,128)(2,1)S(1)} %get-tuple-element.62.d_ref, bf16[3,64,576]{2,1,0:T(8,128)(2,1)S(1)} %turn.1.t_ref), custom_call_target="tpu_custom_call" | custom-call | flops 1 | tf_op jit(solution)/shard_map/fourth/pallas_call | solution.py:936
  36.0 1.0 %collective-permute-done.14.got_ref = bf16[232,128]{1,0:T(8,128)(2,1)S(1)} collective-permute-done((bf16[232,128]{1,0:T(8,128)(2,1)S(1)}, bf16[232,128]{1,0:T(8,128)(2,1)S(1)}, u32[]{:S(2)}, u32[]{:S(2)}) %collective-permute-start.14) | collective-permute-done | bytes 59424 | tf_op jit(solution)/shard_map/ppermute | solution.py:748
  37.1 0.5 %collective-permute-start.15 = (bf16[360,128]{1,0:T(8,128)(2,1)S(1)}, bf16[360,128]{1,0:T(8,128)(2,1)S(1)}, u32[]{:S(2)}, u32[]{:S(2)}) collective-permute-start(bf16[360,128]{1,0:T(8,128)(2,1)S(1)} %get-tuple-element.74), channel_id=1, source_target_pairs={{0,16},{16,0},{1,17},{17,1},{2,18},{18,2},{3,19},{19,3},{4,20},{20... | collective-permute-start | bytes 276488 | tf_op jit(solution)/shard_map/ppermute | solution.py:748
  37.6 0.5 %collective-permute-done.11.got_ref = bf16[232,128]{1,0:T(8,128)(2,1)S(1)} collective-permute-done((bf16[232,128]{1,0:T(8,128)(2,1)S(1)}, bf16[232,128]{1,0:T(8,128)(2,1)S(1)}, u32[]{:S(2)}, u32[]{:S(2)}) %collective-permute-start.11) | collective-permute-done | bytes 59424 | tf_op jit(solution)/shard_map/ppermute | solution.py:748
  38.2 2.6 %collective-permute-start.12 = (bf16[232,128]{1,0:T(8,128)(2,1)S(1)}, bf16[232,128]{1,0:T(8,128)(2,1)S(1)}, u32[]{:S(2)}, u32[]{:S(2)}) collective-permute-start(bf16[232,128]{1,0:T(8,128)(2,1)S(1)} %get-tuple-element.68), channel_id=1, source_target_pairs={{0,2},{1,3},{2,0},{3,1},{4,6},{5,7},{6,4},{7,5},{8,10},{9,11},{10,... | collective-permute-start | bytes 178184 | tf_op jit(solution)/shard_map/ppermute | solution.py:748
  40.8 0.9 %collective-permute-done.15.got2_ref = bf16[360,128]{1,0:T(8,128)(2,1)S(1)} collective-permute-done((bf16[360,128]{1,0:T(8,128)(2,1)S(1)}, bf16[360,128]{1,0:T(8,128)(2,1)S(1)}, u32[]{:S(2)}, u32[]{:S(2)}) %collective-permute-start.15) | collective-permute-done | bytes 92192 | tf_op jit(solution)/shard_map/ppermute | solution.py:748
  41.7 1.6 %collective-permute-done.12.got1_ref = bf16[232,128]{1,0:T(8,128)(2,1)S(1)} collective-permute-done((bf16[232,128]{1,0:T(8,128)(2,1)S(1)}, bf16[232,128]{1,0:T(8,128)(2,1)S(1)}, u32[]{:S(2)}, u32[]{:S(2)}) %collective-permute-start.12) | collective-permute-done | bytes 59424 | tf_op jit(solution)/shard_map/ppermute | solution.py:748
  43.3 1.0 %close.1 = (f32[27,16,64]{2,1,0:T(8,128)}, f32[1,16]{1,0:T(1,128)}, f32[27,16,64]{2,1,0:T(8,128)}, f32[1,16]{1,0:T(1,128)}, bf16[16,4,8,128]{3,2,1,0:T(8,128)(2,1)}, /*index=5*/bf16[16,4,8,128]{3,2,1,0:T(8,128)(2,1)}) custom-call(f32[4,8,16,128]{3,2,1,0:T(8,128)S(1)} %get-tuple-element.63.r_hbm, f32[232,128]{1,0:T(8,128)S(1)} %get-tuple-element.67.a1_ref, ...), custom_call_target="tpu_custom_call" | custom-call | tf_op jit(solution)/shard_map/close/pallas_call | solution.py:958
  (17 shorter events, 0.4 us)
Async XLA Ops:
  1.8 4.6 %collective-permute-start = (bf16[6,8,16,128]{3,2,1,0:T(8,128)(2,1)S(1)}, bf16[6,8,16,128]{3,2,1,0:T(8,128)(2,1)S(1)}, u32[]{:S(2)}, u32[]{:S(2)}) collective-permute-start(bf16[6,8,16,128]{3,2,1,0:T(8,128)(2,1)S(1)} %get-tuple-element.44.refs_0_), channel_id=1, source_target_pairs={{0,4},{4,0},{8,12},{12,8},{1,5},{5,1},{9,13},{13,9},{2,6},{6,2},{1... | collective-permute-start | bytes 589832 | tf_op jit(solution)/shard_map/ppermute | solution.py:170
  2.3 8.1 %collective-permute-start.2 = (bf16[6,8,16,128]{3,2,1,0:T(8,128)(2,1)S(1)}, bf16[6,8,16,128]{3,2,1,0:T(8,128)(2,1)S(1)}, u32[]{:S(2)}, u32[]{:S(2)}) collective-permute-start(bf16[6,8,16,128]{3,2,1,0:T(8,128)(2,1)S(1)} %get-tuple-element.44.refs_0_), channel_id=1, source_target_pairs={{0,8},{4,12},{8,0},{12,4},{1,9},{5,13},{9,1},{13,5},{2,10},{6,14},... | collective-permute-start | bytes 589832 | tf_op jit(solution)/shard_map/ppermute | solution.py:170
  4.9 5.6 %collective-permute-start.1 = (bf16[4,8,16,128]{3,2,1,0:T(8,128)(2,1)S(1)}, bf16[4,8,16,128]{3,2,1,0:T(8,128)(2,1)S(1)}, u32[]{:S(2)}, u32[]{:S(2)}) collective-permute-start(bf16[4,8,16,128]{3,2,1,0:T(8,128)(2,1)S(1)} %get-tuple-element.45), channel_id=1, source_target_pairs={{0,16},{16,0},{1,17},{17,1},{2,18},{18,2},{3,19},{19,3},{4,20},{20... | collective-permute-start | bytes 393224 | tf_op jit(solution)/shard_map/ppermute | solution.py:174
  10.4 2.5 %collective-permute-start.3 = (bf16[6,8,16,128]{3,2,1,0:T(8,128)(2,1)S(1)}, bf16[6,8,16,128]{3,2,1,0:T(8,128)(2,1)S(1)}, u32[]{:S(2)}, u32[]{:S(2)}) collective-permute-start(bf16[6,8,16,128]{3,2,1,0:T(8,128)(2,1)S(1)} %collective-permute-done.2.refs_2_), channel_id=1, source_target_pairs={{0,4},{4,0},{8,12},{12,8},{1,5},{5,1},{9,13},{13,9},{2,6},{6,2},{1... | collective-permute-start | bytes 589832 | tf_op jit(solution)/shard_map/ppermute | solution.py:170
  10.4 4.1 %collective-permute-start.6 = (bf16[6,8,16,128]{3,2,1,0:T(8,128)(2,1)S(1)}, bf16[6,8,16,128]{3,2,1,0:T(8,128)(2,1)S(1)}, u32[]{:S(2)}, u32[]{:S(2)}) collective-permute-start(bf16[6,8,16,128]{3,2,1,0:T(8,128)(2,1)S(1)} %pack2.1.own_hbm.refs_0_.refs_4_), channel_id=1, source_target_pairs={{0,4},{4,0},{8,12},{12,8},{1,5},{5,1},{9,13},{13,9},{2,6},{6,2},{1... | collective-permute-start | bytes 589832 | tf_op jit(solution)/shard_map/ppermute | solution.py:170
  10.9 6.4 %collective-permute-start.5 = (bf16[4,8,16,128]{3,2,1,0:T(8,128)(2,1)S(1)}, bf16[4,8,16,128]{3,2,1,0:T(8,128)(2,1)S(1)}, u32[]{:S(2)}, u32[]{:S(2)}) collective-permute-start(bf16[4,8,16,128]{3,2,1,0:T(8,128)(2,1)S(1)} %collective-permute-done.1.refs_4_.refs_2_), channel_id=1, source_target_pairs={{0,8},{4,12},{8,0},{12,4},{1,9},{5,13},{9,1},{13,5},{2,10},{6,14},... | collective-permute-start | bytes 393224 | tf_op jit(solution)/shard_map/ppermute | solution.py:170
  12.6 7.9 %collective-permute-start.8 = (bf16[6,8,16,128]{3,2,1,0:T(8,128)(2,1)S(1)}, bf16[6,8,16,128]{3,2,1,0:T(8,128)(2,1)S(1)}, u32[]{:S(2)}, u32[]{:S(2)}) collective-permute-start(bf16[6,8,16,128]{3,2,1,0:T(8,128)(2,1)S(1)} %pack2.1.own_hbm.refs_0_.refs_4_), channel_id=1, source_target_pairs={{0,8},{4,12},{8,0},{12,4},{1,9},{5,13},{9,1},{13,5},{2,10},{6,14},... | collective-permute-start | bytes 589832 | tf_op jit(solution)/shard_map/ppermute | solution.py:170
  13.0 4.4 %collective-permute-start.4 = (bf16[4,8,16,128]{3,2,1,0:T(8,128)(2,1)S(1)}, bf16[4,8,16,128]{3,2,1,0:T(8,128)(2,1)S(1)}, u32[]{:S(2)}, u32[]{:S(2)}) collective-permute-start(bf16[4,8,16,128]{3,2,1,0:T(8,128)(2,1)S(1)} %collective-permute-done.1.refs_4_.refs_2_), channel_id=1, source_target_pairs={{0,4},{4,0},{8,12},{12,8},{1,5},{5,1},{9,13},{13,9},{2,6},{6,2},{1... | collective-permute-start | bytes 393224 | tf_op jit(solution)/shard_map/ppermute | solution.py:170
  17.3 1.3 %collective-permute-start.7 = (bf16[4,8,16,128]{3,2,1,0:T(8,128)(2,1)S(1)}, bf16[4,8,16,128]{3,2,1,0:T(8,128)(2,1)S(1)}, u32[]{:S(2)}, u32[]{:S(2)}) collective-permute-start(bf16[4,8,16,128]{3,2,1,0:T(8,128)(2,1)S(1)} %collective-permute-done.5.refs_6_.refs_2_), channel_id=1, source_target_pairs={{0,4},{4,0},{8,12},{12,8},{1,5},{5,1},{9,13},{13,9},{2,6},{6,2},{1... | collective-permute-start | bytes 393224 | tf_op jit(solution)/shard_map/ppermute | solution.py:170
  20.6 3.9 %collective-permute-start.9 = (bf16[6,8,16,128]{3,2,1,0:T(8,128)(2,1)S(1)}, bf16[6,8,16,128]{3,2,1,0:T(8,128)(2,1)S(1)}, u32[]{:S(2)}, u32[]{:S(2)}) collective-permute-start(bf16[6,8,16,128]{3,2,1,0:T(8,128)(2,1)S(1)} %collective-permute-done.8.refs_0_.refs_6_), channel_id=1, source_target_pairs={{0,4},{4,0},{8,12},{12,8},{1,5},{5,1},{9,13},{13,9},{2,6},{6,2},{1... | collective-permute-start | bytes 589832 | tf_op jit(solution)/shard_map/ppermute | solution.py:170
  22.6 8.5 %collective-permute-start.13 = (bf16[232,128]{1,0:T(8,128)(2,1)S(1)}, bf16[232,128]{1,0:T(8,128)(2,1)S(1)}, u32[]{:S(2)}, u32[]{:S(2)}) collective-permute-start(bf16[232,128]{1,0:T(8,128)(2,1)S(1)} %wire.3), channel_id=1, source_target_pairs={{0,1},{1,0},{2,3},{3,2},{4,5},{5,4},{6,7},{7,6},{8,9},{9,8},{10,11... | collective-permute-start | bytes 178184 | tf_op jit(solution)/shard_map/ppermute | solution.py:748
  29.5 4.3 %collective-permute-start.10 = (bf16[232,128]{1,0:T(8,128)(2,1)S(1)}, bf16[232,128]{1,0:T(8,128)(2,1)S(1)}, u32[]{:S(2)}, u32[]{:S(2)}) collective-permute-start(bf16[232,128]{1,0:T(8,128)(2,1)S(1)} %wire.2), channel_id=1, source_target_pairs={{0,16},{16,0},{1,17},{17,1},{2,18},{18,2},{3,19},{19,3},{4,20},{20... | collective-permute-start | bytes 178184 | tf_op jit(solution)/shard_map/ppermute | solution.py:748
  31.2 5.9 %collective-permute-start.14 = (bf16[232,128]{1,0:T(8,128)(2,1)S(1)}, bf16[232,128]{1,0:T(8,128)(2,1)S(1)}, u32[]{:S(2)}, u32[]{:S(2)}) collective-permute-start(bf16[232,128]{1,0:T(8,128)(2,1)S(1)} %get-tuple-element.71), channel_id=1, source_target_pairs={{0,2},{1,3},{2,0},{3,1},{4,6},{5,7},{6,4},{7,5},{8,10},{9,11},{10,... | collective-permute-start | bytes 178184 | tf_op jit(solution)/shard_map/ppermute | solution.py:748
  33.9 4.2 %collective-permute-start.11 = (bf16[232,128]{1,0:T(8,128)(2,1)S(1)}, bf16[232,128]{1,0:T(8,128)(2,1)S(1)}, u32[]{:S(2)}, u32[]{:S(2)}) collective-permute-start(bf16[232,128]{1,0:T(8,128)(2,1)S(1)} %get-tuple-element.66), channel_id=1, source_target_pairs={{0,1},{1,0},{2,3},{3,2},{4,5},{5,4},{6,7},{7,6},{8,9},{9,8},{10,11... | collective-permute-start | bytes 178184 | tf_op jit(solution)/shard_map/ppermute | solution.py:748
  37.1 4.6 %collective-permute-start.15 = (bf16[360,128]{1,0:T(8,128)(2,1)S(1)}, bf16[360,128]{1,0:T(8,128)(2,1)S(1)}, u32[]{:S(2)}, u32[]{:S(2)}) collective-permute-start(bf16[360,128]{1,0:T(8,128)(2,1)S(1)} %get-tuple-element.74), channel_id=1, source_target_pairs={{0,16},{16,0},{1,17},{17,1},{2,18},{18,2},{3,19},{19,3},{4,20},{20... | collective-permute-start | bytes 276488 | tf_op jit(solution)/shard_map/ppermute | solution.py:748
  38.2 5.1 %collective-permute-start.12 = (bf16[232,128]{1,0:T(8,128)(2,1)S(1)}, bf16[232,128]{1,0:T(8,128)(2,1)S(1)}, u32[]{:S(2)}, u32[]{:S(2)}) collective-permute-start(bf16[232,128]{1,0:T(8,128)(2,1)S(1)} %get-tuple-element.68), channel_id=1, source_target_pairs={{0,2},{1,3},{2,0},{3,1},{4,6},{5,7},{6,4},{7,5},{8,10},{9,11},{10,... | collective-permute-start | bytes 178184 | tf_op jit(solution)/shard_map/ppermute | solution.py:748

commit v5 on v4

--- a/solution.py
+++ b/solution.py
@@ -194,7 +194,7 @@
     x = flip_perm(packed, 2)
     y = over(edge)
     c = flip_perm(packed, 1)
-    (second,) = pack(after(upstream, c), weight2, bias2, "pack2")
+    (second,) = pack(upstream, weight2, bias2, "pack2")
     y, x = lax.optimization_barrier((y, x, second))[:2]
     d = flip_perm(y, 2)
     xc = flip_perm(x, 1)
@@ -946,7 +946,7 @@
     steps1 = rounds(plan)
     steps2 = steps1[1:] + steps1[:1]
     got1 = exchange(first_wire(part1, plan), steps1[0])
-    got2 = exchange(first_wire(part2, plan), steps2[0])
+    got2 = exchange(first_wire(after(part2, delta2), plan), steps2[0])
     for step in steps1[1:]:
         part1, got1 = total_step(part1, got1, step, plan)
     for n, step in enumerate(steps2[1:], 2):

time: 44.5 us -> 43.8 us (0.984)
  waiting for transfers between devices: 9.88 us -> 9.27 us
    ppermute x1, waiting for transfers between devices: 2.94 us -> 2.35 us  [over(): return lax.ppermute(value, 'space', [(0, 1), (1, 0)])]
  transfers between devices with their start and end apart: 16 -> 16, of which waited for: 8 -> 7; matrix products, arithmetic and copies ran while one was open for 0% -> 0% of each run, Pallas kernels for 33% -> 29%
where the time goes in v5:
time: 43.8 us; the launch traced here: 43.6 us
  Pallas kernels  16.8 us (38%)
  starting transfers between devices  16.8 us (38%)
  waiting for transfers between devices  9.27 us (21%)
  between operations  0.76 us (2%)
    ppermute x6, starting transfers between devices, exchange(): lax.ppermute(wire, axis, [(i, i ^ bit) for i in range(lax.axis_size(axis))])  9.57 us
    ppermute x9, starting transfers between devices, flip_perm(): return lax.ppermute(value, 'filt', [(i, i ^ flip) for i in range(n)])  5.69 us
    ppermute x6, waiting for transfers between devices, exchange(): lax.ppermute(wire, axis, [(i, i ^ bit) for i in range(lax.axis_size(axis))])  4.01 us
    pallas_call x1, Pallas kernels, local(): call(functools.partial(third_kernel, plan, v_places), (shape((layers, ny,...  3.06 us
    ppermute x9, waiting for transfers between devices, flip_perm(): return lax.ppermute(value, 'filt', [(i, i ^ flip) for i in range(n)])  2.91 us
    ppermute x1, waiting for transfers between devices, over(): return lax.ppermute(value, 'space', [(0, 1), (1, 0)])  2.35 us
    pallas_call x2, Pallas kernels, pack(): pl.pallas_call(functools.partial(pack_kernel, edge), out_shape=tuple(outs...  2.2 us
    pallas_call x1, Pallas kernels, local(): call(functools.partial(far_kernel, plan, [u_places[k] for k in there]), (...  1.96 us
  transfers between devices with their start and end apart: 16, of which 7 were waited for; matrix products, arithmetic and copies ran while one was open for 0% of the time, Pallas kernels for 29%

profile of v5, /device:TPU:0, one launch (start us, length us, event | category | flops | bytes accessed | tf_op | source)
XLA Modules:
  0.0 43.6 jit_solution(10075147059379850020)
XLA Ops:
  0.6 1.1 %pack1.1 = (bf16[6,8,16,128]{3,2,1,0:T(8,128)(2,1)S(1)}, bf16[4,8,16,128]{3,2,1,0:T(8,128)(2,1)S(1)}) custom-call(bf16[16,4,8,128]{3,2,1,0:T(8,128)(2,1)} %bitcast.22, bf16[27,16,64]{2,1,0:T(8,128)(2,1)} %bitcast.23, f32[1,16]{1,0:T(1,128)} %bitcast.25, bf16[16,4,8,128]{3,2,1,0:T(8,128)(2,1)} %bitcast.20), custom_call_target="tpu_custom_call" | custom-call | bytes 262144 | tf_op jit(solution)/shard_map/pack1/pallas_call | solution.py:122
  1.8 3.0 %collective-permute-start.2 = (bf16[6,8,16,128]{3,2,1,0:T(8,128)(2,1)S(1)}, bf16[6,8,16,128]{3,2,1,0:T(8,128)(2,1)S(1)}, u32[]{:S(2)}, u32[]{:S(2)}) collective-permute-start(bf16[6,8,16,128]{3,2,1,0:T(8,128)(2,1)S(1)} %get-tuple-element.44.refs_0_), channel_id=1, source_target_pairs={{0,8},{4,12},{8,0},{12,4},{1,9},{5,13},{9,1},{13,5},{2,10},{6,14},... | collective-permute-start | bytes 589832 | tf_op jit(solution)/shard_map/ppermute | solution.py:170
  4.8 1.5 %collective-permute-start.1 = (bf16[4,8,16,128]{3,2,1,0:T(8,128)(2,1)S(1)}, bf16[4,8,16,128]{3,2,1,0:T(8,128)(2,1)S(1)}, u32[]{:S(2)}, u32[]{:S(2)}) collective-permute-start(bf16[4,8,16,128]{3,2,1,0:T(8,128)(2,1)S(1)} %get-tuple-element.45), channel_id=1, source_target_pairs={{0,16},{16,0},{1,17},{17,1},{2,18},{18,2},{3,19},{19,3},{4,20},{20... | collective-permute-start | bytes 393224 | tf_op jit(solution)/shard_map/ppermute | solution.py:174
  6.3 1.1 %pack2.1.own_hbm.refs_0_.refs_4_ = bf16[6,8,16,128]{3,2,1,0:T(8,128)(2,1)S(1)} custom-call(bf16[16,4,8,128]{3,2,1,0:T(8,128)(2,1)} %bitcast.21, bf16[27,16,64]{2,1,0:T(8,128)(2,1)} %bitcast.24, f32[1,16]{1,0:T(1,128)} %bitcast.26), custom_call_target="tpu_custom_call" | custom-call | bytes 262144 | tf_op jit(solution)/shard_map/pack2/pallas_call | solution.py:122
  7.4 2.4 %collective-permute-done.1.refs_4_.refs_2_ = bf16[4,8,16,128]{3,2,1,0:T(8,128)(2,1)S(1)} collective-permute-done((bf16[4,8,16,128]{3,2,1,0:T(8,128)(2,1)S(1)}, bf16[4,8,16,128]{3,2,1,0:T(8,128)(2,1)S(1)}, u32[]{:S(2)}, u32[]{:S(2)}) %collective-permute-start.1) | collective-permute-done | bytes 131104 | tf_op jit(solution)/shard_map/ppermute | solution.py:174
  9.8 0.5 %collective-permute-start.6 = (bf16[6,8,16,128]{3,2,1,0:T(8,128)(2,1)S(1)}, bf16[6,8,16,128]{3,2,1,0:T(8,128)(2,1)S(1)}, u32[]{:S(2)}, u32[]{:S(2)}) collective-permute-start(bf16[6,8,16,128]{3,2,1,0:T(8,128)(2,1)S(1)} %pack2.1.own_hbm.refs_0_.refs_4_), channel_id=1, source_target_pairs={{0,4},{4,0},{8,12},{12,8},{1,5},{5,1},{9,13},{13,9},{2,6},{6,2},{1... | collective-permute-start | bytes 589832 | tf_op jit(solution)/shard_map/ppermute | solution.py:170
  10.3 1.7 %collective-permute-start.5 = (bf16[4,8,16,128]{3,2,1,0:T(8,128)(2,1)S(1)}, bf16[4,8,16,128]{3,2,1,0:T(8,128)(2,1)S(1)}, u32[]{:S(2)}, u32[]{:S(2)}) collective-permute-start(bf16[4,8,16,128]{3,2,1,0:T(8,128)(2,1)S(1)} %collective-permute-done.1.refs_4_.refs_2_), channel_id=1, source_target_pairs={{0,8},{4,12},{8,0},{12,4},{1,9},{5,13},{9,1},{13,5},{2,10},{6,14},... | collective-permute-start | bytes 393224 | tf_op jit(solution)/shard_map/ppermute | solution.py:170
  11.9 0.4 collective-permute-start.8
  12.3 1.5 %early.1 = (bf16[3,8,64,128]{3,2,1,0:T(8,128)(2,1)S(1)}, f32[3,8,64,128]{3,2,1,0:T(8,128)S(1)}) custom-call(bf16[6,8,16,128]{3,2,1,0:T(8,128)(2,1)S(1)} %get-tuple-element.44.refs_0_, bf16[6,8,16,128]{3,2,1,0:T(8,128)(2,1)S(1)} %collective-permute-done.refs_1_, bf16[6,8,16,128]{3,2,1,0:T(8,128)(2,1)S(1)} %collective-permute-done.2.refs_2_, ...), custom_call_target="tpu_custom_call" | custom-call | flops 1 | tf_op jit(solution)/shard_map/early/pallas_call | solution.py:806
  13.9 1.3 %ahead.1 = (bf16[2,8,32,128]{3,2,1,0:T(8,128)(2,1)S(1)}, bf16[16,2,8,128]{3,2,1,0:T(8,128)(2,1)S(1)}, f32[144,192]{1,0:T(8,128)S(1)}, f32[16,128]{1,0:T(8,128)S(1)}) custom-call(bf16[3,8,64,128]{3,2,1,0:T(8,128)(2,1)S(1)} %get-tuple-element.48.eh_hbm.refs_8_, bf16[6,8,16,128]{3,2,1,0:T(8,128)(2,1)S(1)} %pack2.1.own_hbm.refs_0_.refs_4_, ...), custom_call_target="tpu_custom_call" | custom-call | flops 1 | tf_op jit(solution)/shard_map/ahead/pallas_call | solution.py:816
  15.2 1.4 %collective-permute-done.5.refs_6_.refs_2_ = bf16[4,8,16,128]{3,2,1,0:T(8,128)(2,1)S(1)} collective-permute-done((bf16[4,8,16,128]{3,2,1,0:T(8,128)(2,1)S(1)}, bf16[4,8,16,128]{3,2,1,0:T(8,128)(2,1)S(1)}, u32[]{:S(2)}, u32[]{:S(2)}) %collective-permute-start.5) | collective-permute-done | bytes 131104 | tf_op jit(solution)/shard_map/ppermute | solution.py:170
  16.6 1.3 %collective-permute-done.7.refs_7_.refs_3_ = bf16[4,8,16,128]{3,2,1,0:T(8,128)(2,1)S(1)} collective-permute-done((bf16[4,8,16,128]{3,2,1,0:T(8,128)(2,1)S(1)}, bf16[4,8,16,128]{3,2,1,0:T(8,128)(2,1)S(1)}, u32[]{:S(2)}, u32[]{:S(2)}) %collective-permute-start.7) | collective-permute-done | bytes 131104 | tf_op jit(solution)/shard_map/ppermute | solution.py:170
  18.0 1.8 %first.1 = (bf16[10,10,64,128]{3,2,1,0:T(8,128)(2,1)S(1)}, f32[6,8,64,128]{3,2,1,0:T(8,128)S(1)}) custom-call(bf16[6,8,16,128]{3,2,1,0:T(8,128)(2,1)S(1)} %get-tuple-element.44.refs_0_, bf16[6,8,16,128]{3,2,1,0:T(8,128)(2,1)S(1)} %collective-permute-done.refs_1_, bf16[6,8,16,128]{3,2,1,0:T(8,128)(2,1)S(1)} %collective-permute-done.2.refs_2_, ...), custom_call_target="tpu_custom_call" | custom-call | flops 1 | tf_op jit(solution)/shard_map/first/pallas_call | solution.py:859
  19.8 0.1 collective-permute-done.8.refs_0_.refs_6_
  19.9 0.1 collective-permute-start.9
  20.0 1.9 %near.1 = (bf16[5,8,32,128]{3,2,1,0:T(8,128)(2,1)S(1)}, bf16[16,4,8,128]{3,2,1,0:T(8,128)(2,1)S(1)}, f32[232,128]{1,0:T(8,128)S(1)}) custom-call(bf16[6,8,16,128]{3,2,1,0:T(8,128)(2,1)S(1)} %pack2.1.own_hbm.refs_0_.refs_4_, bf16[6,8,16,128]{3,2,1,0:T(8,128)(2,1)S(1)} %collective-permute-done.6.chip_hbm.refs_1_.refs_5_, ...), custom_call_target="tpu_custom_call" | custom-call | flops 1 | tf_op jit(solution)/shard_map/near/pallas_call | solution.py:872
  22.0 2.0 %far.1 = (bf16[10,10,64,128]{3,2,1,0:T(8,128)(2,1)S(1)}, bf16[3,64,576]{2,1,0:T(8,128)(2,1)S(1)}) custom-call(bf16[6,8,16,128]{3,2,1,0:T(8,128)(2,1)S(1)} %collective-permute-done.8.refs_0_.refs_6_, bf16[6,8,16,128]{3,2,1,0:T(8,128)(2,1)S(1)} %collective-permute-done.9.refs_1_.refs_7_, bf16[4,8,16,128]{3,2,1,0:T(8,128)(2,1)S(1)} %collective-permute-done.5.refs_6_.refs_2_, ...), custom_call_target="tpu_custom_call" | custom-call | flops 1 | tf_op jit(solution)/shard_map/far/pallas_call | solution.py:893
  23.9 1.8 %collective-permute-start.13 = (bf16[232,128]{1,0:T(8,128)(2,1)S(1)}, bf16[232,128]{1,0:T(8,128)(2,1)S(1)}, u32[]{:S(2)}, u32[]{:S(2)}) collective-permute-start(bf16[232,128]{1,0:T(8,128)(2,1)S(1)} %wire.3), channel_id=1, source_target_pairs={{0,1},{1,0},{2,3},{3,2},{4,5},{5,4},{6,7},{7,6},{8,9},{9,8},{10,11... | collective-permute-start | bytes 178184 | tf_op jit(solution)/shard_map/ppermute | solution.py:748
  25.8 3.1 %third.1 = (bf16[4,8,64,128]{3,2,1,0:T(8,128)(2,1)S(1)}, f32[232,128]{1,0:T(8,128)S(1)}) custom-call(bf16[6,8,16,128]{3,2,1,0:T(8,128)(2,1)S(1)} %get-tuple-element.44.refs_0_, bf16[6,8,16,128]{3,2,1,0:T(8,128)(2,1)S(1)} %collective-permute-done.refs_1_, bf16[6,8,16,128]{3,2,1,0:T(8,128)(2,1)S(1)} %collective-permute-done.2.refs_2_, ...), custom_call_target="tpu_custom_call" | custom-call | flops 1 | tf_op jit(solution)/shard_map/third/pallas_call | solution.py:925
  28.9 1.6 %collective-permute-start.10 = (bf16[232,128]{1,0:T(8,128)(2,1)S(1)}, bf16[232,128]{1,0:T(8,128)(2,1)S(1)}, u32[]{:S(2)}, u32[]{:S(2)}) collective-permute-start(bf16[232,128]{1,0:T(8,128)(2,1)S(1)} %wire.2), channel_id=1, source_target_pairs={{0,16},{16,0},{1,17},{17,1},{2,18},{18,2},{3,19},{19,3},{4,20},{20... | collective-permute-start | bytes 178184 | tf_op jit(solution)/shard_map/ppermute | solution.py:748
  30.5 2.6 %collective-permute-start.14 = (bf16[232,128]{1,0:T(8,128)(2,1)S(1)}, bf16[232,128]{1,0:T(8,128)(2,1)S(1)}, u32[]{:S(2)}, u32[]{:S(2)}) collective-permute-start(bf16[232,128]{1,0:T(8,128)(2,1)S(1)} %get-tuple-element.71), channel_id=1, source_target_pairs={{0,2},{1,3},{2,0},{3,1},{4,6},{5,7},{6,4},{7,5},{8,10},{9,11},{10,... | collective-permute-start | bytes 178184 | tf_op jit(solution)/shard_map/ppermute | solution.py:748
  33.2 0.5 %collective-permute-start.11 = (bf16[232,128]{1,0:T(8,128)(2,1)S(1)}, bf16[232,128]{1,0:T(8,128)(2,1)S(1)}, u32[]{:S(2)}, u32[]{:S(2)}) collective-permute-start(bf16[232,128]{1,0:T(8,128)(2,1)S(1)} %get-tuple-element.65), channel_id=1, source_target_pairs={{0,1},{1,0},{2,3},{3,2},{4,5},{5,4},{6,7},{7,6},{8,9},{9,8},{10,11... | collective-permute-start | bytes 178184 | tf_op jit(solution)/shard_map/ppermute | solution.py:748
  33.7 0.3 turn.1.t_ref
  34.0 1.3 %fourth.1 = (f32[4,8,16,128]{3,2,1,0:T(8,128)S(1)}, bf16[128,128]{1,0:T(8,128)(2,1)S(1)}) custom-call(bf16[4,8,64,128]{3,2,1,0:T(8,128)(2,1)S(1)} %get-tuple-element.61.d_ref, bf16[3,64,576]{2,1,0:T(8,128)(2,1)S(1)} %turn.1.t_ref), custom_call_target="tpu_custom_call" | custom-call | flops 1 | tf_op jit(solution)/shard_map/fourth/pallas_call | solution.py:936
  35.4 1.0 %collective-permute-done.14.got_ref = bf16[232,128]{1,0:T(8,128)(2,1)S(1)} collective-permute-done((bf16[232,128]{1,0:T(8,128)(2,1)S(1)}, bf16[232,128]{1,0:T(8,128)(2,1)S(1)}, u32[]{:S(2)}, u32[]{:S(2)}) %collective-permute-start.14) | collective-permute-done | bytes 59424 | tf_op jit(solution)/shard_map/ppermute | solution.py:748
  36.4 0.1 step.7
  36.5 0.5 %collective-permute-start.15 = (bf16[360,128]{1,0:T(8,128)(2,1)S(1)}, bf16[360,128]{1,0:T(8,128)(2,1)S(1)}, u32[]{:S(2)}, u32[]{:S(2)}) collective-permute-start(bf16[360,128]{1,0:T(8,128)(2,1)S(1)} %get-tuple-element.74), channel_id=1, source_target_pairs={{0,16},{16,0},{1,17},{17,1},{2,18},{18,2},{3,19},{19,3},{4,20},{20... | collective-permute-start | bytes 276488 | tf_op jit(solution)/shard_map/ppermute | solution.py:748
  37.0 0.4 collective-permute-done.11.got_ref
  37.4 0.1 step.5
  37.5 2.6 %collective-permute-start.12 = (bf16[232,128]{1,0:T(8,128)(2,1)S(1)}, bf16[232,128]{1,0:T(8,128)(2,1)S(1)}, u32[]{:S(2)}, u32[]{:S(2)}) collective-permute-start(bf16[232,128]{1,0:T(8,128)(2,1)S(1)} %get-tuple-element.67), channel_id=1, source_target_pairs={{0,2},{1,3},{2,0},{3,1},{4,6},{5,7},{6,4},{7,5},{8,10},{9,11},{10,... | collective-permute-start | bytes 178184 | tf_op jit(solution)/shard_map/ppermute | solution.py:748
  40.1 2.5 %collective-permute-done.12.got1_ref = bf16[232,128]{1,0:T(8,128)(2,1)S(1)} collective-permute-done((bf16[232,128]{1,0:T(8,128)(2,1)S(1)}, bf16[232,128]{1,0:T(8,128)(2,1)S(1)}, u32[]{:S(2)}, u32[]{:S(2)}) %collective-permute-start.12) | collective-permute-done | bytes 59424 | tf_op jit(solution)/shard_map/ppermute | solution.py:748
  42.6 1.0 %close.1 = (f32[27,16,64]{2,1,0:T(8,128)}, f32[1,16]{1,0:T(1,128)}, f32[27,16,64]{2,1,0:T(8,128)}, f32[1,16]{1,0:T(1,128)}, bf16[16,4,8,128]{3,2,1,0:T(8,128)(2,1)}, /*index=5*/bf16[16,4,8,128]{3,2,1,0:T(8,128)(2,1)}) custom-call(f32[4,8,16,128]{3,2,1,0:T(8,128)S(1)} %get-tuple-element.62.r_hbm, f32[232,128]{1,0:T(8,128)S(1)} %get-tuple-element.66.a1_ref, ...), custom_call_target="tpu_custom_call" | custom-call | tf_op jit(solution)/shard_map/close/pallas_call | solution.py:958
  (17 shorter events, 0.2 us)
Async XLA Ops:
  1.8 8.0 %collective-permute-start.2 = (bf16[6,8,16,128]{3,2,1,0:T(8,128)(2,1)S(1)}, bf16[6,8,16,128]{3,2,1,0:T(8,128)(2,1)S(1)}, u32[]{:S(2)}, u32[]{:S(2)}) collective-permute-start(bf16[6,8,16,128]{3,2,1,0:T(8,128)(2,1)S(1)} %get-tuple-element.44.refs_0_), channel_id=1, source_target_pairs={{0,8},{4,12},{8,0},{12,4},{1,9},{5,13},{9,1},{13,5},{2,10},{6,14},... | collective-permute-start | bytes 589832 | tf_op jit(solution)/shard_map/ppermute | solution.py:170
  4.8 5.0 %collective-permute-start.1 = (bf16[4,8,16,128]{3,2,1,0:T(8,128)(2,1)S(1)}, bf16[4,8,16,128]{3,2,1,0:T(8,128)(2,1)S(1)}, u32[]{:S(2)}, u32[]{:S(2)}) collective-permute-start(bf16[4,8,16,128]{3,2,1,0:T(8,128)(2,1)S(1)} %get-tuple-element.45), channel_id=1, source_target_pairs={{0,16},{16,0},{1,17},{17,1},{2,18},{18,2},{3,19},{19,3},{4,20},{20... | collective-permute-start | bytes 393224 | tf_op jit(solution)/shard_map/ppermute | solution.py:174
  6.3 6.0 %collective-permute-start = (bf16[6,8,16,128]{3,2,1,0:T(8,128)(2,1)S(1)}, bf16[6,8,16,128]{3,2,1,0:T(8,128)(2,1)S(1)}, u32[]{:S(2)}, u32[]{:S(2)}) collective-permute-start(bf16[6,8,16,128]{3,2,1,0:T(8,128)(2,1)S(1)} %get-tuple-element.44.refs_0_), channel_id=1, source_target_pairs={{0,4},{4,0},{8,12},{12,8},{1,5},{5,1},{9,13},{13,9},{2,6},{6,2},{1... | collective-permute-start | bytes 589832 | tf_op jit(solution)/shard_map/ppermute | solution.py:170
  9.8 2.5 %collective-permute-start.3 = (bf16[6,8,16,128]{3,2,1,0:T(8,128)(2,1)S(1)}, bf16[6,8,16,128]{3,2,1,0:T(8,128)(2,1)S(1)}, u32[]{:S(2)}, u32[]{:S(2)}) collective-permute-start(bf16[6,8,16,128]{3,2,1,0:T(8,128)(2,1)S(1)} %collective-permute-done.2.refs_2_), channel_id=1, source_target_pairs={{0,4},{4,0},{8,12},{12,8},{1,5},{5,1},{9,13},{13,9},{2,6},{6,2},{1... | collective-permute-start | bytes 589832 | tf_op jit(solution)/shard_map/ppermute | solution.py:170
  9.8 4.1 %collective-permute-start.6 = (bf16[6,8,16,128]{3,2,1,0:T(8,128)(2,1)S(1)}, bf16[6,8,16,128]{3,2,1,0:T(8,128)(2,1)S(1)}, u32[]{:S(2)}, u32[]{:S(2)}) collective-permute-start(bf16[6,8,16,128]{3,2,1,0:T(8,128)(2,1)S(1)} %pack2.1.own_hbm.refs_0_.refs_4_), channel_id=1, source_target_pairs={{0,4},{4,0},{8,12},{12,8},{1,5},{5,1},{9,13},{13,9},{2,6},{6,2},{1... | collective-permute-start | bytes 589832 | tf_op jit(solution)/shard_map/ppermute | solution.py:170
  10.3 6.4 %collective-permute-start.5 = (bf16[4,8,16,128]{3,2,1,0:T(8,128)(2,1)S(1)}, bf16[4,8,16,128]{3,2,1,0:T(8,128)(2,1)S(1)}, u32[]{:S(2)}, u32[]{:S(2)}) collective-permute-start(bf16[4,8,16,128]{3,2,1,0:T(8,128)(2,1)S(1)} %collective-permute-done.1.refs_4_.refs_2_), channel_id=1, source_target_pairs={{0,8},{4,12},{8,0},{12,4},{1,9},{5,13},{9,1},{13,5},{2,10},{6,14},... | collective-permute-start | bytes 393224 | tf_op jit(solution)/shard_map/ppermute | solution.py:170
  11.9 7.9 %collective-permute-start.8 = (bf16[6,8,16,128]{3,2,1,0:T(8,128)(2,1)S(1)}, bf16[6,8,16,128]{3,2,1,0:T(8,128)(2,1)S(1)}, u32[]{:S(2)}, u32[]{:S(2)}) collective-permute-start(bf16[6,8,16,128]{3,2,1,0:T(8,128)(2,1)S(1)} %pack2.1.own_hbm.refs_0_.refs_4_), channel_id=1, source_target_pairs={{0,8},{4,12},{8,0},{12,4},{1,9},{5,13},{9,1},{13,5},{2,10},{6,14},... | collective-permute-start | bytes 589832 | tf_op jit(solution)/shard_map/ppermute | solution.py:170
  12.3 4.3 %collective-permute-start.4 = (bf16[4,8,16,128]{3,2,1,0:T(8,128)(2,1)S(1)}, bf16[4,8,16,128]{3,2,1,0:T(8,128)(2,1)S(1)}, u32[]{:S(2)}, u32[]{:S(2)}) collective-permute-start(bf16[4,8,16,128]{3,2,1,0:T(8,128)(2,1)S(1)} %collective-permute-done.1.refs_4_.refs_2_), channel_id=1, source_target_pairs={{0,4},{4,0},{8,12},{12,8},{1,5},{5,1},{9,13},{13,9},{2,6},{6,2},{1... | collective-permute-start | bytes 393224 | tf_op jit(solution)/shard_map/ppermute | solution.py:170
  16.6 1.3 %collective-permute-start.7 = (bf16[4,8,16,128]{3,2,1,0:T(8,128)(2,1)S(1)}, bf16[4,8,16,128]{3,2,1,0:T(8,128)(2,1)S(1)}, u32[]{:S(2)}, u32[]{:S(2)}) collective-permute-start(bf16[4,8,16,128]{3,2,1,0:T(8,128)(2,1)S(1)} %collective-permute-done.5.refs_6_.refs_2_), channel_id=1, source_target_pairs={{0,4},{4,0},{8,12},{12,8},{1,5},{5,1},{9,13},{13,9},{2,6},{6,2},{1... | collective-permute-start | bytes 393224 | tf_op jit(solution)/shard_map/ppermute | solution.py:170
  19.9 2.1 %collective-permute-start.9 = (bf16[6,8,16,128]{3,2,1,0:T(8,128)(2,1)S(1)}, bf16[6,8,16,128]{3,2,1,0:T(8,128)(2,1)S(1)}, u32[]{:S(2)}, u32[]{:S(2)}) collective-permute-start(bf16[6,8,16,128]{3,2,1,0:T(8,128)(2,1)S(1)} %collective-permute-done.8.refs_0_.refs_6_), channel_id=1, source_target_pairs={{0,4},{4,0},{8,12},{12,8},{1,5},{5,1},{9,13},{13,9},{2,6},{6,2},{1... | collective-permute-start | bytes 589832 | tf_op jit(solution)/shard_map/ppermute | solution.py:170
  23.9 6.5 %collective-permute-start.13 = (bf16[232,128]{1,0:T(8,128)(2,1)S(1)}, bf16[232,128]{1,0:T(8,128)(2,1)S(1)}, u32[]{:S(2)}, u32[]{:S(2)}) collective-permute-start(bf16[232,128]{1,0:T(8,128)(2,1)S(1)} %wire.3), channel_id=1, source_target_pairs={{0,1},{1,0},{2,3},{3,2},{4,5},{5,4},{6,7},{7,6},{8,9},{9,8},{10,11... | collective-permute-start | bytes 178184 | tf_op jit(solution)/shard_map/ppermute | solution.py:748
  28.9 4.3 %collective-permute-start.10 = (bf16[232,128]{1,0:T(8,128)(2,1)S(1)}, bf16[232,128]{1,0:T(8,128)(2,1)S(1)}, u32[]{:S(2)}, u32[]{:S(2)}) collective-permute-start(bf16[232,128]{1,0:T(8,128)(2,1)S(1)} %wire.2), channel_id=1, source_target_pairs={{0,16},{16,0},{1,17},{17,1},{2,18},{18,2},{3,19},{19,3},{4,20},{20... | collective-permute-start | bytes 178184 | tf_op jit(solution)/shard_map/ppermute | solution.py:748
  30.5 5.9 %collective-permute-start.14 = (bf16[232,128]{1,0:T(8,128)(2,1)S(1)}, bf16[232,128]{1,0:T(8,128)(2,1)S(1)}, u32[]{:S(2)}, u32[]{:S(2)}) collective-permute-start(bf16[232,128]{1,0:T(8,128)(2,1)S(1)} %get-tuple-element.71), channel_id=1, source_target_pairs={{0,2},{1,3},{2,0},{3,1},{4,6},{5,7},{6,4},{7,5},{8,10},{9,11},{10,... | collective-permute-start | bytes 178184 | tf_op jit(solution)/shard_map/ppermute | solution.py:748
  33.2 4.2 %collective-permute-start.11 = (bf16[232,128]{1,0:T(8,128)(2,1)S(1)}, bf16[232,128]{1,0:T(8,128)(2,1)S(1)}, u32[]{:S(2)}, u32[]{:S(2)}) collective-permute-start(bf16[232,128]{1,0:T(8,128)(2,1)S(1)} %get-tuple-element.65), channel_id=1, source_target_pairs={{0,1},{1,0},{2,3},{3,2},{4,5},{5,4},{6,7},{7,6},{8,9},{9,8},{10,11... | collective-permute-start | bytes 178184 | tf_op jit(solution)/shard_map/ppermute | solution.py:748
  36.5 6.1 %collective-permute-start.15 = (bf16[360,128]{1,0:T(8,128)(2,1)S(1)}, bf16[360,128]{1,0:T(8,128)(2,1)S(1)}, u32[]{:S(2)}, u32[]{:S(2)}) collective-permute-start(bf16[360,128]{1,0:T(8,128)(2,1)S(1)} %get-tuple-element.74), channel_id=1, source_target_pairs={{0,16},{16,0},{1,17},{17,1},{2,18},{18,2},{3,19},{19,3},{4,20},{20... | collective-permute-start | bytes 276488 | tf_op jit(solution)/shard_map/ppermute | solution.py:748
  37.5 5.1 %collective-permute-start.12 = (bf16[232,128]{1,0:T(8,128)(2,1)S(1)}, bf16[232,128]{1,0:T(8,128)(2,1)S(1)}, u32[]{:S(2)}, u32[]{:S(2)}) collective-permute-start(bf16[232,128]{1,0:T(8,128)(2,1)S(1)} %get-tuple-element.67), channel_id=1, source_target_pairs={{0,2},{1,3},{2,0},{3,1},{4,6},{5,7},{6,4},{7,5},{8,10},{9,11},{10,... | collective-permute-start | bytes 178184 | tf_op jit(solution)/shard_map/ppermute | solution.py:748

commit v6 on v5

--- a/solution.py
+++ b/solution.py
@@ -706,12 +706,11 @@
     w_ref[total.shape[0] :] = share_ref[...]
 
 
-def close_kernel(plan, rows, scale, r_hbm, a1_ref, got1_ref, a2_ref, got2_ref, out_ref, *refs):
-    w1_ref, b1_ref, w2_ref, b2_ref, o_ref, out2_ref, r_ref, sem = refs
+def close_kernel(plan, rows, scale, r_hbm, a2_ref, got2_ref, out_ref, *refs):
+    w2_ref, b2_ref, o_ref, out2_ref, r_ref, sem = refs
     copy = pltpu.make_async_copy(r_hbm, r_ref, sem)
     copy.start()
     out2_ref[...] = out_ref[...]
-    last_kernel(rows, plan.group, scale, a1_ref, got1_ref, w1_ref, b1_ref)
     last_kernel(rows, plan.group, scale, a2_ref, got2_ref, w2_ref, b2_ref)
     copy.wait()
     layer = (1 - lax.axis_index("space")) * (plan.layers - 1)
@@ -955,15 +954,15 @@
     volume_shape = shape((group, layers, ny, nz), BF)
     finish_scratch = [VM((layers, ny, group, nz), F32), dma]
     if plan.pair:
-        w1, b1, w2, b2, volume_grad, output = call(
+        w2, b2, volume_grad, output = call(
             functools.partial(close_kernel, plan, part2.shape[0] - group, scale),
-            (*grad_shapes(plan), *grad_shapes(plan), volume_shape, volume_shape),
+            (*grad_shapes(plan), volume_shape, volume_shape),
             1,
-            5,
+            3,
             finish_scratch,
             name="close",
-        )(own_grad, part1, got1, part2, got2, output)
-        grad1, bias_grad1 = as_grads(w1, b1, plan)
+        )(own_grad, part2, got2, output)
+        grad1, bias_grad1 = total_last(after(part1, w2), got1, plan, scale)
         grad2, bias_grad2 = as_grads(w2, b2, plan)
     else:
         grad1, bias_grad1 = total_last(part1, got1, plan, scale)

time: 43.8 us -> 43.6 us (level)
  waiting for transfers between devices: 9.27 us -> 8.36 us
  Pallas kernels: 16.8 us -> 17.5 us
    ppermute x6, waiting for transfers between devices: 4.01 us -> 3.09 us  [exchange(): lax.ppermute(wire, axis, [(i, i ^ bit) for i in range(lax.axis_size(axis))])]
    pallas_call x0 -> x1, Pallas kernels: none -> 0.79 us  [total_last(): call(functools.partial(last_kernel, rows, plan.group, scale), grad_shapes...]
  transfers between devices with their start and end apart: 16 -> 16, of which waited for: 7 -> 8; matrix products, arithmetic and copies ran while one was open for 0% -> 0% of each run, Pallas kernels for 29% -> 31%
where the time goes in v6:
time: 43.6 us; the launch traced here: 43.4 us
  Pallas kernels  17.5 us (40%)
  starting transfers between devices  16.8 us (39%)
  waiting for transfers between devices  8.36 us (19%)
  between operations  0.77 us (2%)
    ppermute x6, starting transfers between devices, exchange(): lax.ppermute(wire, axis, [(i, i ^ bit) for i in range(lax.axis_size(axis))])  9.56 us
    ppermute x9, starting transfers between devices, flip_perm(): return lax.ppermute(value, 'filt', [(i, i ^ flip) for i in range(n)])  5.69 us
    ppermute x6, waiting for transfers between devices, exchange(): lax.ppermute(wire, axis, [(i, i ^ bit) for i in range(lax.axis_size(axis))])  3.09 us
    pallas_call x1, Pallas kernels, local(): call(functools.partial(third_kernel, plan, v_places), (shape((layers, ny,...  3.06 us
    ppermute x9, waiting for transfers between devices, flip_perm(): return lax.ppermute(value, 'filt', [(i, i ^ flip) for i in range(n)])  2.91 us
    ppermute x1, waiting for transfers between devices, over(): return lax.ppermute(value, 'space', [(0, 1), (1, 0)])  2.35 us
    pallas_call x2, Pallas kernels, pack(): pl.pallas_call(functools.partial(pack_kernel, edge), out_shape=tuple(outs...  2.2 us
    pallas_call x1, Pallas kernels, local(): call(functools.partial(far_kernel, plan, [u_places[k] for k in there]), (...  1.96 us
  transfers between devices with their start and end apart: 16, of which 8 were waited for; matrix products, arithmetic and copies ran while one was open for 0% of the time, Pallas kernels for 31%

profile of v6, /device:TPU:0, one launch (start us, length us, event | category | flops | bytes accessed | tf_op | source)
XLA Modules:
  0.0 43.4 jit_solution(1590804897152023052)
XLA Ops:
  0.6 1.1 %pack1.1 = (bf16[6,8,16,128]{3,2,1,0:T(8,128)(2,1)S(1)}, bf16[4,8,16,128]{3,2,1,0:T(8,128)(2,1)S(1)}) custom-call(bf16[16,4,8,128]{3,2,1,0:T(8,128)(2,1)} %bitcast.22, bf16[27,16,64]{2,1,0:T(8,128)(2,1)} %bitcast.23, f32[1,16]{1,0:T(1,128)} %bitcast.25, bf16[16,4,8,128]{3,2,1,0:T(8,128)(2,1)} %bitcast.20), custom_call_target="tpu_custom_call" | custom-call | bytes 262144 | tf_op jit(solution)/shard_map/pack1/pallas_call | solution.py:122
  1.8 3.0 %collective-permute-start.2 = (bf16[6,8,16,128]{3,2,1,0:T(8,128)(2,1)S(1)}, bf16[6,8,16,128]{3,2,1,0:T(8,128)(2,1)S(1)}, u32[]{:S(2)}, u32[]{:S(2)}) collective-permute-start(bf16[6,8,16,128]{3,2,1,0:T(8,128)(2,1)S(1)} %get-tuple-element.45.refs_0_), channel_id=1, source_target_pairs={{0,8},{4,12},{8,0},{12,4},{1,9},{5,13},{9,1},{13,5},{2,10},{6,14},... | collective-permute-start | bytes 589832 | tf_op jit(solution)/shard_map/ppermute | solution.py:170
  4.8 1.5 %collective-permute-start.1 = (bf16[4,8,16,128]{3,2,1,0:T(8,128)(2,1)S(1)}, bf16[4,8,16,128]{3,2,1,0:T(8,128)(2,1)S(1)}, u32[]{:S(2)}, u32[]{:S(2)}) collective-permute-start(bf16[4,8,16,128]{3,2,1,0:T(8,128)(2,1)S(1)} %get-tuple-element.46), channel_id=1, source_target_pairs={{0,16},{16,0},{1,17},{17,1},{2,18},{18,2},{3,19},{19,3},{4,20},{20... | collective-permute-start | bytes 393224 | tf_op jit(solution)/shard_map/ppermute | solution.py:174
  6.3 1.1 %pack2.1.own_hbm.refs_0_.refs_4_ = bf16[6,8,16,128]{3,2,1,0:T(8,128)(2,1)S(1)} custom-call(bf16[16,4,8,128]{3,2,1,0:T(8,128)(2,1)} %bitcast.21, bf16[27,16,64]{2,1,0:T(8,128)(2,1)} %bitcast.24, f32[1,16]{1,0:T(1,128)} %bitcast.26), custom_call_target="tpu_custom_call" | custom-call | bytes 262144 | tf_op jit(solution)/shard_map/pack2/pallas_call | solution.py:122
  7.4 2.4 %collective-permute-done.1.refs_4_.refs_2_ = bf16[4,8,16,128]{3,2,1,0:T(8,128)(2,1)S(1)} collective-permute-done((bf16[4,8,16,128]{3,2,1,0:T(8,128)(2,1)S(1)}, bf16[4,8,16,128]{3,2,1,0:T(8,128)(2,1)S(1)}, u32[]{:S(2)}, u32[]{:S(2)}) %collective-permute-start.1) | collective-permute-done | bytes 131104 | tf_op jit(solution)/shard_map/ppermute | solution.py:174
  9.8 0.5 %collective-permute-start.6 = (bf16[6,8,16,128]{3,2,1,0:T(8,128)(2,1)S(1)}, bf16[6,8,16,128]{3,2,1,0:T(8,128)(2,1)S(1)}, u32[]{:S(2)}, u32[]{:S(2)}) collective-permute-start(bf16[6,8,16,128]{3,2,1,0:T(8,128)(2,1)S(1)} %pack2.1.own_hbm.refs_0_.refs_4_), channel_id=1, source_target_pairs={{0,4},{4,0},{8,12},{12,8},{1,5},{5,1},{9,13},{13,9},{2,6},{6,2},{1... | collective-permute-start | bytes 589832 | tf_op jit(solution)/shard_map/ppermute | solution.py:170
  10.3 1.7 %collective-permute-start.5 = (bf16[4,8,16,128]{3,2,1,0:T(8,128)(2,1)S(1)}, bf16[4,8,16,128]{3,2,1,0:T(8,128)(2,1)S(1)}, u32[]{:S(2)}, u32[]{:S(2)}) collective-permute-start(bf16[4,8,16,128]{3,2,1,0:T(8,128)(2,1)S(1)} %collective-permute-done.1.refs_4_.refs_2_), channel_id=1, source_target_pairs={{0,8},{4,12},{8,0},{12,4},{1,9},{5,13},{9,1},{13,5},{2,10},{6,14},... | collective-permute-start | bytes 393224 | tf_op jit(solution)/shard_map/ppermute | solution.py:170
  11.9 0.4 collective-permute-start.8
  12.3 1.5 %early.1 = (bf16[3,8,64,128]{3,2,1,0:T(8,128)(2,1)S(1)}, f32[3,8,64,128]{3,2,1,0:T(8,128)S(1)}) custom-call(bf16[6,8,16,128]{3,2,1,0:T(8,128)(2,1)S(1)} %get-tuple-element.45.refs_0_, bf16[6,8,16,128]{3,2,1,0:T(8,128)(2,1)S(1)} %collective-permute-done.refs_1_, bf16[6,8,16,128]{3,2,1,0:T(8,128)(2,1)S(1)} %collective-permute-done.2.refs_2_, ...), custom_call_target="tpu_custom_call" | custom-call | flops 1 | tf_op jit(solution)/shard_map/early/pallas_call | solution.py:805
  13.9 1.3 %ahead.1 = (bf16[2,8,32,128]{3,2,1,0:T(8,128)(2,1)S(1)}, bf16[16,2,8,128]{3,2,1,0:T(8,128)(2,1)S(1)}, f32[144,192]{1,0:T(8,128)S(1)}, f32[16,128]{1,0:T(8,128)S(1)}) custom-call(bf16[3,8,64,128]{3,2,1,0:T(8,128)(2,1)S(1)} %get-tuple-element.49.eh_hbm.refs_8_, bf16[6,8,16,128]{3,2,1,0:T(8,128)(2,1)S(1)} %pack2.1.own_hbm.refs_0_.refs_4_, ...), custom_call_target="tpu_custom_call" | custom-call | flops 1 | tf_op jit(solution)/shard_map/ahead/pallas_call | solution.py:815
  15.2 1.4 %collective-permute-done.5.refs_6_.refs_2_ = bf16[4,8,16,128]{3,2,1,0:T(8,128)(2,1)S(1)} collective-permute-done((bf16[4,8,16,128]{3,2,1,0:T(8,128)(2,1)S(1)}, bf16[4,8,16,128]{3,2,1,0:T(8,128)(2,1)S(1)}, u32[]{:S(2)}, u32[]{:S(2)}) %collective-permute-start.5) | collective-permute-done | bytes 131104 | tf_op jit(solution)/shard_map/ppermute | solution.py:170
  16.6 1.3 %collective-permute-done.7.refs_7_.refs_3_ = bf16[4,8,16,128]{3,2,1,0:T(8,128)(2,1)S(1)} collective-permute-done((bf16[4,8,16,128]{3,2,1,0:T(8,128)(2,1)S(1)}, bf16[4,8,16,128]{3,2,1,0:T(8,128)(2,1)S(1)}, u32[]{:S(2)}, u32[]{:S(2)}) %collective-permute-start.7) | collective-permute-done | bytes 131104 | tf_op jit(solution)/shard_map/ppermute | solution.py:170
  18.0 1.8 %first.1 = (bf16[10,10,64,128]{3,2,1,0:T(8,128)(2,1)S(1)}, f32[6,8,64,128]{3,2,1,0:T(8,128)S(1)}) custom-call(bf16[6,8,16,128]{3,2,1,0:T(8,128)(2,1)S(1)} %get-tuple-element.45.refs_0_, bf16[6,8,16,128]{3,2,1,0:T(8,128)(2,1)S(1)} %collective-permute-done.refs_1_, bf16[6,8,16,128]{3,2,1,0:T(8,128)(2,1)S(1)} %collective-permute-done.2.refs_2_, ...), custom_call_target="tpu_custom_call" | custom-call | flops 1 | tf_op jit(solution)/shard_map/first/pallas_call | solution.py:858
  19.8 0.1 collective-permute-done.8.refs_0_.refs_6_
  19.9 0.1 collective-permute-start.9
  20.0 1.9 %near.1 = (bf16[5,8,32,128]{3,2,1,0:T(8,128)(2,1)S(1)}, bf16[16,4,8,128]{3,2,1,0:T(8,128)(2,1)S(1)}, f32[232,128]{1,0:T(8,128)S(1)}) custom-call(bf16[6,8,16,128]{3,2,1,0:T(8,128)(2,1)S(1)} %pack2.1.own_hbm.refs_0_.refs_4_, bf16[6,8,16,128]{3,2,1,0:T(8,128)(2,1)S(1)} %collective-permute-done.6.chip_hbm.refs_1_.refs_5_, ...), custom_call_target="tpu_custom_call" | custom-call | flops 1 | tf_op jit(solution)/shard_map/near/pallas_call | solution.py:871
  22.0 2.0 %far.1 = (bf16[10,10,64,128]{3,2,1,0:T(8,128)(2,1)S(1)}, bf16[3,64,576]{2,1,0:T(8,128)(2,1)S(1)}) custom-call(bf16[6,8,16,128]{3,2,1,0:T(8,128)(2,1)S(1)} %collective-permute-done.8.refs_0_.refs_6_, bf16[6,8,16,128]{3,2,1,0:T(8,128)(2,1)S(1)} %collective-permute-done.9.refs_1_.refs_7_, bf16[4,8,16,128]{3,2,1,0:T(8,128)(2,1)S(1)} %collective-permute-done.5.refs_6_.refs_2_, ...), custom_call_target="tpu_custom_call" | custom-call | flops 1 | tf_op jit(solution)/shard_map/far/pallas_call | solution.py:892
  23.9 1.8 %collective-permute-start.10 = (bf16[232,128]{1,0:T(8,128)(2,1)S(1)}, bf16[232,128]{1,0:T(8,128)(2,1)S(1)}, u32[]{:S(2)}, u32[]{:S(2)}) collective-permute-start(bf16[232,128]{1,0:T(8,128)(2,1)S(1)} %wire.2), channel_id=1, source_target_pairs={{0,1},{1,0},{2,3},{3,2},{4,5},{5,4},{6,7},{7,6},{8,9},{9,8},{10,11... | collective-permute-start | bytes 178184 | tf_op jit(solution)/shard_map/ppermute | solution.py:747
  25.8 3.1 %third.1 = (bf16[4,8,64,128]{3,2,1,0:T(8,128)(2,1)S(1)}, f32[232,128]{1,0:T(8,128)S(1)}) custom-call(bf16[6,8,16,128]{3,2,1,0:T(8,128)(2,1)S(1)} %get-tuple-element.45.refs_0_, bf16[6,8,16,128]{3,2,1,0:T(8,128)(2,1)S(1)} %collective-permute-done.refs_1_, bf16[6,8,16,128]{3,2,1,0:T(8,128)(2,1)S(1)} %collective-permute-done.2.refs_2_, ...), custom_call_target="tpu_custom_call" | custom-call | flops 1 | tf_op jit(solution)/shard_map/third/pallas_call | solution.py:924
  28.9 1.6 %collective-permute-start.13 = (bf16[232,128]{1,0:T(8,128)(2,1)S(1)}, bf16[232,128]{1,0:T(8,128)(2,1)S(1)}, u32[]{:S(2)}, u32[]{:S(2)}) collective-permute-start(bf16[232,128]{1,0:T(8,128)(2,1)S(1)} %wire.3), channel_id=1, source_target_pairs={{0,16},{16,0},{1,17},{17,1},{2,18},{18,2},{3,19},{19,3},{4,20},{20... | collective-permute-start | bytes 178184 | tf_op jit(solution)/shard_map/ppermute | solution.py:747
  30.5 2.6 %collective-permute-start.11 = (bf16[232,128]{1,0:T(8,128)(2,1)S(1)}, bf16[232,128]{1,0:T(8,128)(2,1)S(1)}, u32[]{:S(2)}, u32[]{:S(2)}) collective-permute-start(bf16[232,128]{1,0:T(8,128)(2,1)S(1)} %get-tuple-element.67), channel_id=1, source_target_pairs={{0,2},{1,3},{2,0},{3,1},{4,6},{5,7},{6,4},{7,5},{8,10},{9,11},{10,... | collective-permute-start | bytes 178184 | tf_op jit(solution)/shard_map/ppermute | solution.py:747
  33.2 0.5 %collective-permute-start.14 = (bf16[232,128]{1,0:T(8,128)(2,1)S(1)}, bf16[232,128]{1,0:T(8,128)(2,1)S(1)}, u32[]{:S(2)}, u32[]{:S(2)}) collective-permute-start(bf16[232,128]{1,0:T(8,128)(2,1)S(1)} %get-tuple-element.76), channel_id=1, source_target_pairs={{0,1},{1,0},{2,3},{3,2},{4,5},{5,4},{6,7},{7,6},{8,9},{9,8},{10,11... | collective-permute-start | bytes 178184 | tf_op jit(solution)/shard_map/ppermute | solution.py:747
  33.7 0.3 turn.1.t_ref
  34.0 1.3 %fourth.1 = (f32[4,8,16,128]{3,2,1,0:T(8,128)S(1)}, bf16[128,128]{1,0:T(8,128)(2,1)S(1)}) custom-call(bf16[4,8,64,128]{3,2,1,0:T(8,128)(2,1)S(1)} %get-tuple-element.62.d_ref, bf16[3,64,576]{2,1,0:T(8,128)(2,1)S(1)} %turn.1.t_ref), custom_call_target="tpu_custom_call" | custom-call | flops 1 | tf_op jit(solution)/shard_map/fourth/pallas_call | solution.py:935
  35.4 1.0 %collective-permute-done.11.got_ref = bf16[232,128]{1,0:T(8,128)(2,1)S(1)} collective-permute-done((bf16[232,128]{1,0:T(8,128)(2,1)S(1)}, bf16[232,128]{1,0:T(8,128)(2,1)S(1)}, u32[]{:S(2)}, u32[]{:S(2)}) %collective-permute-start.11) | collective-permute-done | bytes 59424 | tf_op jit(solution)/shard_map/ppermute | solution.py:747
  36.5 0.5 %collective-permute-start.12 = (bf16[360,128]{1,0:T(8,128)(2,1)S(1)}, bf16[360,128]{1,0:T(8,128)(2,1)S(1)}, u32[]{:S(2)}, u32[]{:S(2)}) collective-permute-start(bf16[360,128]{1,0:T(8,128)(2,1)S(1)} %get-tuple-element.70), channel_id=1, source_target_pairs={{0,16},{16,0},{1,17},{17,1},{2,18},{18,2},{3,19},{19,3},{4,20},{20... | collective-permute-start | bytes 276488 | tf_op jit(solution)/shard_map/ppermute | solution.py:747
  37.0 0.4 collective-permute-done.14.got_ref
  37.5 2.6 %collective-permute-start.15 = (bf16[232,128]{1,0:T(8,128)(2,1)S(1)}, bf16[232,128]{1,0:T(8,128)(2,1)S(1)}, u32[]{:S(2)}, u32[]{:S(2)}) collective-permute-start(bf16[232,128]{1,0:T(8,128)(2,1)S(1)} %get-tuple-element.80), channel_id=1, source_target_pairs={{0,2},{1,3},{2,0},{3,1},{4,6},{5,7},{6,4},{7,5},{8,10},{9,11},{10,... | collective-permute-start | bytes 178184 | tf_op jit(solution)/shard_map/ppermute | solution.py:747
  40.1 1.0 %collective-permute-done.12.got2_ref = bf16[360,128]{1,0:T(8,128)(2,1)S(1)} collective-permute-done((bf16[360,128]{1,0:T(8,128)(2,1)S(1)}, bf16[360,128]{1,0:T(8,128)(2,1)S(1)}, u32[]{:S(2)}, u32[]{:S(2)}) %collective-permute-start.12) | collective-permute-done | bytes 92192 | tf_op jit(solution)/shard_map/ppermute | solution.py:747
  41.0 0.9 %close.1 = (f32[27,16,64]{2,1,0:T(8,128)}, f32[1,16]{1,0:T(1,128)}, bf16[16,4,8,128]{3,2,1,0:T(8,128)(2,1)}, bf16[16,4,8,128]{3,2,1,0:T(8,128)(2,1)}) custom-call(f32[4,8,16,128]{3,2,1,0:T(8,128)S(1)} %get-tuple-element.63.r_hbm, f32[232,128]{1,0:T(8,128)S(1)} %get-tuple-element.69.a2_ref, bf16[360,128]{1,0:T(8,128)(2,1)S(1)} %collective-permute-done.12.got2_ref, ...), custom_call_target="tpu_custom_call" | custom-call | tf_op jit(solution)/shard_map/close/pallas_call | solution.py:957
  42.0 0.7 %collective-permute-done.15.got_ref = bf16[232,128]{1,0:T(8,128)(2,1)S(1)} collective-permute-done((bf16[232,128]{1,0:T(8,128)(2,1)S(1)}, bf16[232,128]{1,0:T(8,128)(2,1)S(1)}, u32[]{:S(2)}, u32[]{:S(2)}) %collective-permute-start.15) | collective-permute-done | bytes 59424 | tf_op jit(solution)/shard_map/ppermute | solution.py:747
  42.6 0.8 %last.1 = (f32[27,16,64]{2,1,0:T(8,128)}, f32[1,16]{1,0:T(1,128)}) custom-call(f32[232,128]{1,0:T(8,128)S(1)} %get-tuple-element.79.a_ref, bf16[232,128]{1,0:T(8,128)(2,1)S(1)} %collective-permute-done.15.got_ref), custom_call_target="tpu_custom_call" | custom-call | tf_op jit(solution)/shard_map/last/pallas_call | solution.py:781
  (18 shorter events, 0.4 us)
Async XLA Ops:
  1.8 8.0 %collective-permute-start.2 = (bf16[6,8,16,128]{3,2,1,0:T(8,128)(2,1)S(1)}, bf16[6,8,16,128]{3,2,1,0:T(8,128)(2,1)S(1)}, u32[]{:S(2)}, u32[]{:S(2)}) collective-permute-start(bf16[6,8,16,128]{3,2,1,0:T(8,128)(2,1)S(1)} %get-tuple-element.45.refs_0_), channel_id=1, source_target_pairs={{0,8},{4,12},{8,0},{12,4},{1,9},{5,13},{9,1},{13,5},{2,10},{6,14},... | collective-permute-start | bytes 589832 | tf_op jit(solution)/shard_map/ppermute | solution.py:170
  4.8 5.0 %collective-permute-start.1 = (bf16[4,8,16,128]{3,2,1,0:T(8,128)(2,1)S(1)}, bf16[4,8,16,128]{3,2,1,0:T(8,128)(2,1)S(1)}, u32[]{:S(2)}, u32[]{:S(2)}) collective-permute-start(bf16[4,8,16,128]{3,2,1,0:T(8,128)(2,1)S(1)} %get-tuple-element.46), channel_id=1, source_target_pairs={{0,16},{16,0},{1,17},{17,1},{2,18},{18,2},{3,19},{19,3},{4,20},{20... | collective-permute-start | bytes 393224 | tf_op jit(solution)/shard_map/ppermute | solution.py:174
  6.3 6.0 %collective-permute-start = (bf16[6,8,16,128]{3,2,1,0:T(8,128)(2,1)S(1)}, bf16[6,8,16,128]{3,2,1,0:T(8,128)(2,1)S(1)}, u32[]{:S(2)}, u32[]{:S(2)}) collective-permute-start(bf16[6,8,16,128]{3,2,1,0:T(8,128)(2,1)S(1)} %get-tuple-element.45.refs_0_), channel_id=1, source_target_pairs={{0,4},{4,0},{8,12},{12,8},{1,5},{5,1},{9,13},{13,9},{2,6},{6,2},{1... | collective-permute-start | bytes 589832 | tf_op jit(solution)/shard_map/ppermute | solution.py:170
  9.8 2.5 %collective-permute-start.3 = (bf16[6,8,16,128]{3,2,1,0:T(8,128)(2,1)S(1)}, bf16[6,8,16,128]{3,2,1,0:T(8,128)(2,1)S(1)}, u32[]{:S(2)}, u32[]{:S(2)}) collective-permute-start(bf16[6,8,16,128]{3,2,1,0:T(8,128)(2,1)S(1)} %collective-permute-done.2.refs_2_), channel_id=1, source_target_pairs={{0,4},{4,0},{8,12},{12,8},{1,5},{5,1},{9,13},{13,9},{2,6},{6,2},{1... | collective-permute-start | bytes 589832 | tf_op jit(solution)/shard_map/ppermute | solution.py:170
  9.8 4.1 %collective-permute-start.6 = (bf16[6,8,16,128]{3,2,1,0:T(8,128)(2,1)S(1)}, bf16[6,8,16,128]{3,2,1,0:T(8,128)(2,1)S(1)}, u32[]{:S(2)}, u32[]{:S(2)}) collective-permute-start(bf16[6,8,16,128]{3,2,1,0:T(8,128)(2,1)S(1)} %pack2.1.own_hbm.refs_0_.refs_4_), channel_id=1, source_target_pairs={{0,4},{4,0},{8,12},{12,8},{1,5},{5,1},{9,13},{13,9},{2,6},{6,2},{1... | collective-permute-start | bytes 589832 | tf_op jit(solution)/shard_map/ppermute | solution.py:170
  10.3 6.4 %collective-permute-start.5 = (bf16[4,8,16,128]{3,2,1,0:T(8,128)(2,1)S(1)}, bf16[4,8,16,128]{3,2,1,0:T(8,128)(2,1)S(1)}, u32[]{:S(2)}, u32[]{:S(2)}) collective-permute-start(bf16[4,8,16,128]{3,2,1,0:T(8,128)(2,1)S(1)} %collective-permute-done.1.refs_4_.refs_2_), channel_id=1, source_target_pairs={{0,8},{4,12},{8,0},{12,4},{1,9},{5,13},{9,1},{13,5},{2,10},{6,14},... | collective-permute-start | bytes 393224 | tf_op jit(solution)/shard_map/ppermute | solution.py:170
  11.9 7.9 %collective-permute-start.8 = (bf16[6,8,16,128]{3,2,1,0:T(8,128)(2,1)S(1)}, bf16[6,8,16,128]{3,2,1,0:T(8,128)(2,1)S(1)}, u32[]{:S(2)}, u32[]{:S(2)}) collective-permute-start(bf16[6,8,16,128]{3,2,1,0:T(8,128)(2,1)S(1)} %pack2.1.own_hbm.refs_0_.refs_4_), channel_id=1, source_target_pairs={{0,8},{4,12},{8,0},{12,4},{1,9},{5,13},{9,1},{13,5},{2,10},{6,14},... | collective-permute-start | bytes 589832 | tf_op jit(solution)/shard_map/ppermute | solution.py:170
  12.3 4.3 %collective-permute-start.4 = (bf16[4,8,16,128]{3,2,1,0:T(8,128)(2,1)S(1)}, bf16[4,8,16,128]{3,2,1,0:T(8,128)(2,1)S(1)}, u32[]{:S(2)}, u32[]{:S(2)}) collective-permute-start(bf16[4,8,16,128]{3,2,1,0:T(8,128)(2,1)S(1)} %collective-permute-done.1.refs_4_.refs_2_), channel_id=1, source_target_pairs={{0,4},{4,0},{8,12},{12,8},{1,5},{5,1},{9,13},{13,9},{2,6},{6,2},{1... | collective-permute-start | bytes 393224 | tf_op jit(solution)/shard_map/ppermute | solution.py:170
  16.6 1.3 %collective-permute-start.7 = (bf16[4,8,16,128]{3,2,1,0:T(8,128)(2,1)S(1)}, bf16[4,8,16,128]{3,2,1,0:T(8,128)(2,1)S(1)}, u32[]{:S(2)}, u32[]{:S(2)}) collective-permute-start(bf16[4,8,16,128]{3,2,1,0:T(8,128)(2,1)S(1)} %collective-permute-done.5.refs_6_.refs_2_), channel_id=1, source_target_pairs={{0,4},{4,0},{8,12},{12,8},{1,5},{5,1},{9,13},{13,9},{2,6},{6,2},{1... | collective-permute-start | bytes 393224 | tf_op jit(solution)/shard_map/ppermute | solution.py:170
  19.9 2.1 %collective-permute-start.9 = (bf16[6,8,16,128]{3,2,1,0:T(8,128)(2,1)S(1)}, bf16[6,8,16,128]{3,2,1,0:T(8,128)(2,1)S(1)}, u32[]{:S(2)}, u32[]{:S(2)}) collective-permute-start(bf16[6,8,16,128]{3,2,1,0:T(8,128)(2,1)S(1)} %collective-permute-done.8.refs_0_.refs_6_), channel_id=1, source_target_pairs={{0,4},{4,0},{8,12},{12,8},{1,5},{5,1},{9,13},{13,9},{2,6},{6,2},{1... | collective-permute-start | bytes 589832 | tf_op jit(solution)/shard_map/ppermute | solution.py:170
  23.9 6.5 %collective-permute-start.10 = (bf16[232,128]{1,0:T(8,128)(2,1)S(1)}, bf16[232,128]{1,0:T(8,128)(2,1)S(1)}, u32[]{:S(2)}, u32[]{:S(2)}) collective-permute-start(bf16[232,128]{1,0:T(8,128)(2,1)S(1)} %wire.2), channel_id=1, source_target_pairs={{0,1},{1,0},{2,3},{3,2},{4,5},{5,4},{6,7},{7,6},{8,9},{9,8},{10,11... | collective-permute-start | bytes 178184 | tf_op jit(solution)/shard_map/ppermute | solution.py:747
  28.9 4.3 %collective-permute-start.13 = (bf16[232,128]{1,0:T(8,128)(2,1)S(1)}, bf16[232,128]{1,0:T(8,128)(2,1)S(1)}, u32[]{:S(2)}, u32[]{:S(2)}) collective-permute-start(bf16[232,128]{1,0:T(8,128)(2,1)S(1)} %wire.3), channel_id=1, source_target_pairs={{0,16},{16,0},{1,17},{17,1},{2,18},{18,2},{3,19},{19,3},{4,20},{20... | collective-permute-start | bytes 178184 | tf_op jit(solution)/shard_map/ppermute | solution.py:747
  30.5 5.9 %collective-permute-start.11 = (bf16[232,128]{1,0:T(8,128)(2,1)S(1)}, bf16[232,128]{1,0:T(8,128)(2,1)S(1)}, u32[]{:S(2)}, u32[]{:S(2)}) collective-permute-start(bf16[232,128]{1,0:T(8,128)(2,1)S(1)} %get-tuple-element.67), channel_id=1, source_target_pairs={{0,2},{1,3},{2,0},{3,1},{4,6},{5,7},{6,4},{7,5},{8,10},{9,11},{10,... | collective-permute-start | bytes 178184 | tf_op jit(solution)/shard_map/ppermute | solution.py:747
  33.2 4.2 %collective-permute-start.14 = (bf16[232,128]{1,0:T(8,128)(2,1)S(1)}, bf16[232,128]{1,0:T(8,128)(2,1)S(1)}, u32[]{:S(2)}, u32[]{:S(2)}) collective-permute-start(bf16[232,128]{1,0:T(8,128)(2,1)S(1)} %get-tuple-element.76), channel_id=1, source_target_pairs={{0,1},{1,0},{2,3},{3,2},{4,5},{5,4},{6,7},{7,6},{8,9},{9,8},{10,11... | collective-permute-start | bytes 178184 | tf_op jit(solution)/shard_map/ppermute | solution.py:747
  36.5 4.6 %collective-permute-start.12 = (bf16[360,128]{1,0:T(8,128)(2,1)S(1)}, bf16[360,128]{1,0:T(8,128)(2,1)S(1)}, u32[]{:S(2)}, u32[]{:S(2)}) collective-permute-start(bf16[360,128]{1,0:T(8,128)(2,1)S(1)} %get-tuple-element.70), channel_id=1, source_target_pairs={{0,16},{16,0},{1,17},{17,1},{2,18},{18,2},{3,19},{19,3},{4,20},{20... | collective-permute-start | bytes 276488 | tf_op jit(solution)/shard_map/ppermute | solution.py:747
  37.5 5.1 %collective-permute-start.15 = (bf16[232,128]{1,0:T(8,128)(2,1)S(1)}, bf16[232,128]{1,0:T(8,128)(2,1)S(1)}, u32[]{:S(2)}, u32[]{:S(2)}) collective-permute-start(bf16[232,128]{1,0:T(8,128)(2,1)S(1)} %get-tuple-element.80), channel_id=1, source_target_pairs={{0,2},{1,3},{2,0},{3,1},{4,6},{5,7},{6,4},{7,5},{8,10},{9,11},{10,... | collective-permute-start | bytes 178184 | tf_op jit(solution)/shard_map/ppermute | solution.py:747
